TPU v7x, 32 devices: a whole 2x2x4 slice. The times are simulated.
32 devices in a mesh: row: 8 (over y, x, core), col: 4 (over z).
Axes of the slice: x: 2, y: 2, z: 4, core: 2. Of those that a mesh axis runs over, the one named last changes fastest.
Arguments:
- density: bfloat16 [32, 5, 256, 256], P('row', None, 'col'), may hold values from -1 to 2, as said below
- pattern: int32 [32, 5], P('row'), may hold values from 0 to 1, as said below
- windows: int32 [64], P(('row', 'col')), may hold values from 0 to 61, as said below
- basis_values: bfloat16 [64, 4096, 384], P(('row', 'col')), may hold values from -6 to 6
- basis_grads: bfloat16 [3, 64, 4096, 384], P(None, ('row', 'col')), may hold values from -48 to 48
- weights: float32 [64, 4096], P(('row', 'col')), may hold values from 0.25 to 4
Outputs:
- purified: bfloat16 [32, 5, 256, 256], P('row', None, 'col')
- xc_matrix: float32 [32, 5, 256, 256], P('row', None, 'col')
- grid_density: float32 [64, 4096], P(('row', 'col'))
Inputs may be any that keep to these rules, and one draw needn't show every extreme that they name: density[i, d] is block (i, i + d - 2) of a symmetric matrix: density[i, d] equals density[i + d - 2, 4 - d] transposed; blocks whose column block lies outside the matrix are 0. pattern[i, d] = pattern[i + d - 2, 4 - d]; it is 1 for d = 1, 2, 3 where block i + d - 2 exists and 0 where it does not. Tile t lies on device t // 2 of the joined axes row+col; if that device has row index q, windows[t] lies between 2 * 4 q - 2 and 2 * 4 q + 2 * 4 - 1.
All inputs are finite; a program needn't handle non-finite values.
Results may differ from a plain program's by a relative error of at most 0.011.
Values may be sent and summed in bfloat16 or wider, within the bound.
No kernel may reach another device: no remote copies, remote signals or barrier semaphores. Data moves between devices by JAX's collectives and lax.ppermute only.
A program may use at most 128 MiB of HBM per device.

v0:
```python
import jax
import jax.numpy as jnp
from jax import lax
from jax.sharding import PartitionSpec as P

ITERS = 2


slater_cx = 0.7386
kappa_pbe = 0.804
mu_pbe = 0.2195


def padded(cells, sides, width):
    for axis, dim in sides:
        count = lax.axis_size(axis)
        ends = count - 1
        head = lax.slice_in_dim(cells, 0, width, axis=dim)
        tail = lax.slice_in_dim(cells, cells.shape[dim] - width, cells.shape[dim], axis=dim)
        cells = jnp.concatenate(
            [
                lax.ppermute(tail, axis, [(i, (i + 1) % count) for i in range(ends)]),
                cells,
                lax.ppermute(head, axis, [((i + 1) % count, i) for i in range(ends)]),
            ],
            axis=dim,
        )
    return cells


def shifted_2(value, axis, by):
    length = lax.axis_size(axis)
    pairs = [(i, i + by) for i in range(length) if 0 <= i + by < length]
    return lax.ppermute(value, axis, pairs)


def energy_sum(point_density, grad_square):
    spread = jnp.sqrt(point_density * point_density + 1.0)
    reduced = grad_square / spread ** (8.0 / 3.0)
    enhance = 1.0 + kappa_pbe - kappa_pbe / (1.0 + mu_pbe * reduced / kappa_pbe)
    return jnp.sum(-slater_cx * spread ** (4.0 / 3.0) * enhance)


def tile_terms(values, grads, quadrature, window_block):
    functions = values.shape[1]
    points = values.shape[0]
    projected = jnp.dot(values, window_block, preferred_element_type=jnp.float32)
    point_density = jnp.sum(projected * values.astype(jnp.float32), axis=1) / functions
    slopes = 2.0 * jnp.sum(projected[None] * grads.astype(jnp.float32), axis=2) / functions
    grad_square = jnp.sum(slopes * slopes, axis=0)
    by_density, by_gradient = jax.grad(energy_sum, argnums=(0, 1))(point_density, grad_square)
    scaled = quadrature / points
    weighted = (0.5 * by_density * scaled)[:, None] * values.astype(jnp.float32)
    weighted = weighted + jnp.sum(
        ((2.0 * by_gradient * scaled)[None] * slopes)[:, :, None] * grads.astype(jnp.float32),
        axis=0,
    )
    weighted = weighted.astype(jnp.bfloat16)
    one_side = lax.dot_general(
        values, weighted, (((0,), (0,)), ((), ())), preferred_element_type=jnp.float32
    )
    return (point_density, one_side + one_side.T)


def band_product(left, right_padded):
    blocks = left.shape[0]
    total = None
    for offset_step in range(5):
        shifted = right_padded[offset_step : offset_step + blocks]
        widened = jnp.pad(shifted, ((0, 0), (2, 2), (0, 0), (0, 0)))
        picked = widened[:, 4 - offset_step : 9 - offset_step]
        term = jnp.einsum(
            "brk,bdkc->bdrc", left[:, offset_step], picked, preferred_element_type=jnp.float32
        )
        total = term if total is None else total + term
    return total


def window_of(band_three, lead, offset, functions):
    paired = lax.dynamic_slice_in_dim(band_three, lead, 2, 0)
    upper = jnp.concatenate([paired[0, 1], paired[0, 2]], axis=1)
    lower = jnp.concatenate([paired[1, 0], paired[1, 1]], axis=1)
    dense = jnp.concatenate([upper, lower], axis=0)
    return lax.dynamic_slice(dense, (offset, offset), (functions, functions))


def spread_term(summed, term, lead, offset):
    width = summed.shape[2]
    dense = lax.dynamic_update_slice(
        jnp.zeros((2 * width, 2 * width), summed.dtype), term, (offset, offset)
    )
    nothing = jnp.zeros((width, width), summed.dtype)
    upper = jnp.stack([nothing, dense[:width, :width], dense[:width, width:]])
    lower = jnp.stack([dense[width:, :width], dense[width:, width:], nothing])
    increment = jnp.stack([upper, lower])
    paired = lax.dynamic_slice_in_dim(summed, lead, 2, 0)
    return lax.dynamic_update_slice_in_dim(summed, paired + increment, lead, 0)


def times_current(left, current):
    near_right = padded(current, (("row", 0),), 2)
    return band_product(left, lax.all_gather(near_right, "col", axis=2, tiled=True))


def edge_rows(summed):
    blocks = summed.shape[0] - 2
    from_above = shifted_2(summed[0].astype(jnp.bfloat16), "row", -1).astype(jnp.float32)
    from_below = shifted_2(summed[blocks + 1].astype(jnp.bfloat16), "row", 1).astype(jnp.float32)
    own_rows = summed[1 : blocks + 1]
    return jnp.concatenate(
        [
            own_rows[:1] + from_below[None],
            own_rows[1 : blocks - 1],
            own_rows[blocks - 1 :] + from_above[None],
        ],
        axis=0,
    )


def on_device(density, pattern, windows, basis_values, basis_grads, weights):
    row_index = lax.axis_index("row")
    band_rows = density.shape[0]
    functions = basis_values.shape[2]
    step_size = functions // 3
    kept = (pattern > 0)[:, :, None, None]
    current = jnp.where(kept, density, jnp.zeros_like(density))
    for iteration in range(ITERS):
        square = jnp.where(kept, times_current(current, current), 0.0).astype(jnp.bfloat16)
        cubic = times_current(square, current)
        current = jnp.where(kept, 3.0 * square.astype(jnp.float32) - 2.0 * cubic, 0.0).astype(
            jnp.bfloat16
        )
    rows_full = lax.all_gather(current, "col", axis=2, tiled=True)
    near_full = padded(rows_full, (("row", 0),), 1)
    near = near_full[:, 1:4]
    tiles_here = windows.shape[0]
    points = basis_values.shape[1]
    block_size = near.shape[2]

    def one_tile(tile_index, carry):
        summed, densities = carry
        position = tile_index.astype(jnp.int32)
        start_step = windows[position]
        lead = start_step // 2 - (band_rows * row_index - 1)
        offset = start_step % 2 * step_size
        window_block = window_of(near, lead, offset, functions)
        values = lax.dynamic_index_in_dim(basis_values, position, 0, keepdims=False)
        grads = lax.dynamic_index_in_dim(basis_grads, position, 1, keepdims=False)
        quadrature = lax.dynamic_index_in_dim(weights, position, 0, keepdims=False)
        point_density, contribution = tile_terms(values, grads, quadrature, window_block)
        summed = spread_term(summed, contribution, lead, offset)
        densities = lax.dynamic_update_index_in_dim(densities, point_density, position, 0)
        return (summed, densities)

    start_carry = (
        jnp.zeros((band_rows + 2, 3, block_size, block_size), jnp.float32),
        jnp.zeros((tiles_here, points), jnp.float32),
    )
    local_terms, densities = lax.fori_loop(0, tiles_here, one_tile, start_carry)
    owner_part = lax.psum_scatter(
        local_terms.astype(jnp.bfloat16), "col", scatter_dimension=2, tiled=True
    ).astype(jnp.float32)
    mine = edge_rows(owner_part)
    xc_matrix = jnp.where(kept, jnp.pad(mine, ((0, 0), (1, 1), (0, 0), (0, 0))), 0.0)
    return (current, xc_matrix, densities)


def solution(mesh):
    placed = (
        P("row", None, "col", None),
        P("row", None),
        P(("row", "col")),
        P(("row", "col"), None, None),
        P(None, ("row", "col"), None, None),
        P(("row", "col"), None),
    )
    return jax.shard_map(
        on_device,
        mesh=mesh,
        in_specs=placed,
        out_specs=(
            P("row", None, "col", None),
            P("row", None, "col", None),
            P(("row", "col"), None),
        ),
        check_vma=False,
    )
```

profile of v0, /device:TPU:3, one launch (start us, length us, event | category | flops | bytes accessed | tf_op | source)
XLA Modules:
  0.0 501.9 jit_solution(10504109951317897931)
XLA Ops:
  9.3 3.7 collective-permute-start
  13.0 1.9 collective-permute-start.1
  14.9 2.8 collective-permute-done
  17.7 4.5 collective-permute-done.1
  23.5 97.9 %all-gather.4.cloned.1.call-done = bf16[8,5,256,256]{3,2,0,1:T(8,128)(2,1)} async-done(((bf16[8,5,64,256]{3,2,0,1:T(8,128)(2,1)}), bf16[8,5,256,256]{3,2,0,1:T(8,128)(2,1)}) %all-gather.4.cloned.1.call-update) | async-done | bytes 5242896 | tf_op jit(solution)/shard_map/all_gather | solution.py:102
  121.4 4.5 fusion.96
  127.0 1.5 copy-done.1
  132.7 3.6 collective-permute-start.2
  136.3 1.9 collective-permute-start.3
  138.2 2.8 collective-permute-done.2
  141.0 4.6 collective-permute-done.3
  146.9 95.1 %all-gather.6.cloned.1.call-done = bf16[8,5,256,256]{3,2,0,1:T(8,128)(2,1)} async-done(((bf16[8,5,64,256]{3,2,0,1:T(8,128)(2,1)}), bf16[8,5,256,256]{3,2,0,1:T(8,128)(2,1)}) %all-gather.6.cloned.1.call-update) | async-done | bytes 5242896 | tf_op jit(solution)/shard_map/all_gather | solution.py:102
  241.9 4.5 fusion.95
  247.5 1.5 copy-done.2
  252.6 1.3 fusion.69
  254.0 53.0 %all-gather.8.cloned.1.call-done = bf16[4,5,256,256]{3,2,0,1:T(8,128)(2,1)} async-done(((bf16[4,5,64,256]{3,2,0,1:T(8,128)(2,1)}), bf16[4,5,256,256]{3,2,0,1:T(8,128)(2,1)}) %all-gather.8.cloned.1.call-update) | async-done | bytes 2621456 | tf_op jit(solution)/shard_map/all_gather | solution.py:133
  307.0 1.4 fusion.97
  308.4 3.8 collective-permute-start.4
  312.2 2.1 collective-permute-start.5
  314.3 9.6 %collective-permute-done.4 = bf16[1,5,256,256]{3,2,0,1:T(8,128)(2,1)S(1)} collective-permute-done((bf16[1,5,256,256]{3,2,0,1:T(8,128)(2,1)S(1)}, bf16[1,5,256,256]{3,2,0,1:T(8,128)(2,1)S(1)}, u32[]{:S(2)}, u32[]{:S(2)}) %collective-permute-start.4) | collective-permute-done | bytes 655392 | tf_op jit(solution)/shard_map/ppermute | solution.py:22
  324.0 4.5 collective-permute-done.5
  328.5 1.8 pad_maximum_fusion
  330.3 2.6 broadcast_in_dim.75
  332.9 99.5 %while.18 = (s32[]{:T(128)}, f32[6,3,256,256]{3,2,1,0:T(8,128)}, f32[2,4096]{1,0:T(2,128)}, s32[2]{0:T(128)}, s32[]{:T(128)}, /*index=5*/bf16[2,4096,384]{2,1,0:...) while((s32[]{:T(128)}, f32[6,3,256,256]{3,2,1,0:T(8,128)}, ...), condition=%wide.region_5.6_spmd, body=%wide.region_0.5_spmd.sunk | while | flops 2456809472 | bytes 116916952 | solution.py:159
  337.5 2.2 constant_dynamic-slice_fusion.2
  339.7 3.0 copy.166
  342.7 7.4 %multiply_reduce_fusion.4 = (f32[4096]{0:T(1024)S(1)}, f32[4096,384]{0,1:T(8,128)}) fusion(bf16[1,4096,384]{1,2,0:T(8,128)(2,1)} %copy.166, s32[]{:T(128)S(6)} %select_n.130, bf16[256,256]{1,0:T(8,128)(2,1)} %get-tuple-element.424, bf16[256,256]{1,0:T(8,128)(2,1)S(1)} %get-tuple-element.425, bf16[256,256]{1,0:T(8,128)(2,1)S(1)} %get-tuple-element.426, ...), kind=kOutput, calls=%fused_computation.6.clone.1 | convolution fusion | flops 1213853696 | bytes 13123588 | tf_op jit(solution)/shard_map/while/body/eval_jaxpr/dot_general | solution.py:47
  350.1 6.6 %copy.167 = f32[4096,384]{1,0:T(8,128)} copy(f32[4096,384]{0,1:T(8,128)} %get-tuple-element.428) | data formatting | bytes 12582912 | tf_op jit(solution)/shard_map/while/body/eval_jaxpr/dot_general | solution.py:47
  356.6 6.8 %fusion.112 = f32[3,4096]{1,0:T(4,128)S(1)} fusion(f32[4096,384]{1,0:T(8,128)} %copy.167, bf16[3,2,4096,384]{3,2,1,0:T(8,128)(2,1)} %get-tuple-element.483, s32[]{:T(128)} %get-tuple-element.457), kind=kLoop, calls=%fused_computation.2.clone.1 | loop fusion | flops 14143488 | bytes 15777796 | tf_op jit(solution)/shard_map/while/body/eval_jaxpr/reduce_sum | solution.py:49
  363.9 9.9 %fusion.113 = f32[4096,384]{1,0:T(8,128)S(1)} fusion(f32[3,4096]{1,0:T(4,128)S(1)} %broadcast_multiply_fusion.5, bf16[3,2,4096,384]{3,2,1,0:T(8,128)(2,1)} %get-tuple-element.483, s32[]{:T(128)} %get-tuple-element.457), kind=kLoop, calls=%fused_computation.3.clone.1 | loop fusion | flops 12582912 | bytes 15777796 | tf_op jit(solution)/shard_map/while/body/eval_jaxpr/reduce_sum | solution.py:54
  373.9 3.2 fusion.115
  377.1 1.4 copy.168
  379.0 2.9 fusion.117
  382.7 1.3 dynamic_slice.135
  387.3 2.2 constant_dynamic-slice_fusion.2
  389.5 3.0 copy.166
  392.5 7.3 %multiply_reduce_fusion.4 = (f32[4096]{0:T(1024)S(1)}, f32[4096,384]{0,1:T(8,128)}) fusion(bf16[1,4096,384]{1,2,0:T(8,128)(2,1)} %copy.166, s32[]{:T(128)S(6)} %select_n.130, bf16[256,256]{1,0:T(8,128)(2,1)} %get-tuple-element.424, bf16[256,256]{1,0:T(8,128)(2,1)S(1)} %get-tuple-element.425, bf16[256,256]{1,0:T(8,128)(2,1)S(1)} %get-tuple-element.426, ...), kind=kOutput, calls=%fused_computation.6.clone.1 | convolution fusion | flops 1213853696 | bytes 13123588 | tf_op jit(solution)/shard_map/while/body/eval_jaxpr/dot_general | solution.py:47
  399.8 6.6 %copy.167 = f32[4096,384]{1,0:T(8,128)} copy(f32[4096,384]{0,1:T(8,128)} %get-tuple-element.428) | data formatting | bytes 12582912 | tf_op jit(solution)/shard_map/while/body/eval_jaxpr/dot_general | solution.py:47
  406.4 6.8 %fusion.112 = f32[3,4096]{1,0:T(4,128)S(1)} fusion(f32[4096,384]{1,0:T(8,128)} %copy.167, bf16[3,2,4096,384]{3,2,1,0:T(8,128)(2,1)} %get-tuple-element.483, s32[]{:T(128)} %get-tuple-element.457), kind=kLoop, calls=%fused_computation.2.clone.1 | loop fusion | flops 14143488 | bytes 15777796 | tf_op jit(solution)/shard_map/while/body/eval_jaxpr/reduce_sum | solution.py:49
  413.7 9.9 %fusion.113 = f32[4096,384]{1,0:T(8,128)S(1)} fusion(f32[3,4096]{1,0:T(4,128)S(1)} %broadcast_multiply_fusion.5, bf16[3,2,4096,384]{3,2,1,0:T(8,128)(2,1)} %get-tuple-element.483, s32[]{:T(128)} %get-tuple-element.457), kind=kLoop, calls=%fused_computation.3.clone.1 | loop fusion | flops 12582912 | bytes 15777796 | tf_op jit(solution)/shard_map/while/body/eval_jaxpr/reduce_sum | solution.py:54
  423.6 3.2 fusion.115
  426.8 1.4 copy.168
  428.7 2.9 fusion.117
  432.4 4.1 convert_element_type.113
  436.5 44.7 %reduce-scatter.2.cloned.1.call-done = bf16[6,3,64,256]{3,2,1,0:T(8,128)(2,1)} async-done(((bf16[6,3,256,256]{3,2,1,0:T(8,128)(2,1)}), bf16[6,3,64,256]{3,2,1,0:T(8,128)(2,1)}) %reduce-scatter.2.cloned.1.call-update) | async-done | bytes 589840 | tf_op jit(solution)/shard_map/reduce_scatter | solution.py:160
  482.3 4.1 collective-permute-start.6
  487.2 1.9 collective-permute-start.7
  490.4 3.7 collective-permute-done.7
  (102 shorter events, 24.8 us)
Async XLA Ops:
  7.2 114.3 %all-gather.4.cloned.1.call-start = ((), (), s32[]{:S(2)}) async-start(), calls=%async_computation.1 | async-start | bytes 6553600 | tf_op jit(solution)/shard_map/all_gather | solution.py:102
  8.0 244.6 %copy-start.8 = (pred[4,5]{0,1:T(8,128)(4,1)}, pred[4,5]{0,1:T(8,128)(4,1)S(1)}, u32[]{:S(2)}) copy-start(pred[4,5]{0,1:T(8,128)(4,1)S(1)} %copy.64) | copy-start | bytes 64
  9.3 8.4 %collective-permute-start = (bf16[2,5,64,256]{3,2,0,1:T(8,128)(2,1)S(1)}, bf16[2,5,64,256]{3,2,0,1:T(8,128)(2,1)S(1)}, u32[]{:S(2)}, u32[]{:S(2)}) collective-permute-start(bf16[2,5,64,256]{3,2,0,1:T(8,128)(2,1)S(1)} %get-tuple-element.351), channel_id=1, source_target_pairs={{0,4},{4,8},{8,12},{12,16},{16,20},{20,24},{24,28},{1,5},{5,9},{9,... | collective-permute-start | bytes 983048 | tf_op jit(solution)/shard_map/ppermute | solution.py:22
  13.0 9.3 %collective-permute-start.1 = (bf16[2,5,64,256]{3,2,0,1:T(8,128)(2,1)S(1)}, bf16[2,5,64,256]{3,2,0,1:T(8,128)(2,1)S(1)}, u32[]{:S(2)}, u32[]{:S(2)}) collective-permute-start(bf16[2,5,64,256]{3,2,0,1:T(8,128)(2,1)S(1)} %get-tuple-element.352), channel_id=1, source_target_pairs={{4,0},{8,4},{12,8},{16,12},{20,16},{24,20},{28,24},{5,1},{9,5},{13... | collective-permute-start | bytes 983048 | tf_op jit(solution)/shard_map/ppermute | solution.py:24
  23.5 218.4 %all-gather.6.cloned.1.call-start = ((), (), s32[]{:S(2)}) async-start(), calls=%async_computation.2 | async-start | bytes 6553600 | tf_op jit(solution)/shard_map/all_gather | solution.py:102
  126.0 2.5 copy-start.1
  132.7 8.4 %collective-permute-start.2 = (bf16[2,5,64,256]{3,2,0,1:T(8,128)(2,1)S(1)}, bf16[2,5,64,256]{3,2,0,1:T(8,128)(2,1)S(1)}, u32[]{:S(2)}, u32[]{:S(2)}) collective-permute-start(bf16[2,5,64,256]{3,2,0,1:T(8,128)(2,1)S(1)} %get-tuple-element.349), channel_id=1, source_target_pairs={{0,4},{4,8},{8,12},{12,16},{16,20},{20,24},{24,28},{1,5},{5,9},{9,... | collective-permute-start | bytes 983048 | tf_op jit(solution)/shard_map/ppermute | solution.py:22
  136.3 9.3 %collective-permute-start.3 = (bf16[2,5,64,256]{3,2,0,1:T(8,128)(2,1)S(1)}, bf16[2,5,64,256]{3,2,0,1:T(8,128)(2,1)S(1)}, u32[]{:S(2)}, u32[]{:S(2)}) collective-permute-start(bf16[2,5,64,256]{3,2,0,1:T(8,128)(2,1)S(1)} %get-tuple-element.350), channel_id=1, source_target_pairs={{4,0},{8,4},{12,8},{16,12},{20,16},{24,20},{28,24},{5,1},{9,5},{13... | collective-permute-start | bytes 983048 | tf_op jit(solution)/shard_map/ppermute | solution.py:24
  146.8 160.2 %all-gather.8.cloned.1.call-start = ((), (), s32[]{:S(2)}) async-start(), calls=%async_computation.3 | async-start | bytes 3276800 | tf_op jit(solution)/shard_map/all_gather | solution.py:133
  246.5 2.5 copy-start.2
  254.0 227.3 %reduce-scatter.2.cloned.1.call-start = ((), (), s32[]{:S(2)}) async-start(), calls=%async_computation.4 | async-start | bytes 2949120 | tf_op jit(solution)/shard_map/reduce_scatter | solution.py:160
  308.4 15.6 %collective-permute-start.4 = (bf16[1,5,256,256]{3,2,0,1:T(8,128)(2,1)S(1)}, bf16[1,5,256,256]{3,2,0,1:T(8,128)(2,1)S(1)}, u32[]{:S(2)}, u32[]{:S(2)}) collective-permute-start(bf16[1,5,256,256]{3,2,0,1:T(8,128)(2,1)S(1)} %get-tuple-element.347), channel_id=1, source_target_pairs={{0,4},{4,8},{8,12},{12,16},{16,20},{20,24},{24,28},{1,5},{5,9},{9,... | collective-permute-start | bytes 1966088 | tf_op jit(solution)/shard_map/ppermute | solution.py:22
  312.2 16.3 %collective-permute-start.5 = (bf16[1,5,256,256]{3,2,0,1:T(8,128)(2,1)S(1)}, bf16[1,5,256,256]{3,2,0,1:T(8,128)(2,1)}, u32[]{:S(2)}, u32[]{:S(2)}) collective-permute-start(bf16[1,5,256,256]{3,2,0,1:T(8,128)(2,1)S(1)} %get-tuple-element.348), channel_id=1, source_target_pairs={{4,0},{8,4},{12,8},{16,12},{20,16},{24,20},{28,24},{5,1},{9,5},{13... | collective-permute-start | bytes 1966088 | tf_op jit(solution)/shard_map/ppermute | solution.py:24
  332.9 4.6 copy-start.3
  356.6 6.9 %copy-start.7 = (f32[2,4096]{1,0:T(2,128)S(1)}, f32[2,4096]{1,0:T(2,128)}, u32[]{:S(2)}) copy-start(f32[2,4096]{1,0:T(2,128)} %get-tuple-element.484) | copy-start | bytes 98308 | tf_op jit(solution)/shard_map/while
  377.1 1.5 copy-start
  379.0 2.9 copy-start.10
  379.0 3.7 copy-start.4
  382.0 0.6 copy-start.11
  382.7 4.6 copy-start.3
  406.4 6.9 %copy-start.7 = (f32[2,4096]{1,0:T(2,128)S(1)}, f32[2,4096]{1,0:T(2,128)}, u32[]{:S(2)}) copy-start(f32[2,4096]{1,0:T(2,128)} %get-tuple-element.484) | copy-start | bytes 98308 | tf_op jit(solution)/shard_map/while
  426.8 1.5 copy-start
  428.7 2.9 copy-start.10
  428.7 3.7 copy-start.4
  431.8 0.6 copy-start.11
  436.5 49.9 %copy-start.5 = (bf16[4,5,64,256]{3,2,0,1:T(8,128)(2,1)S(1)}, bf16[4,5,64,256]{3,2,0,1:T(8,128)(2,1)}, u32[]{:S(2)}) copy-start(bf16[4,5,64,256]{3,2,0,1:T(8,128)(2,1)} %fusion.69) | copy-start | bytes 1966084
  436.5 57.6 %copy-start.9 = (pred[4,5]{0,1:T(8,128)(4,1)S(1)}, pred[4,5]{0,1:T(8,128)(4,1)}, u32[]{:S(2)}) copy-start(pred[4,5]{0,1:T(8,128)(4,1)} %copy-done.8) | copy-start | bytes 64
  481.2 12.8 %copy-start.6 = (bf16[6,3,64,256]{3,2,1,0:T(8,128)(2,1)S(1)}, bf16[6,3,64,256]{3,2,1,0:T(8,128)(2,1)}, u32[]{:S(2)}) copy-start(bf16[6,3,64,256]{3,2,1,0:T(8,128)(2,1)} %reduce-scatter.2.cloned.1.call-done) | copy-start | bytes 1769476
  482.3 8.1 %collective-permute-start.6 = (bf16[3,64,256]{2,1,0:T(8,128)(2,1)S(1)}, bf16[3,64,256]{2,1,0:T(8,128)(2,1)S(1)}, u32[]{:S(2)}, u32[]{:S(2)}) collective-permute-start(bf16[3,64,256]{2,1,0:T(8,128)(2,1)S(1)} %get-tuple-element.353), channel_id=1, source_target_pairs={{0,4},{4,8},{8,12},{12,16},{16,20},{20,24},{24,28},{1,5},{5,9},{9,... | collective-permute-start | bytes 294920 | tf_op jit(solution)/shard_map/ppermute | solution.py:34
  487.2 6.8 %collective-permute-start.7 = (bf16[3,64,256]{2,1,0:T(8,128)(2,1)S(1)}, bf16[3,64,256]{2,1,0:T(8,128)(2,1)S(1)}, u32[]{:S(2)}, u32[]{:S(2)}) collective-permute-start(bf16[3,64,256]{2,1,0:T(8,128)(2,1)S(1)} %get-tuple-element.354), channel_id=1, source_target_pairs={{4,0},{8,4},{12,8},{16,12},{20,16},{24,20},{28,24},{5,1},{9,5},{13... | collective-permute-start | bytes 294920 | tf_op jit(solution)/shard_map/ppermute | solution.py:34
Sparse Core Ops, SparseCore 0:
  23.6 97.7 all-gather.3
  146.9 94.9 all-gather.5
  254.1 52.8 all-gather.7
  436.6 44.5 reduce-scatter.1
where the time goes:
time: 503 us; the launch traced here: 502 us
  waiting for transfers between devices  323 us (64%)
  other arithmetic  52.2 us (10%)
  local copies, waits for them, and re-layouts  51.5 us (10%)
  matrix products  32.1 us (6%)
  starting transfers between devices  23.2 us (5%)
  between operations  14.1 us (3%)
  loops' own time  5.51 us (1%)
    all_gather x2, waiting for transfers between devices, times_current(): lax.all_gather(near_right, 'col', axis=2, tiled=True)  193 us
    all_gather x1, waiting for transfers between devices, on_device(): rows_full = lax.all_gather(current, 'col', axis=2, tiled=True)  53 us
    reduce_scatter x1, waiting for transfers between devices, on_device(): lax.psum_scatter(local_terms.astype(jnp.bfloat16), 'col', scatter_dimensi...  44.7 us
    reduce_sum x2, other arithmetic, tile_terms(): jnp.sum(((2.0 * by_gradient * scaled)[None] * slopes)[:, :, None] * grads...  19.9 us
    ppermute x3, waiting for transfers between devices, padded(): lax.ppermute(tail, axis, [(i, (i + 1) % count) for i in range(ends)])  15.3 us
    dot_general x2, matrix products, tile_terms(): jnp.dot(values, window_block, preferred_element_type=jnp.float32)  14.7 us
    reduce_sum x2, other arithmetic, tile_terms(): jnp.sum(projected[None] * grads.astype(jnp.float32), axis=2)  13.6 us
    ppermute x3, waiting for transfers between devices, padded(): lax.ppermute(head, axis, [((i + 1) % count, i) for i in range(ends)])  13.6 us
  transfers between devices with their start and end apart: 12, of which 11 were waited for; matrix products, arithmetic and copies ran while one was open for 0% of the time, Pallas kernels for 0%

commit v1 on v0

--- a/solution.py
+++ b/solution.py
@@ -1,6 +1,8 @@
 import jax
 import jax.numpy as jnp
 from jax import lax
+from jax.experimental import pallas as pl
+from jax.experimental.pallas import tpu as pltpu
 from jax.sharding import PartitionSpec as P
 
 ITERS = 2
@@ -34,33 +36,82 @@
     return lax.ppermute(value, axis, pairs)
 
 
-def energy_sum(point_density, grad_square):
-    spread = jnp.sqrt(point_density * point_density + 1.0)
-    reduced = grad_square / spread ** (8.0 / 3.0)
-    enhance = 1.0 + kappa_pbe - kappa_pbe / (1.0 + mu_pbe * reduced / kappa_pbe)
-    return jnp.sum(-slater_cx * spread ** (4.0 / 3.0) * enhance)
-
-
-def tile_terms(values, grads, quadrature, window_block):
-    functions = values.shape[1]
-    points = values.shape[0]
-    projected = jnp.dot(values, window_block, preferred_element_type=jnp.float32)
-    point_density = jnp.sum(projected * values.astype(jnp.float32), axis=1) / functions
-    slopes = 2.0 * jnp.sum(projected[None] * grads.astype(jnp.float32), axis=2) / functions
-    grad_square = jnp.sum(slopes * slopes, axis=0)
-    by_density, by_gradient = jax.grad(energy_sum, argnums=(0, 1))(point_density, grad_square)
-    scaled = quadrature / points
-    weighted = (0.5 * by_density * scaled)[:, None] * values.astype(jnp.float32)
-    weighted = weighted + jnp.sum(
-        ((2.0 * by_gradient * scaled)[None] * slopes)[:, :, None] * grads.astype(jnp.float32),
-        axis=0,
-    )
-    weighted = weighted.astype(jnp.bfloat16)
-    one_side = lax.dot_general(
-        values, weighted, (((0,), (0,)), ((), ())), preferred_element_type=jnp.float32
-    )
-    return (point_density, one_side + one_side.T)
-
+def pointwise(n,g,w,points):
+    u=n*n+1.0
+    lu=jnp.log(u)
+    a=jnp.exp(lu*(2.0/3.0))
+    ia=1.0/a
+    b=ia*ia
+    sig=g[0]*g[0]+g[1]*g[1]+g[2]*g[2]
+    t=sig*b
+    iden=1.0/(1.0+(mu_pbe/kappa_pbe)*t)
+    fac=1.0+kappa_pbe-kappa_pbe*iden
+    dF=mu_pbe*iden*iden
+    vs=-slater_cx*dF*ia
+    vn=-slater_cx*a*(n/u)*((4.0/3.0)*fac-(8.0/3.0)*t*dF)
+    sc=w*(1.0/points)
+    c0=0.5*vn*sc
+    s2=2.0*vs*sc
+    return c0,[s2*gk for gk in g]
+def tile_kernel(points, v_ref, g_ref, w_ref, win_ref, dens_ref, term_ref, vs_ref, z_ref, y_ref):
+    i=pl.program_id(0); n=pl.num_programs(0)-1
+    tp,fn=v_ref.shape
+    nb=tp//128
+    def stage_a():
+        win=win_ref[...]
+        lane=lax.broadcasted_iota(jnp.int32,(128,128),1)
+        m=jnp.zeros((128,128),jnp.float32)
+        for b in range(nb):
+            v=v_ref[128*b:128*b+128]
+            x=jnp.dot(v,win,preferred_element_type=jnp.float32)
+            m=jnp.where(lane==b,jnp.sum(x*v.astype(jnp.float32),axis=1,keepdims=True),m)
+            for k in range(3):
+                gk=g_ref[k,128*b:128*b+128].astype(jnp.float32)
+                m=jnp.where(lane==nb*(k+1)+b,jnp.sum(x*gk,axis=1,keepdims=True),m)
+        mt=m.T
+        nd=mt[0:nb]*(1.0/fn)
+        g=[mt[nb*(k+1):nb*(k+2)]*(2.0/fn) for k in range(3)]
+        dens_ref[...]=nd
+        c0,ck=pointwise(nd,g,w_ref[...],points)
+        c=jnp.concatenate([c0]+ck+[jnp.zeros((128-4*nb,128),jnp.float32)],axis=0).T
+        for b in range(nb):
+            v=v_ref[128*b:128*b+128]
+            z=c[:,b:b+1]*v.astype(jnp.float32)
+            for k in range(3):
+                z=z+c[:,nb*(k+1)+b:nb*(k+1)+b+1]*g_ref[k,128*b:128*b+128].astype(jnp.float32)
+            z_ref[i%2,128*b:128*b+128]=z.astype(jnp.bfloat16)
+            vs_ref[i%2,128*b:128*b+128]=v
+    def stage_b(first):
+        y=lax.dot_general(vs_ref[(i+1)%2],z_ref[(i+1)%2],(((0,),(0,)),((),())),preferred_element_type=jnp.float32)
+        y_ref[...]=y if first else y_ref[...]+y
+    @pl.when(i==0)
+    def _(): stage_a()
+    @pl.when(i==1)
+    def _():
+        stage_b(True); stage_a()
+    @pl.when((i>1)&(i<n))
+    def _():
+        stage_b(False); stage_a()
+    @pl.when(i==n)
+    def _():
+        stage_b(False)
+        y=y_ref[...]
+        term_ref[...]=y+y.T
+def tile_call(t, basis_values, basis_grads, wts, window, tp=1024):
+    points,fn=basis_values.shape[1:]
+    nch=points//tp; nb=tp//128
+    cl=lambda i: jnp.minimum(i,nch-1)
+    return pl.pallas_call(lambda *r: tile_kernel(points,*r),
+      grid=(nch+1,),
+      in_specs=[pl.BlockSpec((None,tp,fn),lambda i:(t,cl(i),0)),
+                pl.BlockSpec((3,None,tp,fn),lambda i:(0,t,cl(i),0)),
+                pl.BlockSpec((None,nb,128),lambda i:(t,cl(i),0)),
+                pl.BlockSpec((fn,fn),lambda i:(0,0))],
+      out_specs=[pl.BlockSpec((nb,128),lambda i:(cl(i),0)),pl.BlockSpec((fn,fn),lambda i:(0,0))],
+      out_shape=[jax.ShapeDtypeStruct((points//128,128),jnp.float32),jax.ShapeDtypeStruct((fn,fn),jnp.float32)],
+      scratch_shapes=[pltpu.VMEM((2,tp,fn),jnp.bfloat16),pltpu.VMEM((2,tp,fn),jnp.bfloat16),pltpu.VMEM((fn,fn),jnp.float32)],
+      compiler_params=pltpu.CompilerParams(vmem_limit_bytes=48<<20),
+      name="tile")(basis_values,basis_grads,wts,window)
 
 def band_product(left, right_padded):
     blocks = left.shape[0]
@@ -137,26 +188,19 @@
     points = basis_values.shape[1]
     block_size = near.shape[2]
 
-    def one_tile(tile_index, carry):
-        summed, densities = carry
-        position = tile_index.astype(jnp.int32)
-        start_step = windows[position]
+    summed = jnp.zeros((band_rows + 2, 3, block_size, block_size), jnp.float32)
+    quadrature = weights.reshape(tiles_here, points // 128, 128)
+    densities = []
+    for tile in range(tiles_here):
+        start_step = windows[tile]
         lead = start_step // 2 - (band_rows * row_index - 1)
         offset = start_step % 2 * step_size
         window_block = window_of(near, lead, offset, functions)
-        values = lax.dynamic_index_in_dim(basis_values, position, 0, keepdims=False)
-        grads = lax.dynamic_index_in_dim(basis_grads, position, 1, keepdims=False)
-        quadrature = lax.dynamic_index_in_dim(weights, position, 0, keepdims=False)
-        point_density, contribution = tile_terms(values, grads, quadrature, window_block)
+        density_rows, contribution = tile_call(tile, basis_values, basis_grads, quadrature, window_block)
         summed = spread_term(summed, contribution, lead, offset)
-        densities = lax.dynamic_update_index_in_dim(densities, point_density, position, 0)
-        return (summed, densities)
-
-    start_carry = (
-        jnp.zeros((band_rows + 2, 3, block_size, block_size), jnp.float32),
-        jnp.zeros((tiles_here, points), jnp.float32),
-    )
-    local_terms, densities = lax.fori_loop(0, tiles_here, one_tile, start_carry)
+        densities.append(density_rows.reshape(points))
+    densities = jnp.stack(densities)
+    local_terms = summed
     owner_part = lax.psum_scatter(
         local_terms.astype(jnp.bfloat16), "col", scatter_dimension=2, tiled=True
     ).astype(jnp.float32)

time: 503 us -> 439 us (0.87)
  other arithmetic: 52.2 us -> 13.9 us
  Pallas kernels: 0 us -> 25.5 us
  local copies, waits for them, and re-layouts: 51.5 us -> 27.3 us
  matrix products: 32.1 us -> 11 us
  waiting for transfers between devices: 323 us -> 317 us
  loops' own time: 5.51 us -> 0 us
  between operations: 14.1 us -> 19.6 us
    reduce_sum x6 -> x0, other arithmetic: 33.6 us -> none  [the longest x2 19.9 us: tile_terms(): jnp.sum(((2.0 * by_gradient * scaled)[None] * slopes)[:, :, None] * grads...]
    pallas_call x0 -> x2, Pallas kernels: none -> 25.5 us  [tile_call(): pl.pallas_call(lambda *r: tile_kernel(points, *r), grid=(nch + 1,), in_sp...]
    dot_general x4 -> x0, matrix products: 21.1 us -> none  [the longest x2 14.7 us: tile_terms(): jnp.dot(values, window_block, preferred_element_type=jnp.float32)]
    dot_general x4 -> x0, local copies, waits for them, and re-layouts: 15.9 us -> none  [the longest x2 13.1 us: tile_terms(): jnp.dot(values, window_block, preferred_element_type=jnp.float32)]
    dynamic_slice x6 -> x0, local copies, waits for them, and re-layouts: 13 us -> none  [the longest x4 10.4 us: one_tile(): values = lax.dynamic_index_in_dim(basis_values, position, 0, keepdims=False)]
    dynamic_update_slice x2, local copies, waits for them, and re-layouts: 0.26 us -> 9.96 us  [spread_term(): lax.dynamic_update_slice(jnp.zeros((2 * width, 2 * width), summed.dtype),...]
    ppermute x3, waiting for transfers between devices: 15.3 us -> 9.55 us  [padded(): lax.ppermute(tail, axis, [(i, (i + 1) % count) for i in range(ends)])]
    another operation x1 -> x0, loops' own time: 5.51 us -> none  [on_device(): local_terms, densities = lax.fori_loop(0, tiles_here, one_tile, start_carry)]
  transfers between devices with their start and end apart: 12 -> 12, of which waited for: 11 -> 11; matrix products, arithmetic and copies ran while one was open for 0% -> 1% of each run, Pallas kernels for 0% -> 0%
where the time goes in v1:
time: 439 us; the launch traced here: 437 us
  waiting for transfers between devices  317 us (72%)
  local copies, waits for them, and re-layouts  27.3 us (6%)
  Pallas kernels  25.5 us (6%)
  starting transfers between devices  23.2 us (5%)
  between operations  19.6 us (4%)
  other arithmetic  13.9 us (3%)
  matrix products  11 us (3%)
    all_gather x2, waiting for transfers between devices, times_current(): lax.all_gather(near_right, 'col', axis=2, tiled=True)  193 us
    all_gather x1, waiting for transfers between devices, on_device(): rows_full = lax.all_gather(current, 'col', axis=2, tiled=True)  53 us
    reduce_scatter x1, waiting for transfers between devices, on_device(): lax.psum_scatter(local_terms.astype(jnp.bfloat16), 'col', scatter_dimensi...  44.8 us
    pallas_call x2, Pallas kernels, tile_call(): pl.pallas_call(lambda *r: tile_kernel(points, *r), grid=(nch + 1,), in_sp...  25.5 us
    ppermute x3, waiting for transfers between devices, padded(): lax.ppermute(head, axis, [((i + 1) % count, i) for i in range(ends)])  13.5 us
    ppermute x3, starting transfers between devices, padded(): lax.ppermute(tail, axis, [(i, (i + 1) % count) for i in range(ends)])  11.1 us
    dot_general x20, matrix products, band_product(): jnp.einsum('brk,bdkc->bdrc', left[:, offset_step], picked, preferred_elem...  11 us
    dynamic_update_slice x2, local copies, waits for them, and re-layouts, spread_term(): lax.dynamic_update_slice(jnp.zeros((2 * width, 2 * width), summed.dtype),...  9.96 us
  transfers between devices with their start and end apart: 12, of which 11 were waited for; matrix products, arithmetic and copies ran while one was open for 1% of the time, Pallas kernels for 0%

profile of v1, /device:TPU:3, one launch (start us, length us, event | category | flops | bytes accessed | tf_op | source)
XLA Modules:
  0.0 437.4 jit_solution(11361807711885386890)
XLA Ops:
  7.2 0.7 broadcast_compare_fusion
  7.9 1.2 broadcast_select_fusion
  9.2 3.7 collective-permute-start
  12.8 1.9 collective-permute-start.1
  14.8 2.8 collective-permute-done
  17.6 4.5 %collective-permute-done.1 = bf16[2,5,64,256]{3,2,1,0:T(8,128)(2,1)S(1)} collective-permute-done((bf16[2,5,64,256]{3,2,1,0:T(8,128)(2,1)S(1)}, bf16[2,5,64,256]{3,2,1,0:T(8,128)(2,1)S(1)}, u32[]{:S(2)}, u32[]{:S(2)}) %collective-permute-start.1) | collective-permute-done | bytes 327712 | tf_op jit(solution)/shard_map/ppermute | solution.py:26
  22.1 1.2 pad_maximum_fusion.2
  23.4 97.9 %all-gather.4.cloned.1.call-done = bf16[8,5,256,256]{3,2,1,0:T(8,128)(2,1)} async-done(((bf16[8,5,64,256]{3,2,1,0:T(8,128)(2,1)}), bf16[8,5,256,256]{3,2,1,0:T(8,128)(2,1)}) %all-gather.4.cloned.1.call-update) | async-done | bytes 5242896 | tf_op jit(solution)/shard_map/all_gather | solution.py:153
  121.3 4.5 %fusion.88 = (bf16[4,5,256,256]{3,2,1,0:T(8,128)(2,1)S(1)}, bf16[4,5,256,256]{3,2,1,0:T(8,128)(2,1)S(1)}, bf16[4,5,256,256]{3,2,1,0:T(8,128)(2,1)S(1)}, bf16[4,5,256,256]{3,2,1,0:T(8,128)(2,1)S(1)}) fusion(bf16[8,5,256,256]{3,2,1,0:T(8,128)(2,1)} %all-gather.4.cloned.1.call-done), kind=kLoop, calls=%fused_computation.162 | loop fusion | bytes 20971520 | tf_op jit(solution)/shard_map/slice | solution.py:120
  126.4 0.5 fusion.12
  126.9 1.5 copy-done
  128.4 0.6 fusion.4
  130.4 0.5 fusion.13
  130.9 0.6 fusion.6
  132.6 3.6 collective-permute-start.2
  136.2 1.9 collective-permute-start.3
  138.1 2.8 collective-permute-done.2
  141.0 4.5 %collective-permute-done.3 = bf16[2,5,64,256]{3,2,1,0:T(8,128)(2,1)S(1)} collective-permute-done((bf16[2,5,64,256]{3,2,1,0:T(8,128)(2,1)S(1)}, bf16[2,5,64,256]{3,2,1,0:T(8,128)(2,1)S(1)}, u32[]{:S(2)}, u32[]{:S(2)}) %collective-permute-start.3) | collective-permute-done | bytes 327712 | tf_op jit(solution)/shard_map/ppermute | solution.py:26
  145.5 1.2 pad_maximum_fusion.3
  146.8 95.1 %all-gather.6.cloned.1.call-done = bf16[8,5,256,256]{3,2,1,0:T(8,128)(2,1)} async-done(((bf16[8,5,64,256]{3,2,1,0:T(8,128)(2,1)}), bf16[8,5,256,256]{3,2,1,0:T(8,128)(2,1)}) %all-gather.6.cloned.1.call-update) | async-done | bytes 5242896 | tf_op jit(solution)/shard_map/all_gather | solution.py:153
  241.8 4.5 %fusion.87 = (bf16[4,5,256,256]{3,2,1,0:T(8,128)(2,1)S(1)}, bf16[4,5,256,256]{3,2,1,0:T(8,128)(2,1)S(1)}, bf16[4,5,256,256]{3,2,1,0:T(8,128)(2,1)S(1)}, bf16[4,5,256,256]{3,2,1,0:T(8,128)(2,1)S(1)}) fusion(bf16[8,5,256,256]{3,2,1,0:T(8,128)(2,1)} %all-gather.6.cloned.1.call-done), kind=kLoop, calls=%fused_computation.161 | loop fusion | bytes 20971520 | tf_op jit(solution)/shard_map/slice | solution.py:120
  247.4 1.5 copy-done.1
  248.9 0.6 fusion
  250.9 0.5 fusion.21
  251.5 0.6 fusion.2
  252.5 1.4 fusion.51
  254.0 53.0 %all-gather.8.cloned.1.call-done = bf16[4,5,256,256]{3,2,1,0:T(8,128)(2,1)} async-done(((bf16[4,5,64,256]{3,2,1,0:T(8,128)(2,1)}), bf16[4,5,256,256]{3,2,1,0:T(8,128)(2,1)}) %all-gather.8.cloned.1.call-update) | async-done | bytes 2621456 | tf_op jit(solution)/shard_map/all_gather | solution.py:184
  307.0 2.6 fusion.89
  309.5 3.8 collective-permute-start.4
  313.3 2.1 collective-permute-start.5
  315.5 0.6 fusion.92
  321.5 3.9 collective-permute-done.4
  325.4 4.4 %collective-permute-done.5 = bf16[1,5,256,256]{3,2,1,0:T(8,128)(2,1)} collective-permute-done((bf16[1,5,256,256]{3,2,1,0:T(8,128)(2,1)}, bf16[1,5,256,256]{3,2,1,0:T(8,128)(2,1)}, u32[]{:S(2)}, u32[]{:S(2)}) %collective-permute-start.5) | collective-permute-done | bytes 655392 | tf_op jit(solution)/shard_map/ppermute | solution.py:26
  329.8 1.3 pad_maximum_fusion
  331.2 2.7 fusion.66
  333.9 12.6 %tile.2 = (f32[32,128]{1,0:T(8,128)S(1)}, f32[384,384]{1,0:T(8,128)S(1)}) custom-call(bf16[2,4096,384]{2,1,0:T(8,128)(2,1)} %r_0_.3, bf16[3,2,4096,384]{3,2,1,0:T(8,128)(2,1)} %r_1_.3, f32[2,32,128]{2,1,0:T(8,128)S(1)} %bitcast.198, bf16[384,384]{1,0:T(8,128)(2,1)S(1)} %get-tuple-element.52.r_3_), custom_call_target="tpu_custom_call" | custom-call | tf_op jit(solution)/shard_map/tile/pallas_call | solution.py:104
  346.5 12.9 %tile.3 = (f32[32,128]{1,0:T(8,128)S(1)}, f32[384,384]{1,0:T(8,128)S(1)}) custom-call(bf16[2,4096,384]{2,1,0:T(8,128)(2,1)} %r_0_.3, bf16[3,2,4096,384]{3,2,1,0:T(8,128)(2,1)} %r_1_.3, f32[2,32,128]{2,1,0:T(8,128)S(1)} %bitcast.199, bf16[384,384]{1,0:T(8,128)(2,1)S(1)} %get-tuple-element.51.r_3_), custom_call_target="tpu_custom_call" | custom-call | tf_op jit(solution)/shard_map/tile/pallas_call | solution.py:104
  359.5 5.8 %dynamic_update_slice.12 = f32[512,512]{1,0:T(8,128)S(1)} dynamic-update-slice(f32[512,512]{1,0:T(8,128)S(1)} %broadcast.42.clone.1, f32[384,384]{1,0:T(8,128)S(1)} %get-tuple-element.7, s32[]{:T(128)S(6)} %select_n.67, s32[]{:T(128)S(6)} %select_n.67) | dynamic-update-slice | bytes 1179652 | tf_op jit(solution)/shard_map/dynamic_update_slice | solution.py:140
  365.5 4.2 dynamic_update_slice.14
  371.2 1.7 convert_element_type.63
  373.0 44.8 %reduce-scatter.2.cloned.1.call-done = bf16[6,3,64,256]{3,2,1,0:T(8,128)(2,1)} async-done(((bf16[6,3,256,256]{3,2,1,0:T(8,128)(2,1)}), bf16[6,3,64,256]{3,2,1,0:T(8,128)(2,1)}) %reduce-scatter.2.cloned.1.call-update) | async-done | bytes 589840 | tf_op jit(solution)/shard_map/reduce_scatter | solution.py:204
  417.8 1.0 slice_bitcast_fusion.49
  418.8 4.1 collective-permute-start.6
  422.9 1.9 collective-permute-start.7
  424.8 0.6 pad_maximum_fusion.8
  425.4 1.2 convert_element_type.64
  426.7 3.0 collective-permute-done.7
  429.7 1.2 fusion.55
  (46 shorter events, 8.1 us)
Async XLA Ops:
  7.2 114.2 %all-gather.4.cloned.1.call-start = ((), (), s32[]{:S(2)}) async-start(), calls=%async_computation.1 | async-start | bytes 6553600 | tf_op jit(solution)/shard_map/all_gather | solution.py:153
  9.2 8.4 %collective-permute-start = (bf16[2,5,64,256]{3,2,1,0:T(8,128)(2,1)S(1)}, bf16[2,5,64,256]{3,2,1,0:T(8,128)(2,1)S(1)}, u32[]{:S(2)}, u32[]{:S(2)}) collective-permute-start(bf16[2,5,64,256]{3,2,1,0:T(8,128)(2,1)S(1)} %get-tuple-element.41), channel_id=1, source_target_pairs={{0,4},{4,8},{8,12},{12,16},{16,20},{20,24},{24,28},{1,5},{5,9},{9,... | collective-permute-start | bytes 983048 | tf_op jit(solution)/shard_map/ppermute | solution.py:24
  12.8 9.3 %collective-permute-start.1 = (bf16[2,5,64,256]{3,2,1,0:T(8,128)(2,1)S(1)}, bf16[2,5,64,256]{3,2,1,0:T(8,128)(2,1)S(1)}, u32[]{:S(2)}, u32[]{:S(2)}) collective-permute-start(bf16[2,5,64,256]{3,2,1,0:T(8,128)(2,1)S(1)} %get-tuple-element.42), channel_id=1, source_target_pairs={{4,0},{8,4},{12,8},{16,12},{20,16},{24,20},{28,24},{5,1},{9,5},{13... | collective-permute-start | bytes 983048 | tf_op jit(solution)/shard_map/ppermute | solution.py:26
  23.4 218.5 %all-gather.6.cloned.1.call-start = ((), (), s32[]{:S(2)}) async-start(), calls=%async_computation.2 | async-start | bytes 6553600 | tf_op jit(solution)/shard_map/all_gather | solution.py:153
  125.9 2.5 copy-start
  132.6 8.4 %collective-permute-start.2 = (bf16[2,5,64,256]{3,2,1,0:T(8,128)(2,1)S(1)}, bf16[2,5,64,256]{3,2,1,0:T(8,128)(2,1)S(1)}, u32[]{:S(2)}, u32[]{:S(2)}) collective-permute-start(bf16[2,5,64,256]{3,2,1,0:T(8,128)(2,1)S(1)} %get-tuple-element.39), channel_id=1, source_target_pairs={{0,4},{4,8},{8,12},{12,16},{16,20},{20,24},{24,28},{1,5},{5,9},{9,... | collective-permute-start | bytes 983048 | tf_op jit(solution)/shard_map/ppermute | solution.py:24
  136.2 9.3 %collective-permute-start.3 = (bf16[2,5,64,256]{3,2,1,0:T(8,128)(2,1)S(1)}, bf16[2,5,64,256]{3,2,1,0:T(8,128)(2,1)S(1)}, u32[]{:S(2)}, u32[]{:S(2)}) collective-permute-start(bf16[2,5,64,256]{3,2,1,0:T(8,128)(2,1)S(1)} %get-tuple-element.40), channel_id=1, source_target_pairs={{4,0},{8,4},{12,8},{16,12},{20,16},{24,20},{28,24},{5,1},{9,5},{13... | collective-permute-start | bytes 983048 | tf_op jit(solution)/shard_map/ppermute | solution.py:26
  146.7 160.2 %all-gather.8.cloned.1.call-start = ((), (), s32[]{:S(2)}) async-start(), calls=%async_computation.3 | async-start | bytes 3276800 | tf_op jit(solution)/shard_map/all_gather | solution.py:184
  246.4 2.5 copy-start.1
  253.9 61.6 %copy-start.5 = (s32[2]{0:T(128)S(1)}, s32[2]{0:T(128)}, u32[]{:S(2)}) copy-start(s32[2]{0:T(128)} %param.8) | copy-start | bytes 28
  253.9 67.6 %copy-start.4 = (f32[2,4096]{1,0:T(2,128)S(1)}, f32[2,4096]{1,0:T(2,128)}, u32[]{:S(2)}) copy-start(f32[2,4096]{1,0:T(2,128)} %param.11) | copy-start | bytes 98308
  253.9 163.9 %reduce-scatter.2.cloned.1.call-start = ((), (), s32[]{:S(2)}) async-start(), calls=%async_computation.4 | async-start | bytes 2949120 | tf_op jit(solution)/shard_map/reduce_scatter | solution.py:204
  307.0 22.9 %copy-start.2 = (bf16[4,5,256,256]{3,2,1,0:T(8,128)(2,1)S(1)}, bf16[4,5,256,256]{3,2,1,0:T(8,128)(2,1)}, u32[]{:S(2)}) copy-start(bf16[4,5,256,256]{3,2,1,0:T(8,128)(2,1)} %all-gather.8.cloned.1.call-done) | copy-start | bytes 7864324
  309.5 15.9 %collective-permute-start.4 = (bf16[1,5,256,256]{3,2,1,0:T(8,128)(2,1)}, bf16[1,5,256,256]{3,2,1,0:T(8,128)(2,1)S(1)}, u32[]{:S(2)}, u32[]{:S(2)}) collective-permute-start(bf16[1,5,256,256]{3,2,1,0:T(8,128)(2,1)} %get-tuple-element.19), channel_id=1, source_target_pairs={{0,4},{4,8},{8,12},{12,16},{16,20},{20,24},{24,28},{1,5},{5,9},{9,... | collective-permute-start | bytes 1966088 | tf_op jit(solution)/shard_map/ppermute | solution.py:24
  313.3 16.5 %collective-permute-start.5 = (bf16[1,5,256,256]{3,2,1,0:T(8,128)(2,1)}, bf16[1,5,256,256]{3,2,1,0:T(8,128)(2,1)}, u32[]{:S(2)}, u32[]{:S(2)}) collective-permute-start(bf16[1,5,256,256]{3,2,1,0:T(8,128)(2,1)} %get-tuple-element.20), channel_id=1, source_target_pairs={{4,0},{8,4},{12,8},{16,12},{20,16},{24,20},{28,24},{5,1},{9,5},{13... | collective-permute-start | bytes 1966088 | tf_op jit(solution)/shard_map/ppermute | solution.py:26
  417.8 8.9 %copy-start.3 = (bf16[6,3,64,256]{3,2,1,0:T(8,128)(2,1)S(1)}, bf16[6,3,64,256]{3,2,1,0:T(8,128)(2,1)}, u32[]{:S(2)}) copy-start(bf16[6,3,64,256]{3,2,1,0:T(8,128)(2,1)} %reduce-scatter.2.cloned.1.call-done) | copy-start | bytes 1769476
  418.8 7.9 %collective-permute-start.6 = (bf16[3,64,256]{2,1,0:T(8,128)(2,1)S(1)}, bf16[3,64,256]{2,1,0:T(8,128)(2,1)S(1)}, u32[]{:S(2)}, u32[]{:S(2)}) collective-permute-start(bf16[3,64,256]{2,1,0:T(8,128)(2,1)S(1)} %get-tuple-element.43), channel_id=1, source_target_pairs={{0,4},{4,8},{8,12},{12,16},{16,20},{20,24},{24,28},{1,5},{5,9},{9,... | collective-permute-start | bytes 294920 | tf_op jit(solution)/shard_map/ppermute | solution.py:36
  422.9 6.8 %collective-permute-start.7 = (bf16[3,64,256]{2,1,0:T(8,128)(2,1)S(1)}, bf16[3,64,256]{2,1,0:T(8,128)(2,1)S(1)}, u32[]{:S(2)}, u32[]{:S(2)}) collective-permute-start(bf16[3,64,256]{2,1,0:T(8,128)(2,1)S(1)} %get-tuple-element.44), channel_id=1, source_target_pairs={{4,0},{8,4},{12,8},{16,12},{20,16},{24,20},{28,24},{5,1},{9,5},{13... | collective-permute-start | bytes 294920 | tf_op jit(solution)/shard_map/ppermute | solution.py:36
Sparse Core Ops, SparseCore 0:
  23.5 97.7 all-gather.3
  146.9 94.9 all-gather.5
  254.0 52.8 all-gather.7
  373.1 44.6 reduce-scatter.1

commit v2 on v0

--- a/solution.py
+++ b/solution.py
@@ -1,6 +1,8 @@
 import jax
 import jax.numpy as jnp
 from jax import lax
+from jax.experimental import pallas as pl
+from jax.experimental.pallas import tpu as pltpu
 from jax.sharding import PartitionSpec as P
 
 ITERS = 2
@@ -117,7 +119,7 @@
     )
 
 
-def on_device(density, pattern, windows, basis_values, basis_grads, weights):
+def by_gathers(density, pattern, windows, basis_values, basis_grads, weights):
     row_index = lax.axis_index("row")
     band_rows = density.shape[0]
     functions = basis_values.shape[2]
@@ -165,6 +167,410 @@
     return (current, xc_matrix, densities)
 
 
+BF16 = jnp.bfloat16
+F32 = jnp.float32
+
+
+def mixed(index, turn, count):
+    return index ^ turn if count & (count - 1) == 0 else (turn - index) % count
+
+
+class Chain:
+    def __init__(self, rows, cols):
+        self.rows, self.cols, self.count = rows, cols, rows * cols
+
+    def device(self, block_row):
+        pair, step = divmod(block_row, 2 * self.cols)
+        plane, core = divmod(step, 2)
+        plane = plane if pair % 2 == 0 else self.cols - 1 - plane
+        return (2 * pair + core) * self.cols + plane
+
+    def step(self, row_index, col_index):
+        pair, core = row_index // 2, row_index % 2
+        plane = jnp.where(pair % 2 == 0, col_index, self.cols - 1 - col_index)
+        return 2 * plane + core
+
+    def to_rows(self, turn):
+        pairs = []
+        for row in range(self.rows):
+            for col in range(self.cols):
+                pairs.append((row * self.cols + col, self.device(row * self.cols + mixed(col, turn, self.cols))))
+        return pairs
+
+    def to_slices(self, turn):
+        return [(b, a) for a, b in self.to_rows(turn)]
+
+    def shift(self, by):
+        return [(self.device(i), self.device(i + by)) for i in range(self.count) if 0 <= i + by < self.count]
+
+
+BOTH = ("row", "col")
+VMEM_SPEC = pl.BlockSpec(memory_space=pltpu.VMEM)
+SMEM_SPEC = pl.BlockSpec(memory_space=pltpu.SMEM)
+
+
+def small_call(body, name, scalars, arrays, outs, scratch=()):
+    return pl.pallas_call(
+        body,
+        in_specs=[SMEM_SPEC] * len(scalars) + [VMEM_SPEC] * len(arrays),
+        out_specs=[VMEM_SPEC] * len(outs),
+        out_shape=[jax.ShapeDtypeStruct(s, d) for s, d in outs],
+        scratch_shapes=[pltpu.VMEM(s, d) for s, d in scratch],
+        compiler_params=pltpu.CompilerParams(vmem_limit_bytes=48 << 20),
+        name=name,
+    )(*scalars, *arrays)
+
+
+SENDS = ((1, 5), (2, 5), (0, 4), (0, 3))
+
+
+def join_rows(pieces, place, block):
+    cols = len(pieces)
+    high = block // cols
+
+    def body(place_ref, *refs):
+        ins, outs = refs[:cols], refs[cols:]
+        for turn in range(cols):
+            at = pl.ds(pl.multiple_of(mixed(place_ref[0], turn, cols) * high, high), high)
+            for d in range(5):
+                value = ins[turn][d]
+                outs[0][d, at] = value
+                for out, (low, top) in zip(outs[1:], SENDS):
+                    if low <= d < top:
+                        out[d - low, at] = value
+
+    shapes = [((5, block, block), BF16)] + [((top - low, block, block), BF16) for low, top in SENDS]
+    return small_call(body, "join_rows", [place], pieces, shapes)
+
+
+def exchange_rows(chain, sends):
+    return [lax.ppermute(s, BOTH, chain.shift(by)) for s, by in zip(sends, (1, 2, -1, -2))]
+
+
+def purify(own, near, kept, place, block, cols, last):
+    high = block // cols
+
+    def body(kept_ref, place_ref, own_ref, m1, m2, p1, p2, *refs):
+        outs, square = refs[:-1], refs[-1]
+
+        def right(o, far):
+            return (m2, m1, own_ref, p1, p2)[o + 2][far + (2, 2, 2, 1, 0)[o + 2]]
+
+        def product(left, d):
+            far, total = d - 2, None
+            for o in range(max(-2, far - 2), min(2, far + 2) + 1):
+                term = jnp.dot(left[o + 2], right(o, far), preferred_element_type=F32)
+                total = term if total is None else total + term
+            return jnp.where(kept_ref[d] > 0, total, 0.0)
+
+        for d in range(5):
+            square[d] = product(own_ref, d).astype(BF16)
+        for d in range(5):
+            value = 3.0 * square[d].astype(F32) - 2.0 * product(square, d)
+            value = value.astype(BF16)
+            if last:
+                outs[-1][d] = value
+            else:
+                outs[0][d] = value
+                for out, (low, top) in zip(outs[1:], SENDS):
+                    if low <= d < top:
+                        out[d - low] = value
+        if last:
+            for turn in range(cols):
+                at = pl.ds(pl.multiple_of(mixed(place_ref[0], turn, cols) * high, high), high)
+                for d in range(5):
+                    outs[turn][d] = outs[-1][d, at]
+
+    whole = ((5, block, block), BF16)
+    if last:
+        shapes = [((5, high, block), BF16)] * cols + [whole]
+    else:
+        shapes = [whole] + [((top - low, block, block), BF16) for low, top in SENDS]
+    outs = small_call(body, "purify", [kept, place], [own] + list(near), shapes, [whole])
+    return outs[:cols] if last else outs
+
+
+def join_slices(pieces, place, block):
+    cols = len(pieces)
+    high = block // cols
+
+    def body(place_ref, *refs):
+        ins, (out, down, up) = refs[:cols], refs[cols:]
+        for turn in range(cols):
+            out[mixed(place_ref[0], turn, cols)] = ins[turn][...]
+        down[...] = out[cols - 1, 2:4]
+        up[...] = out[0, 1:3]
+
+    edge = ((2, high, block), BF16)
+    return small_call(body, "join_slices", [place], pieces, [((cols, 5, high, block), BF16), edge, edge])
+
+
+def slot_of(step, half):
+    offset = step % 2
+    first = (half - offset + 2) % 2
+    return offset, first, (offset + first) // 2
+
+
+def pack_windows(purified, above, below, steps, place, tiles, functions):
+    cols, _, high, block = purified.shape
+    part = functions // 3
+    per_half = part // high
+
+    def body(steps_ref, place_ref, pur, above_ref, below_ref, *refs):
+        outs, near = refs[:-1], refs[-1]
+        for low in range(2):
+            for b in range(2):
+                at = slice(b * block, (b + 1) * block)
+                for row in range(cols + 2):
+                    if low == 0 and row == 0:
+                        near[low, row, :, at] = above_ref[b]
+                    elif low == 1 and row == cols + 1:
+                        near[low, row, :, at] = below_ref[b]
+                    elif 0 < row < cols + 1:
+                        near[low, row, :, at] = pur[row - 1, 2 - low + b]
+        half = place_ref[0] // per_half
+        for to in range(cols):
+            for tile in range(tiles):
+                step = steps_ref[to, tile]
+                offset, _, low = slot_of(step, half)
+                lanes = pl.ds(pl.multiple_of(offset * part, part), functions)
+                outs[tile][to, 0] = near[low, step // 2 + low, :, lanes]
+                outs[tile][to, 1] = near[1, step // 2 + 1, :, lanes]
+
+    return small_call(
+        body, "pack_windows", [steps, place], [purified, above, below],
+        [((cols, 2, high, functions), BF16)] * tiles, [((2, cols + 2, high, 2 * block), BF16)],
+    )
+
+
+def pointwise(n, g, w, points):
+    u = n * n + 1.0
+    a = jnp.exp(jnp.log(u) * (2.0 / 3.0))
+    ia = 1.0 / a
+    t = (g[0] * g[0] + g[1] * g[1] + g[2] * g[2]) * (ia * ia)
+    part = 1.0 / (1.0 + (mu_pbe / kappa_pbe) * t)
+    enhance = 1.0 + kappa_pbe - kappa_pbe * part
+    slope = mu_pbe * part * part
+    by_gradient = -slater_cx * slope * ia
+    by_density = -slater_cx * a * (n / u) * ((4.0 / 3.0) * enhance - (8.0 / 3.0) * t * slope)
+    scaled = w * (1.0 / points)
+    return 0.5 * by_density * scaled, [2.0 * by_gradient * scaled * gk for gk in g]
+
+
+def tile_call(tile, basis_values, basis_grads, quadrature, pieces, step, rows=1024):
+    points, functions = basis_values.shape[1:]
+    cols, _, high, _ = pieces.shape
+    part = functions // 3
+    per_half = part // high
+    count, blocks = points // rows, rows // 128
+
+    def body(step_ref, v_ref, g_ref, w_ref, pieces_ref, dens_ref, term_ref, win_ref, vs_ref, z_ref, y_ref):
+        i = pl.program_id(0)
+        offset = step_ref[0] % 2
+
+        @pl.when(i == 0)
+        def _():
+            for h in range(3):
+                for sub in range(per_half):
+                    source = per_half * ((offset + h) % 2) + sub
+                    win_ref[part * h + high * sub : part * h + high * (sub + 1)] = pieces_ref[source, h // 2]
+
+        def forward():
+            window = win_ref[...]
+            lane = lax.broadcasted_iota(jnp.int32, (128, 128), 1)
+            sums = jnp.zeros((128, 128), F32)
+            for b in range(blocks):
+                at = slice(128 * b, 128 * (b + 1))
+                v = v_ref[at]
+                x = jnp.dot(v, window, preferred_element_type=F32)
+                sums = jnp.where(lane == b, jnp.sum(x * v.astype(F32), axis=1, keepdims=True), sums)
+                for k in range(3):
+                    gk = g_ref[k, at].astype(F32)
+                    sums = jnp.where(lane == blocks * (k + 1) + b, jnp.sum(x * gk, axis=1, keepdims=True), sums)
+            sums = sums.T
+            n = sums[:blocks] * (1.0 / functions)
+            g = [sums[blocks * (k + 1) : blocks * (k + 2)] * (2.0 / functions) for k in range(3)]
+            dens_ref[...] = n
+            c0, ck = pointwise(n, g, w_ref[...], points)
+            c = jnp.concatenate([c0] + ck + [jnp.zeros((128 - 4 * blocks, 128), F32)], axis=0).T
+            for b in range(blocks):
+                at = slice(128 * b, 128 * (b + 1))
+                v = v_ref[at]
+                z = c[:, b : b + 1] * v.astype(F32)
+                for k in range(3):
+                    col = blocks * (k + 1) + b
+                    z = z + c[:, col : col + 1] * g_ref[k, at].astype(F32)
+                z_ref[i % 2, at] = z.astype(BF16)
+                vs_ref[i % 2, at] = v
+
+        def backward(first):
+            y = lax.dot_general(
+                vs_ref[(i + 1) % 2], z_ref[(i + 1) % 2], (((0,), (0,)), ((), ())), preferred_element_type=F32
+            )
+            y_ref[...] = y if first else y_ref[...] + y
+
+        @pl.when(i == 0)
+        def _():
+            forward()
+
+        @pl.when(i == 1)
+        def _():
+            backward(True)
+            forward()
+
+        @pl.when((i > 1) & (i < count))
+        def _():
+            backward(False)
+            forward()
+
+        @pl.when(i == count)
+        def _():
+            backward(False)
+            y = y_ref[...]
+            y_ref[...] = y + y.T
+            for to in range(cols):
+                _, first, _ = slot_of(step_ref[0], to // per_half)
+                start = pl.multiple_of(part * first + high * (to % per_half), high)
+                term_ref[to, 0] = y_ref[pl.ds(start, high)].astype(BF16)
+                start = 2 * part + high * (to % per_half)
+                term_ref[to, 1] = y_ref[start : start + high].astype(BF16)
+
+    def chunk(i):
+        return jnp.minimum(i, count - 1)
+
+    return pl.pallas_call(
+        body,
+        grid=(count + 1,),
+        in_specs=[
+            SMEM_SPEC,
+            pl.BlockSpec((None, rows, functions), lambda i: (tile, chunk(i), 0)),
+            pl.BlockSpec((3, None, rows, functions), lambda i: (0, tile, chunk(i), 0)),
+            pl.BlockSpec((None, blocks, 128), lambda i: (tile, chunk(i), 0)),
+            pl.BlockSpec(pieces.shape, lambda i: (0, 0, 0, 0)),
+        ],
+        out_specs=[
+            pl.BlockSpec((blocks, 128), lambda i: (chunk(i), 0)),
+            pl.BlockSpec(pieces.shape, lambda i: (0, 0, 0, 0)),
+        ],
+        out_shape=[
+            jax.ShapeDtypeStruct((points // 128, 128), F32),
+            jax.ShapeDtypeStruct(pieces.shape, BF16),
+        ],
+        scratch_shapes=[
+            pltpu.VMEM((functions, functions), BF16),
+            pltpu.VMEM((2, rows, functions), BF16),
+            pltpu.VMEM((2, rows, functions), BF16),
+            pltpu.VMEM((functions, functions), F32),
+        ],
+        compiler_params=pltpu.CompilerParams(vmem_limit_bytes=48 << 20),
+        name="tile",
+    )(step, basis_values, basis_grads, quadrature, pieces)
+
+
+def add_terms(terms, steps, place, block):
+    tiles = len(terms)
+    cols, _, high, functions = terms[0].shape
+    part = functions // 3
+    per_half = part // high
+
+    def body(steps_ref, place_ref, *refs):
+        ins, (own, to_above, to_below, total) = refs[:tiles], refs[tiles:]
+        total[...] = jnp.zeros(total.shape, F32)
+        half = place_ref[0] // per_half
+        for source in range(cols):
+            for tile in range(tiles):
+                step = steps_ref[source, tile]
+                offset, first, low = slot_of(step, half)
+                lanes = pl.ds(pl.multiple_of(offset * part, part), functions)
+                total[low, step // 2 + low, :, lanes] += ins[tile][source, 0].astype(F32)
+
+                @pl.when(first == 0)
+                def _():
+                    total[1, step // 2 + 1, :, lanes] += ins[tile][source, 1].astype(F32)
+
+        for row in range(1, cols + 1):
+            own[row - 1, 0] = total[1, row, :, :block]
+            own[row - 1, 1] = total[1, row, :, block:] + total[0, row, :, :block]
+            own[row - 1, 2] = total[0, row, :, block:]
+        for b in range(2):
+            at = slice(b * block, (b + 1) * block)
+            to_above[b] = total[0, 0, :, at].astype(BF16)
+            to_below[b] = total[1, cols + 1, :, at].astype(BF16)
+
+    edge = ((2, high, block), BF16)
+    return small_call(
+        body, "add_terms", [steps, place], list(terms),
+        [((cols, 3, high, block), F32), edge, edge], [((2, cols + 2, high, 2 * block), F32)],
+    )
+
+
+def by_block_rows(density, pattern, windows, basis_values, basis_grads, weights):
+    rows, cols = lax.axis_size("row"), lax.axis_size("col")
+    row_index, col_index = lax.axis_index("row"), lax.axis_index("col")
+    block = density.shape[3]
+    tiles, points, functions = basis_values.shape
+    chain = Chain(rows, cols)
+    step_here = chain.step(row_index, col_index)
+    place = (step_here % cols).astype(jnp.int32).reshape(1)
+    slice_here = col_index.astype(jnp.int32).reshape(1)
+    kept = (pattern > 0)[:, :, None, None]
+    masked = jnp.where(kept, density, jnp.zeros_like(density))
+    pieces = []
+    for turn in range(cols):
+        piece = lax.dynamic_index_in_dim(masked, mixed(col_index, turn, cols), 0, keepdims=False)
+        pieces.append(lax.ppermute(piece, BOTH, chain.to_rows(turn)))
+    other = lax.ppermute(pattern, "row", [(i, i ^ 1) for i in range(rows)])
+    pattern_two = jnp.where(
+        row_index % 2 == 0, jnp.concatenate([pattern, other]), jnp.concatenate([other, pattern])
+    )
+    kept_row = lax.dynamic_index_in_dim(pattern_two, step_here, 0, keepdims=False)
+    steps_here = (windows - (2 * cols * row_index - 2)).astype(jnp.int32)
+    steps = lax.all_to_all(jnp.broadcast_to(steps_here, (cols, tiles)), "col", 0, 0, tiled=True)
+
+    own, *sends = join_rows(pieces, place, block)
+    for iteration in range(ITERS):
+        near = exchange_rows(chain, sends)
+        out = purify(own, near, kept_row, place, block, cols, iteration == ITERS - 1)
+        own, sends = out[0], out[1:]
+    pieces = [lax.ppermute(p, BOTH, chain.to_slices(turn)) for turn, p in enumerate(out)]
+    purified, down, up = join_slices(pieces, slice_here, block)
+    above = shifted_2(down, "row", 1)
+    below = shifted_2(up, "row", -1)
+    sent = pack_windows(purified, above, below, steps, slice_here, tiles, functions)
+
+    quadrature = weights.reshape(tiles, points // 128, 128)
+    densities, terms = [], []
+    for tile in range(tiles):
+        window = lax.all_to_all(sent[tile], "col", 0, 0, tiled=True)
+        dens, term = tile_call(
+            tile, basis_values, basis_grads, quadrature, window, steps_here[tile : tile + 1]
+        )
+        densities.append(dens.reshape(points))
+        terms.append(lax.all_to_all(term, "col", 0, 0, tiled=True))
+    mine, to_above, to_below = add_terms(terms, steps, slice_here, block)
+    from_below = shifted_2(to_above, "row", -1).astype(F32)
+    from_above = shifted_2(to_below, "row", 1).astype(F32)
+    first = jnp.pad(from_above[None], ((0, cols - 1), (0, 1), (0, 0), (0, 0)))
+    last = jnp.pad(from_below[None], ((cols - 1, 0), (1, 0), (0, 0), (0, 0)))
+    summed = mine + first + last
+    xc_matrix = jnp.where(kept, jnp.pad(summed, ((0, 0), (1, 1), (0, 0), (0, 0))), 0.0)
+    return purified, xc_matrix, jnp.stack(densities)
+
+
+def on_device(density, pattern, windows, basis_values, basis_grads, weights):
+    rows, cols = lax.axis_size("row"), lax.axis_size("col")
+    band_rows, block, functions = density.shape[0], density.shape[3], basis_values.shape[2]
+    fits = (
+        band_rows == cols
+        and rows % 2 == 0
+        and 2 * functions == 3 * block
+        and functions // 3 % density.shape[2] == 0
+        and basis_values.shape[1] % 1024 == 0
+    )
+    plan = by_block_rows if fits else by_gathers
+    return plan(density, pattern, windows, basis_values, basis_grads, weights)
+
+
 def solution(mesh):
     placed = (
         P("row", None, "col", None),

time: 503 us -> 187 us (0.37)
  waiting for transfers between devices: 323 us -> 39.9 us
  local copies, waits for them, and re-layouts: 51.5 us -> 1.84 us
  other arithmetic: 52.2 us -> 3.81 us
  starting transfers between devices: 23.2 us -> 68 us
  Pallas kernels: 0 us -> 36.8 us
  blocking collectives: 0 us -> 33.3 us
  matrix products: 32.1 us -> 0 us
  between operations: 14.1 us -> 1.01 us
  loops' own time: 5.51 us -> 0 us
    all_gather x3 -> x0, waiting for transfers between devices: 246 us -> none  [the longest x2 193 us: times_current(): lax.all_gather(near_right, 'col', axis=2, tiled=True)]
    reduce_scatter x1 -> x0, waiting for transfers between devices: 44.7 us -> none  [on_device(): lax.psum_scatter(local_terms.astype(jnp.bfloat16), 'col', scatter_dimensi...]
    pallas_call x0 -> x8, Pallas kernels: none -> 36.8 us  [the longest x2 27.5 us: tile_call(): pl.pallas_call(body, grid=(count + 1,), in_specs=[SMEM_SPEC, pl.BlockSpec...]
    reduce_sum x6 -> x0, other arithmetic: 33.6 us -> none  [the longest x2 19.9 us: tile_terms(): jnp.sum(((2.0 * by_gradient * scaled)[None] * slopes)[:, :, None] * grads...]
    all_to_all x0 -> x3, blocking collectives: none -> 33.3 us  [the longest x1 12.7 us: by_block_rows(): window = lax.all_to_all(sent[tile], 'col', 0, 0, tiled=True)]
    dot_general x24 -> x0, matrix products: 32.1 us -> none  [the longest x2 14.7 us: tile_terms(): jnp.dot(values, window_block, preferred_element_type=jnp.float32)]
    ppermute x6 -> x17, starting transfers between devices: 17.1 us -> 41.8 us  [the longest x8 27 us: exchange_rows(): lax.ppermute(s, BOTH, chain.shift(by))]
    dot_general x4 -> x0, local copies, waits for them, and re-layouts: 15.9 us -> none  [the longest x2 13.1 us: tile_terms(): jnp.dot(values, window_block, preferred_element_type=jnp.float32)]
  transfers between devices with their start and end apart: 12 -> 23, of which waited for: 11 -> 11; matrix products, arithmetic and copies ran while one was open for 0% -> 1% of each run, Pallas kernels for 0% -> 15%
where the time goes in v2:
time: 187 us; the launch traced here: 185 us
  starting transfers between devices  68 us (36%)
  waiting for transfers between devices  39.9 us (21%)
  Pallas kernels  36.8 us (20%)
  blocking collectives  33.3 us (18%)
  other arithmetic  3.81 us (2%)
    pallas_call x2, Pallas kernels, tile_call(): pl.pallas_call(body, grid=(count + 1,), in_specs=[SMEM_SPEC, pl.BlockSpec...  27.5 us
    ppermute x8, starting transfers between devices, exchange_rows(): lax.ppermute(s, BOTH, chain.shift(by))  27 us
    ppermute x8, waiting for transfers between devices, exchange_rows(): lax.ppermute(s, BOTH, chain.shift(by))  19.5 us
    ppermute x4, starting transfers between devices, shifted_2(): return lax.ppermute(value, axis, pairs)  18.1 us
    all_to_all x1, blocking collectives, by_block_rows(): window = lax.all_to_all(sent[tile], 'col', 0, 0, tiled=True)  12.7 us
    all_to_all x1, blocking collectives, by_block_rows(): terms.append(lax.all_to_all(term, 'col', 0, 0, tiled=True))  12.2 us
    pallas_call x6, Pallas kernels, small_call(): pl.pallas_call(body, in_specs=[SMEM_SPEC] * len(scalars) + [VMEM_SPEC] *...  9.29 us
    ppermute x4, waiting for transfers between devices, by_block_rows(): lax.ppermute(p, BOTH, chain.to_slices(turn))  8.42 us
  transfers between devices with their start and end apart: 23, of which 11 were waited for; matrix products, arithmetic and copies ran while one was open for 1% of the time, Pallas kernels for 15%

profile of v2, /device:TPU:3, one launch (start us, length us, event | category | flops | bytes accessed | tf_op | source)
XLA Modules:
  0.0 184.8 jit_solution(4600725825588953431)
XLA Ops:
  0.6 0.7 broadcast_compare_fusion
  1.3 1.2 broadcast_select_fusion
  2.6 3.8 %collective-permute-start.1 = (bf16[5,64,256]{2,1,0:T(8,128)(2,1)S(1)}, bf16[5,64,256]{2,1,0:T(8,128)(2,1)S(1)}, u32[]{:S(2)}, u32[]{:S(2)}) collective-permute-start(bf16[5,64,256]{2,1,0:T(8,128)(2,1)S(1)} %get-tuple-element.58), channel_id=1, source_target_pairs={{0,0},{1,4},{2,1},{3,5},{4,2},{5,6},{6,3},{7,7},{8,11},{9,15},{10,... | collective-permute-start | bytes 491528 | tf_op jit(solution)/shard_map/ppermute | solution.py:521
  6.5 2.5 %collective-permute-start.3 = (bf16[5,64,256]{2,1,0:T(8,128)(2,1)S(1)}, bf16[5,64,256]{2,1,0:T(8,128)(2,1)S(1)}, u32[]{:S(2)}, u32[]{:S(2)}) collective-permute-start(bf16[5,64,256]{2,1,0:T(8,128)(2,1)S(1)} %get-tuple-element.56), channel_id=1, source_target_pairs={{0,1},{1,5},{2,0},{3,4},{4,3},{5,7},{6,2},{7,6},{8,10},{9,14},{10,... | collective-permute-start | bytes 491528 | tf_op jit(solution)/shard_map/ppermute | solution.py:521
  8.9 0.7 collective-permute-start.4
  9.7 1.8 collective-permute-done.1.refs_0_
  11.5 3.2 %collective-permute-done.2.refs_1_ = bf16[5,64,256]{2,1,0:T(8,128)(2,1)S(1)} collective-permute-done((bf16[5,64,256]{2,1,0:T(8,128)(2,1)S(1)}, bf16[5,64,256]{2,1,0:T(8,128)(2,1)S(1)}, u32[]{:S(2)}, u32[]{:S(2)}) %collective-permute-start.2) | collective-permute-done | bytes 163872 | tf_op jit(solution)/shard_map/ppermute | solution.py:521
  14.7 2.4 %collective-permute-done.3.refs_2_ = bf16[5,64,256]{2,1,0:T(8,128)(2,1)S(1)} collective-permute-done((bf16[5,64,256]{2,1,0:T(8,128)(2,1)S(1)}, bf16[5,64,256]{2,1,0:T(8,128)(2,1)S(1)}, u32[]{:S(2)}, u32[]{:S(2)}) %collective-permute-start.3) | collective-permute-done | bytes 163872 | tf_op jit(solution)/shard_map/ppermute | solution.py:521
  17.2 1.0 join_rows.1
  18.2 7.9 %collective-permute-start.5 = (bf16[4,256,256]{2,1,0:T(8,128)(2,1)S(1)}, bf16[4,256,256]{2,1,0:T(8,128)(2,1)S(1)}, u32[]{:S(2)}, u32[]{:S(2)}) collective-permute-start(bf16[4,256,256]{2,1,0:T(8,128)(2,1)S(1)} %get-tuple-element.30), channel_id=1, source_target_pairs={{0,4},{4,1},{1,5},{5,2},{2,6},{6,3},{3,7},{7,11},{11,15},{15,10},{... | collective-permute-start | bytes 1572872 | tf_op jit(solution)/shard_map/ppermute | solution.py:247
  26.1 1.9 %collective-permute-start.7 = (bf16[4,256,256]{2,1,0:T(8,128)(2,1)S(1)}, bf16[4,256,256]{2,1,0:T(8,128)(2,1)S(1)}, u32[]{:S(2)}, u32[]{:S(2)}) collective-permute-start(bf16[4,256,256]{2,1,0:T(8,128)(2,1)S(1)} %get-tuple-element.32), channel_id=1, source_target_pairs={{4,0},{1,4},{5,1},{2,5},{6,2},{3,6},{7,3},{11,7},{15,11},{10,15},{... | collective-permute-start | bytes 1572872 | tf_op jit(solution)/shard_map/ppermute | solution.py:247
  28.0 3.6 %collective-permute-start.6 = (bf16[3,256,256]{2,1,0:T(8,128)(2,1)}, bf16[3,256,256]{2,1,0:T(8,128)(2,1)S(1)}, u32[]{:S(2)}, u32[]{:S(2)}) collective-permute-start(bf16[3,256,256]{2,1,0:T(8,128)(2,1)} %get-tuple-element.31), channel_id=1, source_target_pairs={{0,1},{4,5},{1,2},{5,6},{2,3},{6,7},{3,11},{7,15},{11,10},{15,14},... | collective-permute-start | bytes 1179656 | tf_op jit(solution)/shard_map/ppermute | solution.py:247
  31.6 1.9 %collective-permute-start.8 = (bf16[3,256,256]{2,1,0:T(8,128)(2,1)}, bf16[3,256,256]{2,1,0:T(8,128)(2,1)S(1)}, u32[]{:S(2)}, u32[]{:S(2)}) collective-permute-start(bf16[3,256,256]{2,1,0:T(8,128)(2,1)} %get-tuple-element.33), channel_id=1, source_target_pairs={{1,0},{5,4},{2,1},{6,5},{3,2},{7,6},{11,3},{15,7},{10,11},{14,15},... | collective-permute-start | bytes 1179656 | tf_op jit(solution)/shard_map/ppermute | solution.py:247
  33.6 1.4 collective-permute-start
  35.0 0.8 collective-permute-done
  35.8 4.5 %collective-permute-done.6.m2 = bf16[3,256,256]{2,1,0:T(8,128)(2,1)S(1)} collective-permute-done((bf16[3,256,256]{2,1,0:T(8,128)(2,1)}, bf16[3,256,256]{2,1,0:T(8,128)(2,1)S(1)}, u32[]{:S(2)}, u32[]{:S(2)}) %collective-permute-start.6) | collective-permute-done | bytes 393248 | tf_op jit(solution)/shard_map/ppermute | solution.py:247
  40.3 4.6 %collective-permute-done.8.p2 = bf16[3,256,256]{2,1,0:T(8,128)(2,1)S(1)} collective-permute-done((bf16[3,256,256]{2,1,0:T(8,128)(2,1)}, bf16[3,256,256]{2,1,0:T(8,128)(2,1)S(1)}, u32[]{:S(2)}, u32[]{:S(2)}) %collective-permute-start.8) | collective-permute-done | bytes 393248 | tf_op jit(solution)/shard_map/ppermute | solution.py:247
  44.9 2.0 %purify.2 = (bf16[5,256,256]{2,1,0:T(8,128)(2,1)S(1)}, bf16[4,256,256]{2,1,0:T(8,128)(2,1)S(1)}, bf16[3,256,256]{2,1,0:T(8,128)(2,1)S(1)}, bf16[4,256,256]{2,1,0:T(8,128)(2,1)S(1)}, bf16[3,256,256]{2,1,0:T(8,128)(2,1)S(1)}) custom-call(s32[5]{0:T(128)S(1)} %fusion.kept_ref, s32[1]{0:T(128)} %bitcast.2.place_ref, ...), custom_call_target="tpu_custom_call" | custom-call | tf_op jit(solution)/shard_map/purify/pallas_call | solution.py:213
  46.9 3.7 %collective-permute-start.11 = (bf16[4,256,256]{2,1,0:T(8,128)(2,1)S(1)}, bf16[4,256,256]{2,1,0:T(8,128)(2,1)S(1)}, u32[]{:S(2)}, u32[]{:S(2)}) collective-permute-start(bf16[4,256,256]{2,1,0:T(8,128)(2,1)S(1)} %get-tuple-element.37), channel_id=1, source_target_pairs={{4,0},{1,4},{5,1},{2,5},{6,2},{3,6},{7,3},{11,7},{15,11},{10,15},{... | collective-permute-start | bytes 1572872 | tf_op jit(solution)/shard_map/ppermute | solution.py:247
  50.6 2.8 %collective-permute-start.9 = (bf16[4,256,256]{2,1,0:T(8,128)(2,1)S(1)}, bf16[4,256,256]{2,1,0:T(8,128)(2,1)S(1)}, u32[]{:S(2)}, u32[]{:S(2)}) collective-permute-start(bf16[4,256,256]{2,1,0:T(8,128)(2,1)S(1)} %get-tuple-element.35), channel_id=1, source_target_pairs={{0,4},{4,1},{1,5},{5,2},{2,6},{6,3},{3,7},{7,11},{11,15},{15,10},{... | collective-permute-start | bytes 1572872 | tf_op jit(solution)/shard_map/ppermute | solution.py:247
  53.4 1.9 %collective-permute-start.10 = (bf16[3,256,256]{2,1,0:T(8,128)(2,1)S(1)}, bf16[3,256,256]{2,1,0:T(8,128)(2,1)S(1)}, u32[]{:S(2)}, u32[]{:S(2)}) collective-permute-start(bf16[3,256,256]{2,1,0:T(8,128)(2,1)S(1)} %get-tuple-element.36), channel_id=1, source_target_pairs={{0,1},{4,5},{1,2},{5,6},{2,3},{6,7},{3,11},{7,15},{11,10},{15,14},... | collective-permute-start | bytes 1179656 | tf_op jit(solution)/shard_map/ppermute | solution.py:247
  55.3 3.4 %collective-permute-start.12 = (bf16[3,256,256]{2,1,0:T(8,128)(2,1)S(1)}, bf16[3,256,256]{2,1,0:T(8,128)(2,1)S(1)}, u32[]{:S(2)}, u32[]{:S(2)}) collective-permute-start(bf16[3,256,256]{2,1,0:T(8,128)(2,1)S(1)} %get-tuple-element.38), channel_id=1, source_target_pairs={{1,0},{5,4},{2,1},{6,5},{3,2},{7,6},{11,3},{15,7},{10,11},{14,15},... | collective-permute-start | bytes 1179656 | tf_op jit(solution)/shard_map/ppermute | solution.py:247
  58.7 10.4 %collective-permute-done.10.m2 = bf16[3,256,256]{2,1,0:T(8,128)(2,1)S(1)} collective-permute-done((bf16[3,256,256]{2,1,0:T(8,128)(2,1)S(1)}, bf16[3,256,256]{2,1,0:T(8,128)(2,1)S(1)}, u32[]{:S(2)}, u32[]{:S(2)}) %collective-permute-start.10) | collective-permute-done | bytes 393248 | tf_op jit(solution)/shard_map/ppermute | solution.py:247
  69.1 2.9 %purify.3 = (bf16[5,64,256]{2,1,0:T(8,128)(2,1)S(1)}, bf16[5,64,256]{2,1,0:T(8,128)(2,1)S(1)}, bf16[5,64,256]{2,1,0:T(8,128)(2,1)S(1)}, bf16[5,64,256]{2,1,0:T(8,128)(2,1)S(1)}, bf16[5,256,256]{2,1,0:T(8,128)(2,1)}) custom-call(s32[5]{0:T(128)S(1)} %fusion.kept_ref, s32[1]{0:T(128)} %bitcast.2.place_ref, bf16[5,256,256]{2,1,0:T(8,128)(2,1)S(1)} %get-tuple-element.34.own_ref, ...), custom_call_target="tpu_custom_call" | custom-call | tf_op jit(solution)/shard_map/purify/pallas_call | solution.py:213
  72.0 4.2 %collective-permute-start.13 = (bf16[5,64,256]{2,1,0:T(8,128)(2,1)S(1)}, bf16[5,64,256]{2,1,0:T(8,128)(2,1)S(1)}, u32[]{:S(2)}, u32[]{:S(2)}) collective-permute-start(bf16[5,64,256]{2,1,0:T(8,128)(2,1)S(1)} %get-tuple-element.39), channel_id=1, source_target_pairs={{0,0},{4,1},{1,2},{5,3},{2,4},{6,5},{3,6},{7,7},{11,8},{15,9},{10,... | collective-permute-start | bytes 491528 | tf_op jit(solution)/shard_map/ppermute | solution.py:535
  76.3 1.5 collective-permute-start.15
  77.8 0.7 collective-permute-start.16
  78.4 1.8 collective-permute-done.13.refs_0_
  80.3 3.8 %collective-permute-done.14.refs_1_ = bf16[5,64,256]{2,1,0:T(8,128)(2,1)S(1)} collective-permute-done((bf16[5,64,256]{2,1,0:T(8,128)(2,1)S(1)}, bf16[5,64,256]{2,1,0:T(8,128)(2,1)S(1)}, u32[]{:S(2)}, u32[]{:S(2)}) %collective-permute-start.14) | collective-permute-done | bytes 163872 | tf_op jit(solution)/shard_map/ppermute | solution.py:535
  84.1 2.8 %collective-permute-done.15.refs_2_ = bf16[5,64,256]{2,1,0:T(8,128)(2,1)S(1)} collective-permute-done((bf16[5,64,256]{2,1,0:T(8,128)(2,1)S(1)}, bf16[5,64,256]{2,1,0:T(8,128)(2,1)S(1)}, u32[]{:S(2)}, u32[]{:S(2)}) %collective-permute-start.15) | collective-permute-done | bytes 163872 | tf_op jit(solution)/shard_map/ppermute | solution.py:535
  86.9 0.9 join_slices.1
  87.7 5.3 %collective-permute-start.17 = (bf16[2,64,256]{2,1,0:T(8,128)(2,1)S(1)}, bf16[2,64,256]{2,1,0:T(8,128)(2,1)S(1)}, u32[]{:S(2)}, u32[]{:S(2)}) collective-permute-start(bf16[2,64,256]{2,1,0:T(8,128)(2,1)S(1)} %get-tuple-element.44), channel_id=1, source_target_pairs={{0,4},{4,8},{8,12},{12,16},{16,20},{20,24},{24,28},{1,5},{5,9},{9,... | collective-permute-start | bytes 196616 | tf_op jit(solution)/shard_map/ppermute | solution.py:36
  93.0 4.2 %collective-permute-start.18 = (bf16[2,64,256]{2,1,0:T(8,128)(2,1)S(1)}, bf16[2,64,256]{2,1,0:T(8,128)(2,1)S(1)}, u32[]{:S(2)}, u32[]{:S(2)}) collective-permute-start(bf16[2,64,256]{2,1,0:T(8,128)(2,1)S(1)} %get-tuple-element.45), channel_id=1, source_target_pairs={{4,0},{8,4},{12,8},{16,12},{20,16},{24,20},{28,24},{5,1},{9,5},{13... | collective-permute-start | bytes 196616 | tf_op jit(solution)/shard_map/ppermute | solution.py:36
  97.3 8.4 %all_to_all.28 = s32[4,1,2]{2,1,0:T(1,128)S(1)} all-to-all(s32[4,1,2]{2,1,0:T(1,128)S(1)} %broadcast_in_dim.35), channel_id=1, replica_groups=mesh['row'=8,'col'=4] {'col'}, dimensions={0} | all-to-all | bytes 64 | tf_op jit(solution)/shard_map/all_to_all | solution.py:528
  105.7 1.1 copy-done
  106.8 1.5 pack_windows.1
  108.2 12.7 %all_to_all.29.pieces_ref = bf16[4,2,64,384]{3,2,1,0:T(8,128)(2,1)S(1)} all-to-all(bf16[4,2,64,384]{3,2,1,0:T(8,128)(2,1)S(1)} %get-tuple-element.48), channel_id=1, replica_groups=mesh['row'=8,'col'=4] {'col'}, dimensions={0} | all-to-all | bytes 786432 | tf_op jit(solution)/shard_map/all_to_all | solution.py:544
  121.0 3.6 %all-to-all-start.1 = ((bf16[4,2,64,384]{3,2,1,0:T(8,128)(2,1)}), bf16[4,2,64,384]{3,2,1,0:T(8,128)(2,1)S(1)}, u32[]{:S(2)}, u32[]{:S(2)}) async-start(bf16[4,2,64,384]{3,2,1,0:T(8,128)(2,1)} %get-tuple-element.46), calls=%async_computation.1 | async-start | bytes 786432 | tf_op jit(solution)/shard_map/all_to_all | solution.py:544
  124.6 0.7 fusion.1
  125.3 14.2 %tile.3 = (f32[32,128]{1,0:T(8,128)S(1)}, bf16[4,2,64,384]{3,2,1,0:T(8,128)(2,1)}) custom-call(s32[1]{0:T(128)} %get-tuple-element.59.step_ref, bf16[2,4096,384]{2,1,0:T(8,128)(2,1)} %v_ref.3, bf16[3,2,4096,384]{3,2,1,0:T(8,128)(2,1)} %g_ref.3, f32[2,32,128]{2,1,0:T(8,128)S(1)} %bitcast.21, bf16[4,2,64,384]{3,2,1,0:T(8,128)(2,1)S(1)} %all_to_all.29.pieces_ref), custom_call_target="tpu_custom_call" | custom-call | tf_op jit(solution)/shard_map/tile/pallas_call | solution.py:441
  139.5 4.5 %all-to-all-start.4 = ((bf16[4,2,64,384]{3,2,1,0:T(8,128)(2,1)}), bf16[4,2,64,384]{3,2,1,0:T(8,128)(2,1)S(1)}, u32[]{:S(2)}, u32[]{:S(2)}) async-start(bf16[4,2,64,384]{3,2,1,0:T(8,128)(2,1)} %get-tuple-element.49), calls=%async_computation.4 | async-start | bytes 786432 | tf_op jit(solution)/shard_map/all_to_all | solution.py:549
  143.9 13.4 %tile.2 = (f32[32,128]{1,0:T(8,128)S(1)}, bf16[4,2,64,384]{3,2,1,0:T(8,128)(2,1)S(1)}) custom-call(s32[1]{0:T(128)} %get-tuple-element.60.step_ref, bf16[2,4096,384]{2,1,0:T(8,128)(2,1)} %v_ref.3, bf16[3,2,4096,384]{3,2,1,0:T(8,128)(2,1)} %g_ref.3, f32[2,32,128]{2,1,0:T(8,128)S(1)} %bitcast.22, bf16[4,2,64,384]{3,2,1,0:T(8,128)(2,1)S(1)} %all-to-all-done.1.pieces_ref), custom_call_target="tpu_custom_call" | custom-call | tf_op jit(solution)/shard_map/tile/pallas_call | solution.py:441
  157.4 12.2 %all_to_all.30.refs_0_ = bf16[4,2,64,384]{3,2,1,0:T(8,128)(2,1)S(1)} all-to-all(bf16[4,2,64,384]{3,2,1,0:T(8,128)(2,1)S(1)} %get-tuple-element.47), channel_id=1, replica_groups=mesh['row'=8,'col'=4] {'col'}, dimensions={0} | all-to-all | bytes 786432 | tf_op jit(solution)/shard_map/all_to_all | solution.py:549
  169.6 1.0 add_terms.1
  170.6 6.4 %collective-permute-start.19 = (bf16[2,64,256]{2,1,0:T(8,128)(2,1)S(1)}, bf16[2,64,256]{2,1,0:T(8,128)(2,1)S(1)}, u32[]{:S(2)}, u32[]{:S(2)}) collective-permute-start(bf16[2,64,256]{2,1,0:T(8,128)(2,1)S(1)} %get-tuple-element.51), channel_id=1, source_target_pairs={{0,4},{4,8},{8,12},{12,16},{16,20},{20,24},{24,28},{1,5},{5,9},{9,... | collective-permute-start | bytes 196616 | tf_op jit(solution)/shard_map/ppermute | solution.py:36
  177.0 2.1 %collective-permute-start.20 = (bf16[2,64,256]{2,1,0:T(8,128)(2,1)S(1)}, bf16[2,64,256]{2,1,0:T(8,128)(2,1)S(1)}, u32[]{:S(2)}, u32[]{:S(2)}) collective-permute-start(bf16[2,64,256]{2,1,0:T(8,128)(2,1)S(1)} %get-tuple-element.52), channel_id=1, source_target_pairs={{4,0},{8,4},{12,8},{16,12},{20,16},{24,20},{28,24},{5,1},{9,5},{13... | collective-permute-start | bytes 196616 | tf_op jit(solution)/shard_map/ppermute | solution.py:36
  179.8 3.7 %collective-permute-done.20 = bf16[2,64,256]{2,1,0:T(8,128)(2,1)S(1)} collective-permute-done((bf16[2,64,256]{2,1,0:T(8,128)(2,1)S(1)}, bf16[2,64,256]{2,1,0:T(8,128)(2,1)S(1)}, u32[]{:S(2)}, u32[]{:S(2)}) %collective-permute-start.20) | collective-permute-done | bytes 65568 | tf_op jit(solution)/shard_map/ppermute | solution.py:36
  183.6 1.2 pad_select_fusion
  (29 shorter events, 1.0 us)
Async XLA Ops:
  2.5 31.0 %copy-start.2 = (s32[4,5]{1,0:T(4,128)S(1)}, s32[4,5]{1,0:T(4,128)}, u32[]{:S(2)}) copy-start(s32[4,5]{1,0:T(4,128)} %param.7) | copy-start | bytes 244
  2.6 8.9 %collective-permute-start.1 = (bf16[5,64,256]{2,1,0:T(8,128)(2,1)S(1)}, bf16[5,64,256]{2,1,0:T(8,128)(2,1)S(1)}, u32[]{:S(2)}, u32[]{:S(2)}) collective-permute-start(bf16[5,64,256]{2,1,0:T(8,128)(2,1)S(1)} %get-tuple-element.58), channel_id=1, source_target_pairs={{0,0},{1,4},{2,1},{3,5},{4,2},{5,6},{6,3},{7,7},{8,11},{9,15},{10,... | collective-permute-start | bytes 491528 | tf_op jit(solution)/shard_map/ppermute | solution.py:521
  6.4 8.3 %collective-permute-start.2 = (bf16[5,64,256]{2,1,0:T(8,128)(2,1)S(1)}, bf16[5,64,256]{2,1,0:T(8,128)(2,1)S(1)}, u32[]{:S(2)}, u32[]{:S(2)}) collective-permute-start(bf16[5,64,256]{2,1,0:T(8,128)(2,1)S(1)} %get-tuple-element.57), channel_id=1, source_target_pairs={{0,4},{1,0},{2,5},{3,1},{4,6},{5,2},{6,7},{7,3},{8,15},{9,11},{10,... | collective-permute-start | bytes 491528 | tf_op jit(solution)/shard_map/ppermute | solution.py:521
  6.5 10.7 %collective-permute-start.3 = (bf16[5,64,256]{2,1,0:T(8,128)(2,1)S(1)}, bf16[5,64,256]{2,1,0:T(8,128)(2,1)S(1)}, u32[]{:S(2)}, u32[]{:S(2)}) collective-permute-start(bf16[5,64,256]{2,1,0:T(8,128)(2,1)S(1)} %get-tuple-element.56), channel_id=1, source_target_pairs={{0,1},{1,5},{2,0},{3,4},{4,3},{5,7},{6,2},{7,6},{8,10},{9,14},{10,... | collective-permute-start | bytes 491528 | tf_op jit(solution)/shard_map/ppermute | solution.py:521
  8.9 8.2 %collective-permute-start.4 = (bf16[5,64,256]{2,1,0:T(8,128)(2,1)S(1)}, bf16[5,64,256]{2,1,0:T(8,128)(2,1)S(1)}, u32[]{:S(2)}, u32[]{:S(2)}) collective-permute-start(bf16[5,64,256]{2,1,0:T(8,128)(2,1)S(1)} %get-tuple-element.55), channel_id=1, source_target_pairs={{0,5},{1,1},{2,4},{3,0},{4,7},{5,3},{6,6},{7,2},{8,14},{9,10},{10,... | collective-permute-start | bytes 491528 | tf_op jit(solution)/shard_map/ppermute | solution.py:521
  18.2 26.7 %collective-permute-start.5 = (bf16[4,256,256]{2,1,0:T(8,128)(2,1)S(1)}, bf16[4,256,256]{2,1,0:T(8,128)(2,1)S(1)}, u32[]{:S(2)}, u32[]{:S(2)}) collective-permute-start(bf16[4,256,256]{2,1,0:T(8,128)(2,1)S(1)} %get-tuple-element.30), channel_id=1, source_target_pairs={{0,4},{4,1},{1,5},{5,2},{2,6},{6,3},{3,7},{7,11},{11,15},{15,10},{... | collective-permute-start | bytes 1572872 | tf_op jit(solution)/shard_map/ppermute | solution.py:247
  26.1 18.8 %collective-permute-start.7 = (bf16[4,256,256]{2,1,0:T(8,128)(2,1)S(1)}, bf16[4,256,256]{2,1,0:T(8,128)(2,1)S(1)}, u32[]{:S(2)}, u32[]{:S(2)}) collective-permute-start(bf16[4,256,256]{2,1,0:T(8,128)(2,1)S(1)} %get-tuple-element.32), channel_id=1, source_target_pairs={{4,0},{1,4},{5,1},{2,5},{6,2},{3,6},{7,3},{11,7},{15,11},{10,15},{... | collective-permute-start | bytes 1572872 | tf_op jit(solution)/shard_map/ppermute | solution.py:247
  28.0 12.2 %collective-permute-start.6 = (bf16[3,256,256]{2,1,0:T(8,128)(2,1)}, bf16[3,256,256]{2,1,0:T(8,128)(2,1)S(1)}, u32[]{:S(2)}, u32[]{:S(2)}) collective-permute-start(bf16[3,256,256]{2,1,0:T(8,128)(2,1)} %get-tuple-element.31), channel_id=1, source_target_pairs={{0,1},{4,5},{1,2},{5,6},{2,3},{6,7},{3,11},{7,15},{11,10},{15,14},... | collective-permute-start | bytes 1179656 | tf_op jit(solution)/shard_map/ppermute | solution.py:247
  31.6 13.3 %collective-permute-start.8 = (bf16[3,256,256]{2,1,0:T(8,128)(2,1)}, bf16[3,256,256]{2,1,0:T(8,128)(2,1)S(1)}, u32[]{:S(2)}, u32[]{:S(2)}) collective-permute-start(bf16[3,256,256]{2,1,0:T(8,128)(2,1)} %get-tuple-element.33), channel_id=1, source_target_pairs={{1,0},{5,4},{2,1},{6,5},{3,2},{7,6},{11,3},{15,7},{10,11},{14,15},... | collective-permute-start | bytes 1179656 | tf_op jit(solution)/shard_map/ppermute | solution.py:247
  33.6 2.2 %collective-permute-start = (s32[4,5]{1,0:T(4,128)S(1)}, s32[4,5]{1,0:T(4,128)S(1)}, u32[]{:S(2)}, u32[]{:S(2)}) collective-permute-start(s32[4,5]{1,0:T(4,128)S(1)} %copy-done.2), channel_id=1, source_target_pairs={{0,4},{4,0},{8,12},{12,8},{16,20},{20,16},{24,28},{28,24},{1,5},{5... | collective-permute-start | bytes 248 | tf_op jit(solution)/shard_map/ppermute | solution.py:522
  46.9 22.2 %collective-permute-start.11 = (bf16[4,256,256]{2,1,0:T(8,128)(2,1)S(1)}, bf16[4,256,256]{2,1,0:T(8,128)(2,1)S(1)}, u32[]{:S(2)}, u32[]{:S(2)}) collective-permute-start(bf16[4,256,256]{2,1,0:T(8,128)(2,1)S(1)} %get-tuple-element.37), channel_id=1, source_target_pairs={{4,0},{1,4},{5,1},{2,5},{6,2},{3,6},{7,3},{11,7},{15,11},{10,15},{... | collective-permute-start | bytes 1572872 | tf_op jit(solution)/shard_map/ppermute | solution.py:247
  50.6 18.6 %collective-permute-start.9 = (bf16[4,256,256]{2,1,0:T(8,128)(2,1)S(1)}, bf16[4,256,256]{2,1,0:T(8,128)(2,1)S(1)}, u32[]{:S(2)}, u32[]{:S(2)}) collective-permute-start(bf16[4,256,256]{2,1,0:T(8,128)(2,1)S(1)} %get-tuple-element.35), channel_id=1, source_target_pairs={{0,4},{4,1},{1,5},{5,2},{2,6},{6,3},{3,7},{7,11},{11,15},{15,10},{... | collective-permute-start | bytes 1572872 | tf_op jit(solution)/shard_map/ppermute | solution.py:247
  53.4 15.7 %collective-permute-start.10 = (bf16[3,256,256]{2,1,0:T(8,128)(2,1)S(1)}, bf16[3,256,256]{2,1,0:T(8,128)(2,1)S(1)}, u32[]{:S(2)}, u32[]{:S(2)}) collective-permute-start(bf16[3,256,256]{2,1,0:T(8,128)(2,1)S(1)} %get-tuple-element.36), channel_id=1, source_target_pairs={{0,1},{4,5},{1,2},{5,6},{2,3},{6,7},{3,11},{7,15},{11,10},{15,14},... | collective-permute-start | bytes 1179656 | tf_op jit(solution)/shard_map/ppermute | solution.py:247
  55.3 13.8 %collective-permute-start.12 = (bf16[3,256,256]{2,1,0:T(8,128)(2,1)S(1)}, bf16[3,256,256]{2,1,0:T(8,128)(2,1)S(1)}, u32[]{:S(2)}, u32[]{:S(2)}) collective-permute-start(bf16[3,256,256]{2,1,0:T(8,128)(2,1)S(1)} %get-tuple-element.38), channel_id=1, source_target_pairs={{1,0},{5,4},{2,1},{6,5},{3,2},{7,6},{11,3},{15,7},{10,11},{14,15},... | collective-permute-start | bytes 1179656 | tf_op jit(solution)/shard_map/ppermute | solution.py:247
  69.1 28.1 %copy-start.3 = (s32[2]{0:T(128)S(1)}, s32[2]{0:T(128)}, u32[]{:S(2)}) copy-start(s32[2]{0:T(128)} %param.8) | copy-start | bytes 28
  72.0 8.3 %collective-permute-start.13 = (bf16[5,64,256]{2,1,0:T(8,128)(2,1)S(1)}, bf16[5,64,256]{2,1,0:T(8,128)(2,1)S(1)}, u32[]{:S(2)}, u32[]{:S(2)}) collective-permute-start(bf16[5,64,256]{2,1,0:T(8,128)(2,1)S(1)} %get-tuple-element.39), channel_id=1, source_target_pairs={{0,0},{4,1},{1,2},{5,3},{2,4},{6,5},{3,6},{7,7},{11,8},{15,9},{10,... | collective-permute-start | bytes 491528 | tf_op jit(solution)/shard_map/ppermute | solution.py:535
  76.2 7.8 %collective-permute-start.14 = (bf16[5,64,256]{2,1,0:T(8,128)(2,1)S(1)}, bf16[5,64,256]{2,1,0:T(8,128)(2,1)S(1)}, u32[]{:S(2)}, u32[]{:S(2)}) collective-permute-start(bf16[5,64,256]{2,1,0:T(8,128)(2,1)S(1)} %get-tuple-element.40), channel_id=1, source_target_pairs={{4,0},{0,1},{5,2},{1,3},{6,4},{2,5},{7,6},{3,7},{15,8},{11,9},{14,... | collective-permute-start | bytes 491528 | tf_op jit(solution)/shard_map/ppermute | solution.py:535
  76.3 10.5 %collective-permute-start.15 = (bf16[5,64,256]{2,1,0:T(8,128)(2,1)S(1)}, bf16[5,64,256]{2,1,0:T(8,128)(2,1)S(1)}, u32[]{:S(2)}, u32[]{:S(2)}) collective-permute-start(bf16[5,64,256]{2,1,0:T(8,128)(2,1)S(1)} %get-tuple-element.41), channel_id=1, source_target_pairs={{1,0},{5,1},{0,2},{4,3},{3,4},{7,5},{2,6},{6,7},{10,8},{14,9},{11,... | collective-permute-start | bytes 491528 | tf_op jit(solution)/shard_map/ppermute | solution.py:535
  77.8 9.1 %collective-permute-start.16 = (bf16[5,64,256]{2,1,0:T(8,128)(2,1)S(1)}, bf16[5,64,256]{2,1,0:T(8,128)(2,1)S(1)}, u32[]{:S(2)}, u32[]{:S(2)}) collective-permute-start(bf16[5,64,256]{2,1,0:T(8,128)(2,1)S(1)} %get-tuple-element.42), channel_id=1, source_target_pairs={{5,0},{1,1},{4,2},{0,3},{7,4},{3,5},{6,6},{2,7},{14,8},{10,9},{15,... | collective-permute-start | bytes 491528 | tf_op jit(solution)/shard_map/ppermute | solution.py:535
  86.8 37.8 %copy-start.1 = (f32[2,4096]{1,0:T(2,128)S(1)}, f32[2,4096]{1,0:T(2,128)}, u32[]{:S(2)}) copy-start(f32[2,4096]{1,0:T(2,128)} %param.11) | copy-start | bytes 98308
  87.7 17.9 %collective-permute-start.17 = (bf16[2,64,256]{2,1,0:T(8,128)(2,1)S(1)}, bf16[2,64,256]{2,1,0:T(8,128)(2,1)S(1)}, u32[]{:S(2)}, u32[]{:S(2)}) collective-permute-start(bf16[2,64,256]{2,1,0:T(8,128)(2,1)S(1)} %get-tuple-element.44), channel_id=1, source_target_pairs={{0,4},{4,8},{8,12},{12,16},{16,20},{20,24},{24,28},{1,5},{5,9},{9,... | collective-permute-start | bytes 196616 | tf_op jit(solution)/shard_map/ppermute | solution.py:36
  93.0 12.7 %collective-permute-start.18 = (bf16[2,64,256]{2,1,0:T(8,128)(2,1)S(1)}, bf16[2,64,256]{2,1,0:T(8,128)(2,1)S(1)}, u32[]{:S(2)}, u32[]{:S(2)}) collective-permute-start(bf16[2,64,256]{2,1,0:T(8,128)(2,1)S(1)} %get-tuple-element.45), channel_id=1, source_target_pairs={{4,0},{8,4},{12,8},{16,12},{20,16},{24,20},{28,24},{5,1},{9,5},{13... | collective-permute-start | bytes 196616 | tf_op jit(solution)/shard_map/ppermute | solution.py:36
  105.7 1.1 copy-start
  121.0 18.5 %all-to-all-start.1 = ((bf16[4,2,64,384]{3,2,1,0:T(8,128)(2,1)}), bf16[4,2,64,384]{3,2,1,0:T(8,128)(2,1)S(1)}, u32[]{:S(2)}, u32[]{:S(2)}) async-start(bf16[4,2,64,384]{3,2,1,0:T(8,128)(2,1)} %get-tuple-element.46), calls=%async_computation.1 | async-start | bytes 786432 | tf_op jit(solution)/shard_map/all_to_all | solution.py:544
  139.5 17.9 %all-to-all-start.4 = ((bf16[4,2,64,384]{3,2,1,0:T(8,128)(2,1)}), bf16[4,2,64,384]{3,2,1,0:T(8,128)(2,1)S(1)}, u32[]{:S(2)}, u32[]{:S(2)}) async-start(bf16[4,2,64,384]{3,2,1,0:T(8,128)(2,1)} %get-tuple-element.49), calls=%async_computation.4 | async-start | bytes 786432 | tf_op jit(solution)/shard_map/all_to_all | solution.py:549
  170.6 9.2 %collective-permute-start.19 = (bf16[2,64,256]{2,1,0:T(8,128)(2,1)S(1)}, bf16[2,64,256]{2,1,0:T(8,128)(2,1)S(1)}, u32[]{:S(2)}, u32[]{:S(2)}) collective-permute-start(bf16[2,64,256]{2,1,0:T(8,128)(2,1)S(1)} %get-tuple-element.51), channel_id=1, source_target_pairs={{0,4},{4,8},{8,12},{12,16},{16,20},{20,24},{24,28},{1,5},{5,9},{9,... | collective-permute-start | bytes 196616 | tf_op jit(solution)/shard_map/ppermute | solution.py:36
  177.0 6.5 %collective-permute-start.20 = (bf16[2,64,256]{2,1,0:T(8,128)(2,1)S(1)}, bf16[2,64,256]{2,1,0:T(8,128)(2,1)S(1)}, u32[]{:S(2)}, u32[]{:S(2)}) collective-permute-start(bf16[2,64,256]{2,1,0:T(8,128)(2,1)S(1)} %get-tuple-element.52), channel_id=1, source_target_pairs={{4,0},{8,4},{12,8},{16,12},{20,16},{24,20},{28,24},{5,1},{9,5},{13... | collective-permute-start | bytes 196616 | tf_op jit(solution)/shard_map/ppermute | solution.py:36

commit v3 on v2

--- a/solution.py
+++ b/solution.py
@@ -221,60 +221,115 @@
     )(*scalars, *arrays)
 
 
+HELD = (0, 2, 3)
 SENDS = ((1, 5), (2, 5), (0, 4), (0, 3))
 
 
-def join_rows(pieces, place, block):
-    cols = len(pieces)
+def join_rows(pieces, steps, place, slice_here, block):
+    cols, tiles = len(pieces), steps[0].shape[0]
     high = block // cols
 
-    def body(place_ref, *refs):
-        ins, outs = refs[:cols], refs[cols:]
+    def body(place_ref, slice_ref, *refs):
+        step_ins, ins = refs[:cols], refs[cols : 2 * cols]
+        own, up, down, steps_out = refs[2 * cols :]
         for turn in range(cols):
+            for tile in range(tiles):
+                steps_out[mixed(slice_ref[0], turn, cols), tile] = step_ins[turn][tile]
             at = pl.ds(pl.multiple_of(mixed(place_ref[0], turn, cols) * high, high), high)
-            for d in range(5):
-                value = ins[turn][d]
-                outs[0][d, at] = value
-                for out, (low, top) in zip(outs[1:], SENDS):
-                    if low <= d < top:
-                        out[d - low, at] = value
-
-    shapes = [((5, block, block), BF16)] + [((top - low, block, block), BF16) for low, top in SENDS]
-    return small_call(body, "join_rows", [place], pieces, shapes)
+            for k in range(3):
+                value = ins[turn][k]
+                own[k, at] = value
+                if k > 0:
+                    up[k - 1, at] = value
+                if k < 2:
+                    down[k, at] = value
+
+    two, three = ((2, block, block), BF16), ((3, block, block), BF16)
+    return pl.pallas_call(
+        body,
+        in_specs=[SMEM_SPEC] * (2 + cols) + [VMEM_SPEC] * cols,
+        out_specs=[VMEM_SPEC] * 3 + [SMEM_SPEC],
+        out_shape=[jax.ShapeDtypeStruct(*x) for x in (three, two, two, ((cols, tiles), jnp.int32))],
+        name="join_rows",
+    )(place, slice_here, *steps, *pieces)
 
 
 def exchange_rows(chain, sends):
-    return [lax.ppermute(s, BOTH, chain.shift(by)) for s, by in zip(sends, (1, 2, -1, -2))]
-
-
-def purify(own, near, kept, place, block, cols, last):
+    far = [lax.ppermute(s, BOTH, chain.shift(by)) for s, by in zip(sends[1::2], (2, -2))]
+    near = [lax.ppermute(s, BOTH, chain.shift(by)) for s, by in zip(sends[0::2], (1, -1))]
+    return near[0], far[0], near[1], far[1]
+
+
+def purify_math(kept_ref, left, right, square, store):
+    def product(left, d):
+        far, total = d - 2, None
+        for o in range(max(-2, far - 2), min(2, far + 2) + 1):
+            term = jnp.dot(left(o), right(o, far), preferred_element_type=F32)
+            total = term if total is None else total + term
+        return jnp.where(kept_ref[d] > 0, total, 0.0)
+
+    for d in range(5):
+        square[d] = product(left, d).astype(BF16)
+    for d in range(5):
+        value = 3.0 * square[d].astype(F32) - 2.0 * product(lambda o: square[o + 2], d)
+        store(d, value.astype(BF16))
+
+
+def purify_first(own, near, kept, block):
+    places = [(a, b) for a in range(-2, 3) for b in range(-2, 3) if abs(a - b) <= 2]
+    held = [(-2, -2), (-2, -1), (-1, -1), (-1, 0), (0, -2), (0, 0), (0, 1), (1, -1), (1, 1), (1, 2), (2, 0), (2, 2)]
+    flipped = [(a, b) for a, b in places if (a, b) not in held]
+
+    def body(kept_ref, own_ref, m1, m2, p1, p2, *refs):
+        outs, (square, turned) = refs[:-2], refs[-2:]
+        source = [(m2, 0), (m2, 1), (m1, 0), (m1, 1), (own_ref, 0), (own_ref, 1), (own_ref, 2)]
+        source += [(p1, 0), (p1, 1), (p1, 2), (p2, 0), (p2, 1)]
+        source = dict(zip(held, source))
+        for k, (a, b) in enumerate(flipped):
+            ref, at = source[b, a]
+            turned[k] = ref[at].T
+            source[a, b] = (turned, k)
+
+        def block_at(a, b):
+            ref, at = source[a, b]
+            return ref[at]
+
+        def store(d, value):
+            outs[0][d] = value
+            for out, (low, top) in zip(outs[1:], SENDS):
+                if low <= d < top:
+                    out[d - low] = value
+
+        purify_math(kept_ref, lambda o: block_at(0, o), block_at, square, store)
+
+    whole = ((5, block, block), BF16)
+    shapes = [whole] + [((top - low, block, block), BF16) for low, top in SENDS]
+    scratch = [whole, ((len(flipped), block, block), BF16)]
+    return small_call(body, "purify_first", [kept], [own] + list(near), shapes, scratch)
+
+
+def purify_next(own, near, kept, block, place, cols):
     high = block // cols
-
-    def body(kept_ref, place_ref, own_ref, m1, m2, p1, p2, *refs):
-        outs, square = refs[:-1], refs[-1]
+    last = place is not None
+
+    def body(kept_ref, *refs):
+        place_ref, refs = (refs[0], refs[1:]) if last else (None, refs)
+        own_ref, m1, m2, p1, p2 = refs[:5]
+        outs, square = refs[5:-1], refs[-1]
 
         def right(o, far):
             return (m2, m1, own_ref, p1, p2)[o + 2][far + (2, 2, 2, 1, 0)[o + 2]]
 
-        def product(left, d):
-            far, total = d - 2, None
-            for o in range(max(-2, far - 2), min(2, far + 2) + 1):
-                term = jnp.dot(left[o + 2], right(o, far), preferred_element_type=F32)
-                total = term if total is None else total + term
-            return jnp.where(kept_ref[d] > 0, total, 0.0)
-
-        for d in range(5):
-            square[d] = product(own_ref, d).astype(BF16)
-        for d in range(5):
-            value = 3.0 * square[d].astype(F32) - 2.0 * product(square, d)
-            value = value.astype(BF16)
+        def store(d, value):
             if last:
                 outs[-1][d] = value
-            else:
-                outs[0][d] = value
-                for out, (low, top) in zip(outs[1:], SENDS):
-                    if low <= d < top:
-                        out[d - low] = value
+                return
+            outs[0][d] = value
+            for out, (low, top) in zip(outs[1:], SENDS):
+                if low <= d < top:
+                    out[d - low] = value
+
+        purify_math(kept_ref, lambda o: own_ref[o + 2], right, square, store)
         if last:
             for turn in range(cols):
                 at = pl.ds(pl.multiple_of(mixed(place_ref[0], turn, cols) * high, high), high)
@@ -286,7 +341,7 @@
         shapes = [((5, high, block), BF16)] * cols + [whole]
     else:
         shapes = [whole] + [((top - low, block, block), BF16) for low, top in SENDS]
-    outs = small_call(body, "purify", [kept, place], [own] + list(near), shapes, [whole])
+    outs = small_call(body, "purify", [kept] + ([place] if last else []), [own] + list(near), shapes, [whole])
     return outs[:cols] if last else outs
 
 
@@ -515,9 +570,10 @@
     slice_here = col_index.astype(jnp.int32).reshape(1)
     kept = (pattern > 0)[:, :, None, None]
     masked = jnp.where(kept, density, jnp.zeros_like(density))
+    held = jnp.stack([masked[:, d] for d in HELD], axis=1)
     pieces = []
     for turn in range(cols):
-        piece = lax.dynamic_index_in_dim(masked, mixed(col_index, turn, cols), 0, keepdims=False)
+        piece = lax.dynamic_index_in_dim(held, mixed(col_index, turn, cols), 0, keepdims=False)
         pieces.append(lax.ppermute(piece, BOTH, chain.to_rows(turn)))
     other = lax.ppermute(pattern, "row", [(i, i ^ 1) for i in range(rows)])
     pattern_two = jnp.where(
@@ -525,12 +581,19 @@
     )
     kept_row = lax.dynamic_index_in_dim(pattern_two, step_here, 0, keepdims=False)
     steps_here = (windows - (2 * cols * row_index - 2)).astype(jnp.int32)
-    steps = lax.all_to_all(jnp.broadcast_to(steps_here, (cols, tiles)), "col", 0, 0, tiled=True)
-
-    own, *sends = join_rows(pieces, place, block)
+    rounds = [[(i, mixed(i, turn, cols)) for i in range(cols)] for turn in range(cols)]
+    steps = [
+        steps_here if all(a == b for a, b in pairs) else lax.ppermute(steps_here, "col", pairs) for pairs in rounds
+    ]
+    own, up, down, steps = join_rows(pieces, steps, place, slice_here, block)
+    sends = (up, up, own, down)
     for iteration in range(ITERS):
         near = exchange_rows(chain, sends)
-        out = purify(own, near, kept_row, place, block, cols, iteration == ITERS - 1)
+        last = place if iteration == ITERS - 1 else None
+        if iteration == 0:
+            out = purify_first(own, near, kept_row, block)
+        else:
+            out = purify_next(own, near, kept_row, block, last, cols)
         own, sends = out[0], out[1:]
     pieces = [lax.ppermute(p, BOTH, chain.to_slices(turn)) for turn, p in enumerate(out)]
     purified, down, up = join_slices(pieces, slice_here, block)

time: 187 us -> 187 us (level)
    all_to_all x1 -> x0, blocking collectives: 8.37 us -> none  [by_block_rows(): lax.all_to_all(jnp.broadcast_to(steps_here, (cols, tiles)), 'col', 0, 0,...]
    ppermute x0 -> x3, waiting for transfers between devices: none -> 8.05 us  [by_block_rows(): lax.ppermute(steps_here, 'col', pairs)]
    ppermute x4, waiting for transfers between devices: 7.49 us -> 0.01 us  [by_block_rows(): pieces.append(lax.ppermute(piece, BOTH, chain.to_rows(turn)))]
    ppermute x0 -> x3, starting transfers between devices: none -> 5.21 us  [by_block_rows(): lax.ppermute(steps_here, 'col', pairs)]
    all_to_all x1, blocking collectives: 12.7 us -> 17.1 us  [by_block_rows(): window = lax.all_to_all(sent[tile], 'col', 0, 0, tiled=True)]
    ppermute x8, waiting for transfers between devices: 19.5 us -> 16.6 us  [exchange_rows(): lax.ppermute(s, BOTH, chain.shift(by))]
    all_to_all x1, blocking collectives: 12.2 us -> 14.7 us  [by_block_rows(): terms.append(lax.all_to_all(term, 'col', 0, 0, tiled=True))]
    ppermute x4, waiting for transfers between devices: 3.68 us -> 5.84 us  [shifted_2(): return lax.ppermute(value, axis, pairs)]
  transfers between devices with their start and end apart: 23 -> 26, of which waited for: 11 -> 13; matrix products, arithmetic and copies ran while one was open for 1% -> 1% of each run, Pallas kernels for 15% -> 15%
where the time goes in v3:
time: 187 us; the launch traced here: 186 us
  starting transfers between devices  69.7 us (37%)
  waiting for transfers between devices  38.1 us (20%)
  Pallas kernels  37.8 us (20%)
  blocking collectives  31.8 us (17%)
  other arithmetic  3.87 us (2%)
  local copies, waits for them, and re-layouts  3.44 us (2%)
    pallas_call x2, Pallas kernels, tile_call(): pl.pallas_call(body, grid=(count + 1,), in_specs=[SMEM_SPEC, pl.BlockSpec...  27.5 us
    ppermute x8, starting transfers between devices, exchange_rows(): lax.ppermute(s, BOTH, chain.shift(by))  25.6 us
    ppermute x4, starting transfers between devices, shifted_2(): return lax.ppermute(value, axis, pairs)  18.2 us
    all_to_all x1, blocking collectives, by_block_rows(): window = lax.all_to_all(sent[tile], 'col', 0, 0, tiled=True)  17.1 us
    ppermute x8, waiting for transfers between devices, exchange_rows(): lax.ppermute(s, BOTH, chain.shift(by))  16.6 us
    all_to_all x1, blocking collectives, by_block_rows(): terms.append(lax.all_to_all(term, 'col', 0, 0, tiled=True))  14.7 us
    pallas_call x5, Pallas kernels, small_call(): pl.pallas_call(body, in_specs=[SMEM_SPEC] * len(scalars) + [VMEM_SPEC] *...  8.33 us
    ppermute x3, waiting for transfers between devices, by_block_rows(): lax.ppermute(steps_here, 'col', pairs)  8.05 us
  transfers between devices with their start and end apart: 26, of which 13 were waited for; matrix products, arithmetic and copies ran while one was open for 1% of the time, Pallas kernels for 15%

profile of v3, /device:TPU:3, one launch (start us, length us, event | category | flops | bytes accessed | tf_op | source)
XLA Modules:
  0.0 185.9 jit_solution(2146037838908658342)
XLA Ops:
  0.6 0.7 broadcast_compare_fusion
  1.3 1.2 broadcast_select_fusion
  2.7 3.8 %collective-permute-start.4 = (bf16[3,64,256]{2,1,0:T(8,128)(2,1)S(1)}, bf16[3,64,256]{2,1,0:T(8,128)(2,1)S(1)}, u32[]{:S(2)}, u32[]{:S(2)}) collective-permute-start(bf16[3,64,256]{2,1,0:T(8,128)(2,1)S(1)} %get-tuple-element.54), channel_id=1, source_target_pairs={{0,0},{1,4},{2,1},{3,5},{4,2},{5,6},{6,3},{7,7},{8,11},{9,15},{10,... | collective-permute-start | bytes 294920 | tf_op jit(solution)/shard_map/ppermute | solution.py:577
  6.5 2.5 %collective-permute-start.6 = (bf16[3,64,256]{2,1,0:T(8,128)(2,1)S(1)}, bf16[3,64,256]{2,1,0:T(8,128)(2,1)S(1)}, u32[]{:S(2)}, u32[]{:S(2)}) collective-permute-start(bf16[3,64,256]{2,1,0:T(8,128)(2,1)S(1)} %get-tuple-element.56), channel_id=1, source_target_pairs={{0,1},{1,5},{2,0},{3,4},{4,3},{5,7},{6,2},{7,6},{8,10},{9,14},{10,... | collective-permute-start | bytes 294920 | tf_op jit(solution)/shard_map/ppermute | solution.py:577
  9.7 2.7 %collective-permute-start.1 = (s32[2]{0:T(128)S(1)}, s32[2]{0:T(128)S(1)}, u32[]{:S(2)}, u32[]{:S(2)}) collective-permute-start(s32[2]{0:T(128)S(1)} %broadcast_subtract_fusion.refs_0_), channel_id=1, source_target_pairs={{0,1},{1,0},{2,3},{3,2},{4,5},{5,4},{6,7},{7,6},{8,9},{9,8},{10,11... | collective-permute-start | bytes 32 | tf_op jit(solution)/shard_map/ppermute | solution.py:586
  12.4 3.0 %collective-permute-done.1.refs_1_ = s32[2]{0:T(128)S(1)} collective-permute-done((s32[2]{0:T(128)S(1)}, s32[2]{0:T(128)S(1)}, u32[]{:S(2)}, u32[]{:S(2)}) %collective-permute-start.1) | collective-permute-done | bytes 40 | tf_op jit(solution)/shard_map/ppermute | solution.py:586
  15.4 1.1 collective-permute-start.2
  16.5 2.2 %collective-permute-done.2.refs_2_ = s32[2]{0:T(128)S(1)} collective-permute-done((s32[2]{0:T(128)S(1)}, s32[2]{0:T(128)S(1)}, u32[]{:S(2)}, u32[]{:S(2)}) %collective-permute-start.2) | collective-permute-done | bytes 40 | tf_op jit(solution)/shard_map/ppermute | solution.py:586
  18.8 1.4 collective-permute-start.3
  20.2 2.8 %collective-permute-done.3.refs_3_ = s32[2]{0:T(128)S(1)} collective-permute-done((s32[2]{0:T(128)S(1)}, s32[2]{0:T(128)S(1)}, u32[]{:S(2)}, u32[]{:S(2)}) %collective-permute-start.3) | collective-permute-done | bytes 40 | tf_op jit(solution)/shard_map/ppermute | solution.py:586
  23.8 2.0 %join_rows.1 = (bf16[3,256,256]{2,1,0:T(8,128)(2,1)}, bf16[2,256,256]{2,1,0:T(8,128)(2,1)}, bf16[2,256,256]{2,1,0:T(8,128)(2,1)}, s32[4,2]{1,0:T(4,128)}) custom-call(s32[1]{0:T(128)} %bitcast.2.place_ref.refs_0_, s32[1]{0:T(128)} %bitcast.slice_ref.place_ref, s32[2]{0:T(128)} %copy-done.9, s32[2]{0:T(128)} %copy-done.11, s32[2]{0:T(128)} %copy-done.12, ...), custom_call_target="tpu_custom_call" | custom-call | tf_op jit(solution)/shard_map/join_rows/pallas_call | solution.py:248
  25.8 5.0 %collective-permute-start.10 = (bf16[3,256,256]{2,1,0:T(8,128)(2,1)}, bf16[3,256,256]{2,1,0:T(8,128)(2,1)S(1)}, u32[]{:S(2)}, u32[]{:S(2)}) collective-permute-start(bf16[3,256,256]{2,1,0:T(8,128)(2,1)} %get-tuple-element.28.own_ref), channel_id=1, source_target_pairs={{4,0},{1,4},{5,1},{2,5},{6,2},{3,6},{7,3},{11,7},{15,11},{10,15},{... | collective-permute-start | bytes 1179656 | tf_op jit(solution)/shard_map/ppermute | solution.py:259
  30.8 1.9 %collective-permute-start.11 = (bf16[2,256,256]{2,1,0:T(8,128)(2,1)}, bf16[2,256,256]{2,1,0:T(8,128)(2,1)S(1)}, u32[]{:S(2)}, u32[]{:S(2)}) collective-permute-start(bf16[2,256,256]{2,1,0:T(8,128)(2,1)} %get-tuple-element.30), channel_id=1, source_target_pairs={{1,0},{5,4},{2,1},{6,5},{3,2},{7,6},{11,3},{15,7},{10,11},{14,15},... | collective-permute-start | bytes 786440 | tf_op jit(solution)/shard_map/ppermute | solution.py:258
  32.8 4.4 %collective-permute-start.8 = (bf16[2,256,256]{2,1,0:T(8,128)(2,1)}, bf16[2,256,256]{2,1,0:T(8,128)(2,1)S(1)}, u32[]{:S(2)}, u32[]{:S(2)}) collective-permute-start(bf16[2,256,256]{2,1,0:T(8,128)(2,1)} %get-tuple-element.29), channel_id=1, source_target_pairs={{0,4},{4,1},{1,5},{5,2},{2,6},{6,3},{3,7},{7,11},{11,15},{15,10},{... | collective-permute-start | bytes 786440 | tf_op jit(solution)/shard_map/ppermute | solution.py:259
  37.2 1.9 %collective-permute-start.9 = (bf16[2,256,256]{2,1,0:T(8,128)(2,1)}, bf16[2,256,256]{2,1,0:T(8,128)(2,1)S(1)}, u32[]{:S(2)}, u32[]{:S(2)}) collective-permute-start(bf16[2,256,256]{2,1,0:T(8,128)(2,1)} %get-tuple-element.29), channel_id=1, source_target_pairs={{0,1},{4,5},{1,2},{5,6},{2,3},{6,7},{3,11},{7,15},{11,10},{15,14},... | collective-permute-start | bytes 786440 | tf_op jit(solution)/shard_map/ppermute | solution.py:258
  39.8 0.8 collective-permute-done
  40.7 1.5 collective-permute-done.11.p2
  42.1 4.3 %collective-permute-done.9.m2 = bf16[2,256,256]{2,1,0:T(8,128)(2,1)S(1)} collective-permute-done((bf16[2,256,256]{2,1,0:T(8,128)(2,1)}, bf16[2,256,256]{2,1,0:T(8,128)(2,1)S(1)}, u32[]{:S(2)}, u32[]{:S(2)}) %collective-permute-start.9) | collective-permute-done | bytes 262176 | tf_op jit(solution)/shard_map/ppermute | solution.py:258
  46.5 1.0 copy-done.1
  47.4 2.1 %purify_first.1 = (bf16[5,256,256]{2,1,0:T(8,128)(2,1)S(1)}, bf16[4,256,256]{2,1,0:T(8,128)(2,1)S(1)}, bf16[3,256,256]{2,1,0:T(8,128)(2,1)S(1)}, bf16[4,256,256]...) custom-call(s32[5]{0:T(128)S(1)} %fusion.8.kept_ref, bf16[3,256,256]{2,1,0:T(8,128)(2,1)S(1)} %copy-done.1, ...), custom_call_target="tpu_custom_call" | custom-call | tf_op jit(solution)/shard_map/purify_first/pallas_call | solution.py:213
  49.5 5.1 %collective-permute-start.12 = (bf16[4,256,256]{2,1,0:T(8,128)(2,1)S(1)}, bf16[4,256,256]{2,1,0:T(8,128)(2,1)S(1)}, u32[]{:S(2)}, u32[]{:S(2)}) collective-permute-start(bf16[4,256,256]{2,1,0:T(8,128)(2,1)S(1)} %get-tuple-element.32), channel_id=1, source_target_pairs={{0,4},{4,1},{1,5},{5,2},{2,6},{6,3},{3,7},{7,11},{11,15},{15,10},{... | collective-permute-start | bytes 1572872 | tf_op jit(solution)/shard_map/ppermute | solution.py:259
  54.6 1.9 %collective-permute-start.14 = (bf16[4,256,256]{2,1,0:T(8,128)(2,1)S(1)}, bf16[4,256,256]{2,1,0:T(8,128)(2,1)S(1)}, u32[]{:S(2)}, u32[]{:S(2)}) collective-permute-start(bf16[4,256,256]{2,1,0:T(8,128)(2,1)S(1)} %get-tuple-element.34), channel_id=1, source_target_pairs={{4,0},{1,4},{5,1},{2,5},{6,2},{3,6},{7,3},{11,7},{15,11},{10,15},{... | collective-permute-start | bytes 1572872 | tf_op jit(solution)/shard_map/ppermute | solution.py:259
  56.5 2.1 %collective-permute-start.13 = (bf16[3,256,256]{2,1,0:T(8,128)(2,1)S(1)}, bf16[3,256,256]{2,1,0:T(8,128)(2,1)S(1)}, u32[]{:S(2)}, u32[]{:S(2)}) collective-permute-start(bf16[3,256,256]{2,1,0:T(8,128)(2,1)S(1)} %get-tuple-element.33), channel_id=1, source_target_pairs={{0,1},{4,5},{1,2},{5,6},{2,3},{6,7},{3,11},{7,15},{11,10},{15,14},... | collective-permute-start | bytes 1179656 | tf_op jit(solution)/shard_map/ppermute | solution.py:258
  58.7 3.2 %collective-permute-start.15 = (bf16[3,256,256]{2,1,0:T(8,128)(2,1)S(1)}, bf16[3,256,256]{2,1,0:T(8,128)(2,1)S(1)}, u32[]{:S(2)}, u32[]{:S(2)}) collective-permute-start(bf16[3,256,256]{2,1,0:T(8,128)(2,1)S(1)} %get-tuple-element.35), channel_id=1, source_target_pairs={{1,0},{5,4},{2,1},{6,5},{3,2},{7,6},{11,3},{15,7},{10,11},{14,15},... | collective-permute-start | bytes 1179656 | tf_op jit(solution)/shard_map/ppermute | solution.py:258
  61.8 7.0 %collective-permute-done.13.refs_3_ = bf16[3,256,256]{2,1,0:T(8,128)(2,1)S(1)} collective-permute-done((bf16[3,256,256]{2,1,0:T(8,128)(2,1)S(1)}, bf16[3,256,256]{2,1,0:T(8,128)(2,1)S(1)}, u32[]{:S(2)}, u32[]{:S(2)}) %collective-permute-start.13) | collective-permute-done | bytes 393248 | tf_op jit(solution)/shard_map/ppermute | solution.py:258
  68.9 3.7 %collective-permute-done.15.refs_5_ = bf16[3,256,256]{2,1,0:T(8,128)(2,1)S(1)} collective-permute-done((bf16[3,256,256]{2,1,0:T(8,128)(2,1)S(1)}, bf16[3,256,256]{2,1,0:T(8,128)(2,1)S(1)}, u32[]{:S(2)}, u32[]{:S(2)}) %collective-permute-start.15) | collective-permute-done | bytes 393248 | tf_op jit(solution)/shard_map/ppermute | solution.py:258
  72.6 2.9 %purify.1 = (bf16[5,64,256]{2,1,0:T(8,128)(2,1)S(1)}, bf16[5,64,256]{2,1,0:T(8,128)(2,1)S(1)}, bf16[5,64,256]{2,1,0:T(8,128)(2,1)S(1)}, bf16[5,64,256]{2,1,0:T(8,128)(2,1)S(1)}, bf16[5,256,256]{2,1,0:T(8,128)(2,1)}) custom-call(s32[5]{0:T(128)S(1)} %fusion.8.kept_ref, s32[1]{0:T(128)} %bitcast.2.place_ref.refs_0_, ...), custom_call_target="tpu_custom_call" | custom-call | tf_op jit(solution)/shard_map/purify/pallas_call | solution.py:213
  75.5 1.9 %collective-permute-start.16 = (bf16[5,64,256]{2,1,0:T(8,128)(2,1)S(1)}, bf16[5,64,256]{2,1,0:T(8,128)(2,1)S(1)}, u32[]{:S(2)}, u32[]{:S(2)}) collective-permute-start(bf16[5,64,256]{2,1,0:T(8,128)(2,1)S(1)} %get-tuple-element.36), channel_id=1, source_target_pairs={{0,0},{4,1},{1,2},{5,3},{2,4},{6,5},{3,6},{7,7},{11,8},{15,9},{10,... | collective-permute-start | bytes 491528 | tf_op jit(solution)/shard_map/ppermute | solution.py:598
  77.4 2.6 %collective-permute-start.17 = (bf16[5,64,256]{2,1,0:T(8,128)(2,1)S(1)}, bf16[5,64,256]{2,1,0:T(8,128)(2,1)S(1)}, u32[]{:S(2)}, u32[]{:S(2)}) collective-permute-start(bf16[5,64,256]{2,1,0:T(8,128)(2,1)S(1)} %get-tuple-element.37), channel_id=1, source_target_pairs={{4,0},{0,1},{5,2},{1,3},{6,4},{2,5},{7,6},{3,7},{15,8},{11,9},{14,... | collective-permute-start | bytes 491528 | tf_op jit(solution)/shard_map/ppermute | solution.py:598
  80.7 2.7 %collective-permute-done.16.refs_0_ = bf16[5,64,256]{2,1,0:T(8,128)(2,1)S(1)} collective-permute-done((bf16[5,64,256]{2,1,0:T(8,128)(2,1)S(1)}, bf16[5,64,256]{2,1,0:T(8,128)(2,1)S(1)}, u32[]{:S(2)}, u32[]{:S(2)}) %collective-permute-start.16) | collective-permute-done | bytes 163872 | tf_op jit(solution)/shard_map/ppermute | solution.py:598
  84.0 3.5 %collective-permute-done.18.refs_2_ = bf16[5,64,256]{2,1,0:T(8,128)(2,1)S(1)} collective-permute-done((bf16[5,64,256]{2,1,0:T(8,128)(2,1)S(1)}, bf16[5,64,256]{2,1,0:T(8,128)(2,1)S(1)}, u32[]{:S(2)}, u32[]{:S(2)}) %collective-permute-start.18) | collective-permute-done | bytes 163872 | tf_op jit(solution)/shard_map/ppermute | solution.py:598
  87.5 0.9 join_slices.1
  88.4 5.9 %collective-permute-start.20 = (bf16[2,64,256]{2,1,0:T(8,128)(2,1)S(1)}, bf16[2,64,256]{2,1,0:T(8,128)(2,1)S(1)}, u32[]{:S(2)}, u32[]{:S(2)}) collective-permute-start(bf16[2,64,256]{2,1,0:T(8,128)(2,1)S(1)} %get-tuple-element.42), channel_id=1, source_target_pairs={{0,4},{4,8},{8,12},{12,16},{16,20},{20,24},{24,28},{1,5},{5,9},{9,... | collective-permute-start | bytes 196616 | tf_op jit(solution)/shard_map/ppermute | solution.py:36
  94.4 4.8 %collective-permute-start.21 = (bf16[2,64,256]{2,1,0:T(8,128)(2,1)S(1)}, bf16[2,64,256]{2,1,0:T(8,128)(2,1)S(1)}, u32[]{:S(2)}, u32[]{:S(2)}) collective-permute-start(bf16[2,64,256]{2,1,0:T(8,128)(2,1)S(1)} %get-tuple-element.43), channel_id=1, source_target_pairs={{4,0},{8,4},{12,8},{16,12},{20,16},{24,20},{28,24},{5,1},{9,5},{13... | collective-permute-start | bytes 196616 | tf_op jit(solution)/shard_map/ppermute | solution.py:36
  99.2 1.9 %collective-permute-done.21.below_ref = bf16[2,64,256]{2,1,0:T(8,128)(2,1)S(1)} collective-permute-done((bf16[2,64,256]{2,1,0:T(8,128)(2,1)S(1)}, bf16[2,64,256]{2,1,0:T(8,128)(2,1)S(1)}, u32[]{:S(2)}, u32[]{:S(2)}) %collective-permute-start.21) | collective-permute-done | bytes 65568 | tf_op jit(solution)/shard_map/ppermute | solution.py:36
  101.1 1.1 copy-done
  102.2 1.5 pack_windows.1
  103.7 17.1 %all_to_all.20.pieces_ref = bf16[4,2,64,384]{3,2,1,0:T(8,128)(2,1)S(1)} all-to-all(bf16[4,2,64,384]{3,2,1,0:T(8,128)(2,1)S(1)} %get-tuple-element.46), channel_id=1, replica_groups=mesh['row'=8,'col'=4] {'col'}, dimensions={0} | all-to-all | bytes 786432 | tf_op jit(solution)/shard_map/all_to_all | solution.py:607
  120.8 3.6 %all-to-all-start = ((bf16[4,2,64,384]{3,2,1,0:T(8,128)(2,1)}), bf16[4,2,64,384]{3,2,1,0:T(8,128)(2,1)S(1)}, u32[]{:S(2)}, u32[]{:S(2)}) async-start(bf16[4,2,64,384]{3,2,1,0:T(8,128)(2,1)} %get-tuple-element.44), calls=%async_computation | async-start | bytes 786432 | tf_op jit(solution)/shard_map/all_to_all | solution.py:607
  125.1 14.1 %tile.3 = (f32[32,128]{1,0:T(8,128)S(1)}, bf16[4,2,64,384]{3,2,1,0:T(8,128)(2,1)}) custom-call(s32[1]{0:T(128)} %get-tuple-element.57.step_ref, bf16[2,4096,384]{2,1,0:T(8,128)(2,1)} %v_ref.3, bf16[3,2,4096,384]{3,2,1,0:T(8,128)(2,1)} %g_ref.3, f32[2,32,128]{2,1,0:T(8,128)S(1)} %bitcast.20, bf16[4,2,64,384]{3,2,1,0:T(8,128)(2,1)S(1)} %all_to_all.20.pieces_ref), custom_call_target="tpu_custom_call" | custom-call | tf_op jit(solution)/shard_map/tile/pallas_call | solution.py:496
  139.2 4.3 %all-to-all-start.3 = ((bf16[4,2,64,384]{3,2,1,0:T(8,128)(2,1)}), bf16[4,2,64,384]{3,2,1,0:T(8,128)(2,1)S(1)}, u32[]{:S(2)}, u32[]{:S(2)}) async-start(bf16[4,2,64,384]{3,2,1,0:T(8,128)(2,1)} %get-tuple-element.47), calls=%async_computation.3 | async-start | bytes 786432 | tf_op jit(solution)/shard_map/all_to_all | solution.py:612
  143.5 13.4 %tile.2 = (f32[32,128]{1,0:T(8,128)S(1)}, bf16[4,2,64,384]{3,2,1,0:T(8,128)(2,1)S(1)}) custom-call(s32[1]{0:T(128)} %get-tuple-element.58.step_ref, bf16[2,4096,384]{2,1,0:T(8,128)(2,1)} %v_ref.3, bf16[3,2,4096,384]{3,2,1,0:T(8,128)(2,1)} %g_ref.3, f32[2,32,128]{2,1,0:T(8,128)S(1)} %bitcast.21, bf16[4,2,64,384]{3,2,1,0:T(8,128)(2,1)S(1)} %all-to-all-done.pieces_ref), custom_call_target="tpu_custom_call" | custom-call | tf_op jit(solution)/shard_map/tile/pallas_call | solution.py:496
  156.9 14.7 %all_to_all.21.refs_0_ = bf16[4,2,64,384]{3,2,1,0:T(8,128)(2,1)S(1)} all-to-all(bf16[4,2,64,384]{3,2,1,0:T(8,128)(2,1)S(1)} %get-tuple-element.45), channel_id=1, replica_groups=mesh['row'=8,'col'=4] {'col'}, dimensions={0} | all-to-all | bytes 786432 | tf_op jit(solution)/shard_map/all_to_all | solution.py:612
  171.6 1.0 add_terms.1
  172.6 5.5 %collective-permute-start.22 = (bf16[2,64,256]{2,1,0:T(8,128)(2,1)S(1)}, bf16[2,64,256]{2,1,0:T(8,128)(2,1)S(1)}, u32[]{:S(2)}, u32[]{:S(2)}) collective-permute-start(bf16[2,64,256]{2,1,0:T(8,128)(2,1)S(1)} %get-tuple-element.49), channel_id=1, source_target_pairs={{0,4},{4,8},{8,12},{12,16},{16,20},{20,24},{24,28},{1,5},{5,9},{9,... | collective-permute-start | bytes 196616 | tf_op jit(solution)/shard_map/ppermute | solution.py:36
  178.1 1.9 %collective-permute-start.23 = (bf16[2,64,256]{2,1,0:T(8,128)(2,1)S(1)}, bf16[2,64,256]{2,1,0:T(8,128)(2,1)S(1)}, u32[]{:S(2)}, u32[]{:S(2)}) collective-permute-start(bf16[2,64,256]{2,1,0:T(8,128)(2,1)S(1)} %get-tuple-element.50), channel_id=1, source_target_pairs={{4,0},{8,4},{12,8},{16,12},{20,16},{24,20},{28,24},{5,1},{9,5},{13... | collective-permute-start | bytes 196616 | tf_op jit(solution)/shard_map/ppermute | solution.py:36
  180.7 3.9 %collective-permute-done.23 = bf16[2,64,256]{2,1,0:T(8,128)(2,1)S(1)} collective-permute-done((bf16[2,64,256]{2,1,0:T(8,128)(2,1)S(1)}, bf16[2,64,256]{2,1,0:T(8,128)(2,1)S(1)}, u32[]{:S(2)}, u32[]{:S(2)}) %collective-permute-start.23) | collective-permute-done | bytes 65568 | tf_op jit(solution)/shard_map/ppermute | solution.py:36
  184.7 1.2 pad_select_fusion
  (57 shorter events, 4.9 us)
Async XLA Ops:
  1.3 8.3 %copy-start.14 = (s32[2]{0:T(128)S(1)}, s32[2]{0:T(128)}, u32[]{:S(2)}) copy-start(s32[2]{0:T(128)} %param.8) | copy-start | bytes 28
  2.6 36.6 %copy-start.8 = (s32[4,5]{1,0:T(4,128)S(1)}, s32[4,5]{1,0:T(4,128)}, u32[]{:S(2)}) copy-start(s32[4,5]{1,0:T(4,128)} %param.7) | copy-start | bytes 244
  2.7 20.3 %collective-permute-start.4 = (bf16[3,64,256]{2,1,0:T(8,128)(2,1)S(1)}, bf16[3,64,256]{2,1,0:T(8,128)(2,1)S(1)}, u32[]{:S(2)}, u32[]{:S(2)}) collective-permute-start(bf16[3,64,256]{2,1,0:T(8,128)(2,1)S(1)} %get-tuple-element.54), channel_id=1, source_target_pairs={{0,0},{1,4},{2,1},{3,5},{4,2},{5,6},{6,3},{7,7},{8,11},{9,15},{10,... | collective-permute-start | bytes 294920 | tf_op jit(solution)/shard_map/ppermute | solution.py:577
  6.5 16.5 %collective-permute-start.5 = (bf16[3,64,256]{2,1,0:T(8,128)(2,1)S(1)}, bf16[3,64,256]{2,1,0:T(8,128)(2,1)S(1)}, u32[]{:S(2)}, u32[]{:S(2)}) collective-permute-start(bf16[3,64,256]{2,1,0:T(8,128)(2,1)S(1)} %get-tuple-element.55), channel_id=1, source_target_pairs={{0,4},{1,0},{2,5},{3,1},{4,6},{5,2},{6,7},{7,3},{8,15},{9,11},{10,... | collective-permute-start | bytes 294920 | tf_op jit(solution)/shard_map/ppermute | solution.py:577
  6.5 16.5 %collective-permute-start.6 = (bf16[3,64,256]{2,1,0:T(8,128)(2,1)S(1)}, bf16[3,64,256]{2,1,0:T(8,128)(2,1)S(1)}, u32[]{:S(2)}, u32[]{:S(2)}) collective-permute-start(bf16[3,64,256]{2,1,0:T(8,128)(2,1)S(1)} %get-tuple-element.56), channel_id=1, source_target_pairs={{0,1},{1,5},{2,0},{3,4},{4,3},{5,7},{6,2},{7,6},{8,10},{9,14},{10,... | collective-permute-start | bytes 294920 | tf_op jit(solution)/shard_map/ppermute | solution.py:577
  9.0 14.0 %collective-permute-start.7 = (bf16[3,64,256]{2,1,0:T(8,128)(2,1)S(1)}, bf16[3,64,256]{2,1,0:T(8,128)(2,1)S(1)}, u32[]{:S(2)}, u32[]{:S(2)}) collective-permute-start(bf16[3,64,256]{2,1,0:T(8,128)(2,1)S(1)} %get-tuple-element.53), channel_id=1, source_target_pairs={{0,5},{1,1},{2,4},{3,0},{4,7},{5,3},{6,6},{7,2},{8,14},{9,10},{10,... | collective-permute-start | bytes 294920 | tf_op jit(solution)/shard_map/ppermute | solution.py:577
  9.7 13.3 %copy-start.9 = (s32[2]{0:T(128)}, s32[2]{0:T(128)S(1)}, u32[]{:S(2)}) copy-start(s32[2]{0:T(128)S(1)} %broadcast_subtract_fusion.refs_0_) | copy-start | bytes 28
  9.7 5.7 %collective-permute-start.1 = (s32[2]{0:T(128)S(1)}, s32[2]{0:T(128)S(1)}, u32[]{:S(2)}, u32[]{:S(2)}) collective-permute-start(s32[2]{0:T(128)S(1)} %broadcast_subtract_fusion.refs_0_), channel_id=1, source_target_pairs={{0,1},{1,0},{2,3},{3,2},{4,5},{5,4},{6,7},{7,6},{8,9},{9,8},{10,11... | collective-permute-start | bytes 32 | tf_op jit(solution)/shard_map/ppermute | solution.py:586
  15.4 7.6 %copy-start.11 = (s32[2]{0:T(128)}, s32[2]{0:T(128)S(1)}, u32[]{:S(2)}) copy-start(s32[2]{0:T(128)S(1)} %collective-permute-done.1.refs_1_) | copy-start | bytes 28
  15.4 3.3 %collective-permute-start.2 = (s32[2]{0:T(128)S(1)}, s32[2]{0:T(128)S(1)}, u32[]{:S(2)}, u32[]{:S(2)}) collective-permute-start(s32[2]{0:T(128)S(1)} %broadcast_subtract_fusion.refs_0_), channel_id=1, source_target_pairs={{0,2},{1,3},{2,0},{3,1},{4,6},{5,7},{6,4},{7,5},{8,10},{9,11},{10,... | collective-permute-start | bytes 32 | tf_op jit(solution)/shard_map/ppermute | solution.py:586
  18.8 4.3 %copy-start.12 = (s32[2]{0:T(128)}, s32[2]{0:T(128)S(1)}, u32[]{:S(2)}) copy-start(s32[2]{0:T(128)S(1)} %collective-permute-done.2.refs_2_) | copy-start | bytes 28
  18.8 4.2 %collective-permute-start.3 = (s32[2]{0:T(128)S(1)}, s32[2]{0:T(128)S(1)}, u32[]{:S(2)}, u32[]{:S(2)}) collective-permute-start(s32[2]{0:T(128)S(1)} %broadcast_subtract_fusion.refs_0_), channel_id=1, source_target_pairs={{0,3},{1,2},{2,1},{3,0},{4,7},{5,6},{6,5},{7,4},{8,11},{9,10},{10,... | collective-permute-start | bytes 32 | tf_op jit(solution)/shard_map/ppermute | solution.py:586
  23.0 0.5 copy-start.13
  23.0 0.6 copy-start.3
  23.0 0.7 copy-start.4
  23.0 0.7 copy-start.5
  23.0 0.7 copy-start.6
  25.8 20.7 %collective-permute-start.10 = (bf16[3,256,256]{2,1,0:T(8,128)(2,1)}, bf16[3,256,256]{2,1,0:T(8,128)(2,1)S(1)}, u32[]{:S(2)}, u32[]{:S(2)}) collective-permute-start(bf16[3,256,256]{2,1,0:T(8,128)(2,1)} %get-tuple-element.28.own_ref), channel_id=1, source_target_pairs={{4,0},{1,4},{5,1},{2,5},{6,2},{3,6},{7,3},{11,7},{15,11},{10,15},{... | collective-permute-start | bytes 1179656 | tf_op jit(solution)/shard_map/ppermute | solution.py:259
  30.8 11.3 %collective-permute-start.11 = (bf16[2,256,256]{2,1,0:T(8,128)(2,1)}, bf16[2,256,256]{2,1,0:T(8,128)(2,1)S(1)}, u32[]{:S(2)}, u32[]{:S(2)}) collective-permute-start(bf16[2,256,256]{2,1,0:T(8,128)(2,1)} %get-tuple-element.30), channel_id=1, source_target_pairs={{1,0},{5,4},{2,1},{6,5},{3,2},{7,6},{11,3},{15,7},{10,11},{14,15},... | collective-permute-start | bytes 786440 | tf_op jit(solution)/shard_map/ppermute | solution.py:258
  32.8 9.4 %collective-permute-start.8 = (bf16[2,256,256]{2,1,0:T(8,128)(2,1)}, bf16[2,256,256]{2,1,0:T(8,128)(2,1)S(1)}, u32[]{:S(2)}, u32[]{:S(2)}) collective-permute-start(bf16[2,256,256]{2,1,0:T(8,128)(2,1)} %get-tuple-element.29), channel_id=1, source_target_pairs={{0,4},{4,1},{1,5},{5,2},{2,6},{6,3},{3,7},{7,11},{11,15},{15,10},{... | collective-permute-start | bytes 786440 | tf_op jit(solution)/shard_map/ppermute | solution.py:259
  37.2 9.2 %collective-permute-start.9 = (bf16[2,256,256]{2,1,0:T(8,128)(2,1)}, bf16[2,256,256]{2,1,0:T(8,128)(2,1)S(1)}, u32[]{:S(2)}, u32[]{:S(2)}) collective-permute-start(bf16[2,256,256]{2,1,0:T(8,128)(2,1)} %get-tuple-element.29), channel_id=1, source_target_pairs={{0,1},{4,5},{1,2},{5,6},{2,3},{6,7},{3,11},{7,15},{11,10},{15,14},... | collective-permute-start | bytes 786440 | tf_op jit(solution)/shard_map/ppermute | solution.py:258
  39.2 1.5 collective-permute-start
  46.5 1.0 copy-start.1
  49.5 23.1 %collective-permute-start.12 = (bf16[4,256,256]{2,1,0:T(8,128)(2,1)S(1)}, bf16[4,256,256]{2,1,0:T(8,128)(2,1)S(1)}, u32[]{:S(2)}, u32[]{:S(2)}) collective-permute-start(bf16[4,256,256]{2,1,0:T(8,128)(2,1)S(1)} %get-tuple-element.32), channel_id=1, source_target_pairs={{0,4},{4,1},{1,5},{5,2},{2,6},{6,3},{3,7},{7,11},{11,15},{15,10},{... | collective-permute-start | bytes 1572872 | tf_op jit(solution)/shard_map/ppermute | solution.py:259
  54.6 18.0 %collective-permute-start.14 = (bf16[4,256,256]{2,1,0:T(8,128)(2,1)S(1)}, bf16[4,256,256]{2,1,0:T(8,128)(2,1)S(1)}, u32[]{:S(2)}, u32[]{:S(2)}) collective-permute-start(bf16[4,256,256]{2,1,0:T(8,128)(2,1)S(1)} %get-tuple-element.34), channel_id=1, source_target_pairs={{4,0},{1,4},{5,1},{2,5},{6,2},{3,6},{7,3},{11,7},{15,11},{10,15},{... | collective-permute-start | bytes 1572872 | tf_op jit(solution)/shard_map/ppermute | solution.py:259
  56.5 12.3 %collective-permute-start.13 = (bf16[3,256,256]{2,1,0:T(8,128)(2,1)S(1)}, bf16[3,256,256]{2,1,0:T(8,128)(2,1)S(1)}, u32[]{:S(2)}, u32[]{:S(2)}) collective-permute-start(bf16[3,256,256]{2,1,0:T(8,128)(2,1)S(1)} %get-tuple-element.33), channel_id=1, source_target_pairs={{0,1},{4,5},{1,2},{5,6},{2,3},{6,7},{3,11},{7,15},{11,10},{15,14},... | collective-permute-start | bytes 1179656 | tf_op jit(solution)/shard_map/ppermute | solution.py:258
  58.7 13.9 %collective-permute-start.15 = (bf16[3,256,256]{2,1,0:T(8,128)(2,1)S(1)}, bf16[3,256,256]{2,1,0:T(8,128)(2,1)S(1)}, u32[]{:S(2)}, u32[]{:S(2)}) collective-permute-start(bf16[3,256,256]{2,1,0:T(8,128)(2,1)S(1)} %get-tuple-element.35), channel_id=1, source_target_pairs={{1,0},{5,4},{2,1},{6,5},{3,2},{7,6},{11,3},{15,7},{10,11},{14,15},... | collective-permute-start | bytes 1179656 | tf_op jit(solution)/shard_map/ppermute | solution.py:258
  72.6 28.5 %copy-start.2 = (s32[4,2]{1,0:T(4,128)S(1)}, s32[4,2]{1,0:T(4,128)}, u32[]{:S(2)}) copy-start(s32[4,2]{1,0:T(4,128)} %get-tuple-element.41.steps_ref) | copy-start | bytes 100
  75.5 7.9 %collective-permute-start.16 = (bf16[5,64,256]{2,1,0:T(8,128)(2,1)S(1)}, bf16[5,64,256]{2,1,0:T(8,128)(2,1)S(1)}, u32[]{:S(2)}, u32[]{:S(2)}) collective-permute-start(bf16[5,64,256]{2,1,0:T(8,128)(2,1)S(1)} %get-tuple-element.36), channel_id=1, source_target_pairs={{0,0},{4,1},{1,2},{5,3},{2,4},{6,5},{3,6},{7,7},{11,8},{15,9},{10,... | collective-permute-start | bytes 491528 | tf_op jit(solution)/shard_map/ppermute | solution.py:598
  77.4 6.6 %collective-permute-start.17 = (bf16[5,64,256]{2,1,0:T(8,128)(2,1)S(1)}, bf16[5,64,256]{2,1,0:T(8,128)(2,1)S(1)}, u32[]{:S(2)}, u32[]{:S(2)}) collective-permute-start(bf16[5,64,256]{2,1,0:T(8,128)(2,1)S(1)} %get-tuple-element.37), channel_id=1, source_target_pairs={{4,0},{0,1},{5,2},{1,3},{6,4},{2,5},{7,6},{3,7},{15,8},{11,9},{14,... | collective-permute-start | bytes 491528 | tf_op jit(solution)/shard_map/ppermute | solution.py:598
  80.0 7.5 %collective-permute-start.18 = (bf16[5,64,256]{2,1,0:T(8,128)(2,1)S(1)}, bf16[5,64,256]{2,1,0:T(8,128)(2,1)S(1)}, u32[]{:S(2)}, u32[]{:S(2)}) collective-permute-start(bf16[5,64,256]{2,1,0:T(8,128)(2,1)S(1)} %get-tuple-element.38), channel_id=1, source_target_pairs={{1,0},{5,1},{0,2},{4,3},{3,4},{7,5},{2,6},{6,7},{10,8},{14,9},{11,... | collective-permute-start | bytes 491528 | tf_op jit(solution)/shard_map/ppermute | solution.py:598
  80.0 7.5 %collective-permute-start.19 = (bf16[5,64,256]{2,1,0:T(8,128)(2,1)S(1)}, bf16[5,64,256]{2,1,0:T(8,128)(2,1)S(1)}, u32[]{:S(2)}, u32[]{:S(2)}) collective-permute-start(bf16[5,64,256]{2,1,0:T(8,128)(2,1)S(1)} %get-tuple-element.39), channel_id=1, source_target_pairs={{5,0},{1,1},{4,2},{0,3},{7,4},{3,5},{6,6},{2,7},{14,8},{10,9},{15,... | collective-permute-start | bytes 491528 | tf_op jit(solution)/shard_map/ppermute | solution.py:598
  87.5 36.9 %copy-start.7 = (f32[2,4096]{1,0:T(2,128)S(1)}, f32[2,4096]{1,0:T(2,128)}, u32[]{:S(2)}) copy-start(f32[2,4096]{1,0:T(2,128)} %param.11) | copy-start | bytes 98308
  88.4 36.1 %copy-start.10 = (s32[2]{0:T(128)S(1)}, s32[2]{0:T(128)}, u32[]{:S(2)}) copy-start(s32[2]{0:T(128)} %copy-done.9) | copy-start | bytes 28
  88.4 10.8 %collective-permute-start.20 = (bf16[2,64,256]{2,1,0:T(8,128)(2,1)S(1)}, bf16[2,64,256]{2,1,0:T(8,128)(2,1)S(1)}, u32[]{:S(2)}, u32[]{:S(2)}) collective-permute-start(bf16[2,64,256]{2,1,0:T(8,128)(2,1)S(1)} %get-tuple-element.42), channel_id=1, source_target_pairs={{0,4},{4,8},{8,12},{12,16},{16,20},{20,24},{24,28},{1,5},{5,9},{9,... | collective-permute-start | bytes 196616 | tf_op jit(solution)/shard_map/ppermute | solution.py:36
  94.4 6.8 %collective-permute-start.21 = (bf16[2,64,256]{2,1,0:T(8,128)(2,1)S(1)}, bf16[2,64,256]{2,1,0:T(8,128)(2,1)S(1)}, u32[]{:S(2)}, u32[]{:S(2)}) collective-permute-start(bf16[2,64,256]{2,1,0:T(8,128)(2,1)S(1)} %get-tuple-element.43), channel_id=1, source_target_pairs={{4,0},{8,4},{12,8},{16,12},{20,16},{24,20},{28,24},{5,1},{9,5},{13... | collective-permute-start | bytes 196616 | tf_op jit(solution)/shard_map/ppermute | solution.py:36
  101.1 1.1 copy-start
  120.8 18.4 %all-to-all-start = ((bf16[4,2,64,384]{3,2,1,0:T(8,128)(2,1)}), bf16[4,2,64,384]{3,2,1,0:T(8,128)(2,1)S(1)}, u32[]{:S(2)}, u32[]{:S(2)}) async-start(bf16[4,2,64,384]{3,2,1,0:T(8,128)(2,1)} %get-tuple-element.44), calls=%async_computation | async-start | bytes 786432 | tf_op jit(solution)/shard_map/all_to_all | solution.py:607
  139.2 17.7 %all-to-all-start.3 = ((bf16[4,2,64,384]{3,2,1,0:T(8,128)(2,1)}), bf16[4,2,64,384]{3,2,1,0:T(8,128)(2,1)S(1)}, u32[]{:S(2)}, u32[]{:S(2)}) async-start(bf16[4,2,64,384]{3,2,1,0:T(8,128)(2,1)} %get-tuple-element.47), calls=%async_computation.3 | async-start | bytes 786432 | tf_op jit(solution)/shard_map/all_to_all | solution.py:612
  172.6 8.1 %collective-permute-start.22 = (bf16[2,64,256]{2,1,0:T(8,128)(2,1)S(1)}, bf16[2,64,256]{2,1,0:T(8,128)(2,1)S(1)}, u32[]{:S(2)}, u32[]{:S(2)}) collective-permute-start(bf16[2,64,256]{2,1,0:T(8,128)(2,1)S(1)} %get-tuple-element.49), channel_id=1, source_target_pairs={{0,4},{4,8},{8,12},{12,16},{16,20},{20,24},{24,28},{1,5},{5,9},{9,... | collective-permute-start | bytes 196616 | tf_op jit(solution)/shard_map/ppermute | solution.py:36
  178.1 6.5 %collective-permute-start.23 = (bf16[2,64,256]{2,1,0:T(8,128)(2,1)S(1)}, bf16[2,64,256]{2,1,0:T(8,128)(2,1)S(1)}, u32[]{:S(2)}, u32[]{:S(2)}) collective-permute-start(bf16[2,64,256]{2,1,0:T(8,128)(2,1)S(1)} %get-tuple-element.50), channel_id=1, source_target_pairs={{4,0},{8,4},{12,8},{16,12},{20,16},{24,20},{28,24},{5,1},{9,5},{13... | collective-permute-start | bytes 196616 | tf_op jit(solution)/shard_map/ppermute | solution.py:36

commit v4 on v3

--- a/solution.py
+++ b/solution.py
@@ -223,35 +223,61 @@
 
 HELD = (0, 2, 3)
 SENDS = ((1, 5), (2, 5), (0, 4), (0, 3))
-
-
-def join_rows(pieces, steps, place, slice_here, block):
-    cols, tiles = len(pieces), steps[0].shape[0]
+NOTE = 16
+
+
+def grid_of(shape, axis):
+    return lax.broadcasted_iota(jnp.int32, shape, axis)
+
+
+def prepare(density, pattern, steps, slice_here):
+    cols, _, high, block = density.shape
+    tiles = steps.shape[0]
+
+    def body(pattern_ref, steps_ref, slice_ref, density_ref, *outs):
+        row, lane = grid_of((NOTE, block), 0), grid_of((NOTE, block), 1)
+        for turn in range(cols):
+            j = mixed(slice_ref[0], turn, cols)
+            for k, d in enumerate(HELD):
+                value = density_ref[j, d]
+                outs[turn][k * high : (k + 1) * high] = jnp.where(pattern_ref[j, d] > 0, value, jnp.zeros_like(value))
+            note = jnp.zeros((NOTE, block), F32)
+            for d in range(5):
+                note = jnp.where((row == 0) & (lane == d), (pattern_ref[j, d] > 0).astype(F32), note)
+            for tile in range(tiles):
+                note = jnp.where((row == 1) & (lane == tile), steps_ref[tile].astype(F32), note)
+            outs[turn][3 * high :] = note.astype(BF16)
+
+    shapes = [((3 * high + NOTE, block), BF16)] * cols
+    return small_call(body, "prepare", [pattern, steps, slice_here], [density], shapes)
+
+
+def join_rows(pieces, place, block):
+    cols = len(pieces)
     high = block // cols
 
-    def body(place_ref, slice_ref, *refs):
-        step_ins, ins = refs[:cols], refs[cols : 2 * cols]
-        own, up, down, steps_out = refs[2 * cols :]
+    def body(place_ref, *refs):
+        ins, (own, up, down, kept, steps) = refs[:cols], refs[cols:]
+        row = grid_of((NOTE, block), 0)
+        total = jnp.zeros((NOTE, block), F32)
         for turn in range(cols):
-            for tile in range(tiles):
-                steps_out[mixed(slice_ref[0], turn, cols), tile] = step_ins[turn][tile]
-            at = pl.ds(pl.multiple_of(mixed(place_ref[0], turn, cols) * high, high), high)
+            source = mixed(place_ref[0], turn, cols)
+            at = pl.ds(pl.multiple_of(source * high, high), high)
             for k in range(3):
-                value = ins[turn][k]
+                value = ins[turn][k * high : (k + 1) * high]
                 own[k, at] = value
                 if k > 0:
                     up[k - 1, at] = value
                 if k < 2:
                     down[k, at] = value
+            note = ins[turn][3 * high :].astype(F32)
+            total = jnp.where(row == source, note[1:2], total)
+        kept[...] = note
+        steps[...] = total.astype(BF16)
 
     two, three = ((2, block, block), BF16), ((3, block, block), BF16)
-    return pl.pallas_call(
-        body,
-        in_specs=[SMEM_SPEC] * (2 + cols) + [VMEM_SPEC] * cols,
-        out_specs=[VMEM_SPEC] * 3 + [SMEM_SPEC],
-        out_shape=[jax.ShapeDtypeStruct(*x) for x in (three, two, two, ((cols, tiles), jnp.int32))],
-        name="join_rows",
-    )(place, slice_here, *steps, *pieces)
+    shapes = [three, two, two, ((NOTE, block), F32), ((NOTE, block), BF16)]
+    return small_call(body, "join_rows", [place], pieces, shapes)
 
 
 def exchange_rows(chain, sends):
@@ -266,7 +292,7 @@
         for o in range(max(-2, far - 2), min(2, far + 2) + 1):
             term = jnp.dot(left(o), right(o, far), preferred_element_type=F32)
             total = term if total is None else total + term
-        return jnp.where(kept_ref[d] > 0, total, 0.0)
+        return jnp.where(kept_ref[0:1, d : d + 1] > 0.0, total, 0.0)
 
     for d in range(5):
         square[d] = product(left, d).astype(BF16)
@@ -305,24 +331,24 @@
     whole = ((5, block, block), BF16)
     shapes = [whole] + [((top - low, block, block), BF16) for low, top in SENDS]
     scratch = [whole, ((len(flipped), block, block), BF16)]
-    return small_call(body, "purify_first", [kept], [own] + list(near), shapes, scratch)
-
-
-def purify_next(own, near, kept, block, place, cols):
+    return small_call(body, "purify_first", [], [kept, own] + list(near), shapes, scratch)
+
+
+def purify_next(own, near, kept, block, place, steps, cols):
     high = block // cols
     last = place is not None
 
-    def body(kept_ref, *refs):
+    def body(*refs):
         place_ref, refs = (refs[0], refs[1:]) if last else (None, refs)
-        own_ref, m1, m2, p1, p2 = refs[:5]
-        outs, square = refs[5:-1], refs[-1]
+        kept_ref, own_ref, m1, m2, p1, p2, steps_ref = refs[:7]
+        outs, (square, whole_ref) = refs[7:-2], refs[-2:]
 
         def right(o, far):
             return (m2, m1, own_ref, p1, p2)[o + 2][far + (2, 2, 2, 1, 0)[o + 2]]
 
         def store(d, value):
             if last:
-                outs[-1][d] = value
+                whole_ref[d] = value
                 return
             outs[0][d] = value
             for out, (low, top) in zip(outs[1:], SENDS):
@@ -334,30 +360,49 @@
             for turn in range(cols):
                 at = pl.ds(pl.multiple_of(mixed(place_ref[0], turn, cols) * high, high), high)
                 for d in range(5):
-                    outs[turn][d] = outs[-1][d, at]
+                    outs[turn][d * high : (d + 1) * high] = whole_ref[d, at]
+                outs[turn][5 * high :] = steps_ref[...]
 
     whole = ((5, block, block), BF16)
     if last:
-        shapes = [((5, high, block), BF16)] * cols + [whole]
+        shapes = [((5 * high + NOTE, block), BF16)] * cols
     else:
         shapes = [whole] + [((top - low, block, block), BF16) for low, top in SENDS]
-    outs = small_call(body, "purify", [kept] + ([place] if last else []), [own] + list(near), shapes, [whole])
-    return outs[:cols] if last else outs
-
-
-def join_slices(pieces, place, block):
+    return small_call(
+        body, "purify", [place] if last else [], [kept, own] + list(near) + [steps], shapes, [whole, whole]
+    )
+
+
+def join_slices(pieces, place, tiles, block):
     cols = len(pieces)
     high = block // cols
 
     def body(place_ref, *refs):
-        ins, (out, down, up) = refs[:cols], refs[cols:]
+        ins, (out, down, up, steps) = refs[:cols], refs[cols:]
         for turn in range(cols):
-            out[mixed(place_ref[0], turn, cols)] = ins[turn][...]
+            j = mixed(place_ref[0], turn, cols)
+            for d in range(5):
+                out[j, d] = ins[turn][d * high : (d + 1) * high]
         down[...] = out[cols - 1, 2:4]
         up[...] = out[0, 1:3]
-
-    edge = ((2, high, block), BF16)
-    return small_call(body, "join_slices", [place], pieces, [((cols, 5, high, block), BF16), edge, edge])
+        note = ins[0][5 * high :].astype(F32)
+        row, lane = grid_of((NOTE, block), 0), grid_of((NOTE, block), 1)
+        for source in range(cols):
+            for tile in range(tiles):
+                here = jnp.where((row == source) & (lane == tile), note, 0.0)
+                steps[source, tile] = jnp.sum(here).astype(jnp.int32)
+
+    edge = jax.ShapeDtypeStruct((2, high, block), BF16)
+    return pl.pallas_call(
+        body,
+        in_specs=[SMEM_SPEC] + [VMEM_SPEC] * cols,
+        out_specs=[VMEM_SPEC] * 3 + [SMEM_SPEC],
+        out_shape=[
+            jax.ShapeDtypeStruct((cols, 5, high, block), BF16), edge, edge,
+            jax.ShapeDtypeStruct((cols, tiles), jnp.int32),
+        ],
+        name="join_slices",
+    )(place, *pieces)
 
 
 def slot_of(step, half):
@@ -569,23 +614,10 @@
     place = (step_here % cols).astype(jnp.int32).reshape(1)
     slice_here = col_index.astype(jnp.int32).reshape(1)
     kept = (pattern > 0)[:, :, None, None]
-    masked = jnp.where(kept, density, jnp.zeros_like(density))
-    held = jnp.stack([masked[:, d] for d in HELD], axis=1)
-    pieces = []
-    for turn in range(cols):
-        piece = lax.dynamic_index_in_dim(held, mixed(col_index, turn, cols), 0, keepdims=False)
-        pieces.append(lax.ppermute(piece, BOTH, chain.to_rows(turn)))
-    other = lax.ppermute(pattern, "row", [(i, i ^ 1) for i in range(rows)])
-    pattern_two = jnp.where(
-        row_index % 2 == 0, jnp.concatenate([pattern, other]), jnp.concatenate([other, pattern])
-    )
-    kept_row = lax.dynamic_index_in_dim(pattern_two, step_here, 0, keepdims=False)
     steps_here = (windows - (2 * cols * row_index - 2)).astype(jnp.int32)
-    rounds = [[(i, mixed(i, turn, cols)) for i in range(cols)] for turn in range(cols)]
-    steps = [
-        steps_here if all(a == b for a, b in pairs) else lax.ppermute(steps_here, "col", pairs) for pairs in rounds
-    ]
-    own, up, down, steps = join_rows(pieces, steps, place, slice_here, block)
+    pieces = prepare(density, pattern, steps_here, slice_here)
+    pieces = [lax.ppermute(p, BOTH, chain.to_rows(turn)) for turn, p in enumerate(pieces)]
+    own, up, down, kept_row, steps = join_rows(pieces, place, block)
     sends = (up, up, own, down)
     for iteration in range(ITERS):
         near = exchange_rows(chain, sends)
@@ -593,10 +625,10 @@
         if iteration == 0:
             out = purify_first(own, near, kept_row, block)
         else:
-            out = purify_next(own, near, kept_row, block, last, cols)
+            out = purify_next(own, near, kept_row, block, last, steps, cols)
         own, sends = out[0], out[1:]
     pieces = [lax.ppermute(p, BOTH, chain.to_slices(turn)) for turn, p in enumerate(out)]
-    purified, down, up = join_slices(pieces, slice_here, block)
+    purified, down, up, steps = join_slices(pieces, slice_here, tiles, block)
     above = shifted_2(down, "row", 1)
     below = shifted_2(up, "row", -1)
     sent = pack_windows(purified, above, below, steps, slice_here, tiles, functions)
@@ -628,6 +660,8 @@
         and rows % 2 == 0
         and 2 * functions == 3 * block
         and functions // 3 % density.shape[2] == 0
+        and cols <= NOTE
+        and 2 * cols + 2 <= 256
         and basis_values.shape[1] % 1024 == 0
     )
     plan = by_block_rows if fits else by_gathers

time: 187 us -> 178 us (0.952); the launches traced: 186 us -> 175 us
  blocking collectives: 31.8 us -> 15.9 us
  waiting for transfers between devices: 38.1 us -> 46.7 us
  starting transfers between devices: 69.7 us -> 66.8 us
  local copies, waits for them, and re-layouts: 3.44 us -> 5.49 us
    all_to_all x1 -> x0, blocking collectives: 14.7 us -> none  [by_block_rows(): terms.append(lax.all_to_all(term, 'col', 0, 0, tiled=True))]
    all_to_all x1 -> x2, waiting for transfers between devices: 0.01 us -> 11.7 us  [by_block_rows(): terms.append(lax.all_to_all(term, 'col', 0, 0, tiled=True))]
    ppermute x8 -> x4, starting transfers between devices: 12.8 us -> 6.96 us  [by_block_rows(): lax.ppermute(p, BOTH, chain.to_rows(turn))]
    ppermute x8 -> x4, waiting for transfers between devices: 8.88 us -> 3.29 us  [by_block_rows(): lax.ppermute(p, BOTH, chain.to_rows(turn))]
    all_to_all x1 -> x2, starting transfers between devices: 4.27 us -> 8.84 us  [by_block_rows(): terms.append(lax.all_to_all(term, 'col', 0, 0, tiled=True))]
    ppermute x4, starting transfers between devices: 18.2 us -> 14 us  [shifted_2(): return lax.ppermute(value, axis, pairs)]
    ppermute x8, starting transfers between devices: 25.6 us -> 28.5 us  [exchange_rows(): lax.ppermute(s, BOTH, chain.shift(by))]
    unnamed x31 -> x23, local copies, waits for them, and re-layouts: 2.81 us -> 4.89 us
  transfers between devices with their start and end apart: 26 -> 23, of which waited for: 13 -> 13; matrix products, arithmetic and copies ran while one was open for 1% -> 1% of each run, Pallas kernels for 15% -> 16%
where the time goes in v4:
time: 178 us; the launch traced here: 175 us
  starting transfers between devices  66.8 us (38%)
  waiting for transfers between devices  46.7 us (26%)
  Pallas kernels  36.5 us (21%)
  blocking collectives  15.9 us (9%)
  local copies, waits for them, and re-layouts  5.49 us (3%)
  other arithmetic  2.58 us (1%)
    ppermute x8, starting transfers between devices, exchange_rows(): lax.ppermute(s, BOTH, chain.shift(by))  28.5 us
    pallas_call x2, Pallas kernels, tile_call(): pl.pallas_call(body, grid=(count + 1,), in_specs=[SMEM_SPEC, pl.BlockSpec...  28.2 us
    ppermute x8, waiting for transfers between devices, exchange_rows(): lax.ppermute(s, BOTH, chain.shift(by))  16.7 us
    all_to_all x1, blocking collectives, by_block_rows(): window = lax.all_to_all(sent[tile], 'col', 0, 0, tiled=True)  15.9 us
    ppermute x4, starting transfers between devices, shifted_2(): return lax.ppermute(value, axis, pairs)  14 us
    all_to_all x2, waiting for transfers between devices, by_block_rows(): terms.append(lax.all_to_all(term, 'col', 0, 0, tiled=True))  11.7 us
    all_to_all x2, starting transfers between devices, by_block_rows(): terms.append(lax.all_to_all(term, 'col', 0, 0, tiled=True))  8.84 us
    ppermute x4, waiting for transfers between devices, by_block_rows(): lax.ppermute(p, BOTH, chain.to_slices(turn))  8.59 us
  transfers between devices with their start and end apart: 23, of which 13 were waited for; matrix products, arithmetic and copies ran while one was open for 1% of the time, Pallas kernels for 16%

profile of v4, /device:TPU:3, one launch (start us, length us, event | category | flops | bytes accessed | tf_op | source)
XLA Modules:
  0.0 174.9 jit_solution(10115308156745992)
XLA Ops:
  0.6 0.7 broadcast_subtract_fusion.steps_ref
  1.3 1.1 copy-done
  2.4 0.7 copy-done.4
  3.1 0.6 prepare.1
  3.7 3.8 %collective-permute-start = (bf16[208,256]{1,0:T(8,128)(2,1)S(1)}, bf16[208,256]{1,0:T(8,128)(2,1)S(1)}, u32[]{:S(2)}, u32[]{:S(2)}) collective-permute-start(bf16[208,256]{1,0:T(8,128)(2,1)S(1)} %get-tuple-element.34), channel_id=1, source_target_pairs={{0,0},{1,4},{2,1},{3,5},{4,2},{5,6},{6,3},{7,7},{8,11},{9,15},{10,... | collective-permute-start | bytes 319496 | tf_op jit(solution)/shard_map/ppermute | solution.py:619
  7.6 2.5 %collective-permute-start.2 = (bf16[208,256]{1,0:T(8,128)(2,1)S(1)}, bf16[208,256]{1,0:T(8,128)(2,1)S(1)}, u32[]{:S(2)}, u32[]{:S(2)}) collective-permute-start(bf16[208,256]{1,0:T(8,128)(2,1)S(1)} %get-tuple-element.36), channel_id=1, source_target_pairs={{0,1},{1,5},{2,0},{3,4},{4,3},{5,7},{6,2},{7,6},{8,10},{9,14},{10,... | collective-permute-start | bytes 319496 | tf_op jit(solution)/shard_map/ppermute | solution.py:619
  10.0 0.7 collective-permute-start.3
  11.4 1.6 collective-permute-done.1.refs_1_
  13.0 1.0 collective-permute-done.2.refs_2_
  14.1 4.9 %collective-permute-start.6 = (bf16[3,256,256]{2,1,0:T(8,128)(2,1)S(1)}, bf16[3,256,256]{2,1,0:T(8,128)(2,1)S(1)}, u32[]{:S(2)}, u32[]{:S(2)}) collective-permute-start(bf16[3,256,256]{2,1,0:T(8,128)(2,1)S(1)} %get-tuple-element.39.own_ref), channel_id=1, source_target_pairs={{4,0},{1,4},{5,1},{2,5},{6,2},{3,6},{7,3},{11,7},{15,11},{10,15},{... | collective-permute-start | bytes 1179656 | tf_op jit(solution)/shard_map/ppermute | solution.py:285
  19.0 4.8 %collective-permute-start.4 = (bf16[2,256,256]{2,1,0:T(8,128)(2,1)S(1)}, bf16[2,256,256]{2,1,0:T(8,128)(2,1)S(1)}, u32[]{:S(2)}, u32[]{:S(2)}) collective-permute-start(bf16[2,256,256]{2,1,0:T(8,128)(2,1)S(1)} %get-tuple-element.40), channel_id=1, source_target_pairs={{0,4},{4,1},{1,5},{5,2},{2,6},{6,3},{3,7},{7,11},{11,15},{15,10},{... | collective-permute-start | bytes 786440 | tf_op jit(solution)/shard_map/ppermute | solution.py:285
  23.9 4.2 %collective-permute-start.5 = (bf16[2,256,256]{2,1,0:T(8,128)(2,1)S(1)}, bf16[2,256,256]{2,1,0:T(8,128)(2,1)S(1)}, u32[]{:S(2)}, u32[]{:S(2)}) collective-permute-start(bf16[2,256,256]{2,1,0:T(8,128)(2,1)S(1)} %get-tuple-element.40), channel_id=1, source_target_pairs={{0,1},{4,5},{1,2},{5,6},{2,3},{6,7},{3,11},{7,15},{11,10},{15,14},... | collective-permute-start | bytes 786440 | tf_op jit(solution)/shard_map/ppermute | solution.py:284
  28.1 1.9 %collective-permute-start.7 = (bf16[2,256,256]{2,1,0:T(8,128)(2,1)S(1)}, bf16[2,256,256]{2,1,0:T(8,128)(2,1)S(1)}, u32[]{:S(2)}, u32[]{:S(2)}) collective-permute-start(bf16[2,256,256]{2,1,0:T(8,128)(2,1)S(1)} %get-tuple-element.41), channel_id=1, source_target_pairs={{1,0},{5,4},{2,1},{6,5},{3,2},{7,6},{11,3},{15,7},{10,11},{14,15},... | collective-permute-start | bytes 786440 | tf_op jit(solution)/shard_map/ppermute | solution.py:284
  30.0 4.2 %collective-permute-done.5.m2 = bf16[2,256,256]{2,1,0:T(8,128)(2,1)S(1)} collective-permute-done((bf16[2,256,256]{2,1,0:T(8,128)(2,1)S(1)}, bf16[2,256,256]{2,1,0:T(8,128)(2,1)S(1)}, u32[]{:S(2)}, u32[]{:S(2)}) %collective-permute-start.5) | collective-permute-done | bytes 262176 | tf_op jit(solution)/shard_map/ppermute | solution.py:284
  34.2 4.2 %collective-permute-done.7.p2 = bf16[2,256,256]{2,1,0:T(8,128)(2,1)S(1)} collective-permute-done((bf16[2,256,256]{2,1,0:T(8,128)(2,1)S(1)}, bf16[2,256,256]{2,1,0:T(8,128)(2,1)S(1)}, u32[]{:S(2)}, u32[]{:S(2)}) %collective-permute-start.7) | collective-permute-done | bytes 262176 | tf_op jit(solution)/shard_map/ppermute | solution.py:284
  38.4 1.5 purify_first.1
  40.0 2.1 %collective-permute-start.10 = (bf16[4,256,256]{2,1,0:T(8,128)(2,1)S(1)}, bf16[4,256,256]{2,1,0:T(8,128)(2,1)S(1)}, u32[]{:S(2)}, u32[]{:S(2)}) collective-permute-start(bf16[4,256,256]{2,1,0:T(8,128)(2,1)S(1)} %get-tuple-element.45), channel_id=1, source_target_pairs={{4,0},{1,4},{5,1},{2,5},{6,2},{3,6},{7,3},{11,7},{15,11},{10,15},{... | collective-permute-start | bytes 1572872 | tf_op jit(solution)/shard_map/ppermute | solution.py:285
  42.1 4.4 %collective-permute-start.8 = (bf16[4,256,256]{2,1,0:T(8,128)(2,1)S(1)}, bf16[4,256,256]{2,1,0:T(8,128)(2,1)S(1)}, u32[]{:S(2)}, u32[]{:S(2)}) collective-permute-start(bf16[4,256,256]{2,1,0:T(8,128)(2,1)S(1)} %get-tuple-element.43), channel_id=1, source_target_pairs={{0,4},{4,1},{1,5},{5,2},{2,6},{6,3},{3,7},{7,11},{11,15},{15,10},{... | collective-permute-start | bytes 1572872 | tf_op jit(solution)/shard_map/ppermute | solution.py:285
  46.4 1.9 %collective-permute-start.11 = (bf16[3,256,256]{2,1,0:T(8,128)(2,1)S(1)}, bf16[3,256,256]{2,1,0:T(8,128)(2,1)S(1)}, u32[]{:S(2)}, u32[]{:S(2)}) collective-permute-start(bf16[3,256,256]{2,1,0:T(8,128)(2,1)S(1)} %get-tuple-element.46), channel_id=1, source_target_pairs={{1,0},{5,4},{2,1},{6,5},{3,2},{7,6},{11,3},{15,7},{10,11},{14,15},... | collective-permute-start | bytes 1179656 | tf_op jit(solution)/shard_map/ppermute | solution.py:284
  48.4 4.3 %collective-permute-start.9 = (bf16[3,256,256]{2,1,0:T(8,128)(2,1)S(1)}, bf16[3,256,256]{2,1,0:T(8,128)(2,1)S(1)}, u32[]{:S(2)}, u32[]{:S(2)}) collective-permute-start(bf16[3,256,256]{2,1,0:T(8,128)(2,1)S(1)} %get-tuple-element.44), channel_id=1, source_target_pairs={{0,1},{4,5},{1,2},{5,6},{2,3},{6,7},{3,11},{7,15},{11,10},{15,14},... | collective-permute-start | bytes 1179656 | tf_op jit(solution)/shard_map/ppermute | solution.py:284
  52.6 7.2 %collective-permute-done.11.refs_6_ = bf16[3,256,256]{2,1,0:T(8,128)(2,1)S(1)} collective-permute-done((bf16[3,256,256]{2,1,0:T(8,128)(2,1)S(1)}, bf16[3,256,256]{2,1,0:T(8,128)(2,1)S(1)}, u32[]{:S(2)}, u32[]{:S(2)}) %collective-permute-start.11) | collective-permute-done | bytes 393248 | tf_op jit(solution)/shard_map/ppermute | solution.py:284
  59.8 1.2 collective-permute-done.9.refs_4_
  61.0 1.5 purify.1
  62.5 2.7 %collective-permute-start.12 = (bf16[336,256]{1,0:T(8,128)(2,1)S(1)}, bf16[336,256]{1,0:T(8,128)(2,1)S(1)}, u32[]{:S(2)}, u32[]{:S(2)}) collective-permute-start(bf16[336,256]{1,0:T(8,128)(2,1)S(1)} %get-tuple-element.48), channel_id=1, source_target_pairs={{0,0},{4,1},{1,2},{5,3},{2,4},{6,5},{3,6},{7,7},{11,8},{15,9},{10,... | collective-permute-start | bytes 516104 | tf_op jit(solution)/shard_map/ppermute | solution.py:630
  65.6 1.1 collective-permute-start.14
  66.8 0.7 collective-permute-start.15
  67.4 7.8 %collective-permute-done.12.refs_0_ = bf16[336,256]{1,0:T(8,128)(2,1)S(1)} collective-permute-done((bf16[336,256]{1,0:T(8,128)(2,1)S(1)}, bf16[336,256]{1,0:T(8,128)(2,1)S(1)}, u32[]{:S(2)}, u32[]{:S(2)}) %collective-permute-start.12) | collective-permute-done | bytes 172064 | tf_op jit(solution)/shard_map/ppermute | solution.py:630
  76.7 0.7 copy-done.9
  77.4 2.1 %join_slices.1 = (bf16[4,5,64,256]{3,2,1,0:T(8,128)(2,1)}, bf16[2,64,256]{2,1,0:T(8,128)(2,1)}, bf16[2,64,256]{2,1,0:T(8,128)(2,1)}, s32[4,2]{1,0:T(4,128)}) custom-call(s32[1]{0:T(128)} %bitcast.slice_ref.place_ref, bf16[336,256]{1,0:T(8,128)(2,1)} %copy-done.6, bf16[336,256]{1,0:T(8,128)(2,1)} %copy-done.7, bf16[336,256]{1,0:T(8,128)(2,1)} %copy-done.8, ...), custom_call_target="tpu_custom_call" | custom-call | tf_op jit(solution)/shard_map/join_slices/pallas_call | solution.py:396
  79.5 4.5 %collective-permute-start.16 = (bf16[2,64,256]{2,1,0:T(8,128)(2,1)}, bf16[2,64,256]{2,1,0:T(8,128)(2,1)S(1)}, u32[]{:S(2)}, u32[]{:S(2)}) collective-permute-start(bf16[2,64,256]{2,1,0:T(8,128)(2,1)} %get-tuple-element.54), channel_id=1, source_target_pairs={{0,4},{4,8},{8,12},{12,16},{16,20},{20,24},{24,28},{1,5},{5,9},{9,... | collective-permute-start | bytes 196616 | tf_op jit(solution)/shard_map/ppermute | solution.py:36
  84.0 4.7 %collective-permute-start.17 = (bf16[2,64,256]{2,1,0:T(8,128)(2,1)}, bf16[2,64,256]{2,1,0:T(8,128)(2,1)S(1)}, u32[]{:S(2)}, u32[]{:S(2)}) collective-permute-start(bf16[2,64,256]{2,1,0:T(8,128)(2,1)} %get-tuple-element.55), channel_id=1, source_target_pairs={{4,0},{8,4},{12,8},{16,12},{20,16},{24,20},{28,24},{5,1},{9,5},{13... | collective-permute-start | bytes 196616 | tf_op jit(solution)/shard_map/ppermute | solution.py:36
  88.7 3.4 %collective-permute-done.17.below_ref = bf16[2,64,256]{2,1,0:T(8,128)(2,1)S(1)} collective-permute-done((bf16[2,64,256]{2,1,0:T(8,128)(2,1)}, bf16[2,64,256]{2,1,0:T(8,128)(2,1)S(1)}, u32[]{:S(2)}, u32[]{:S(2)}) %collective-permute-start.17) | collective-permute-done | bytes 65568 | tf_op jit(solution)/shard_map/ppermute | solution.py:36
  92.1 1.1 copy-done.1
  93.2 0.7 copy-done.2
  93.9 1.5 pack_windows.1
  95.4 15.9 %all_to_all.20.pieces_ref = bf16[4,2,64,384]{3,2,1,0:T(8,128)(2,1)S(1)} all-to-all(bf16[4,2,64,384]{3,2,1,0:T(8,128)(2,1)S(1)} %get-tuple-element.58), channel_id=1, replica_groups=mesh['row'=8,'col'=4] {'col'}, dimensions={0} | all-to-all | bytes 786432 | tf_op jit(solution)/shard_map/all_to_all | solution.py:639
  111.2 3.6 %all-to-all-start = ((bf16[4,2,64,384]{3,2,1,0:T(8,128)(2,1)}), bf16[4,2,64,384]{3,2,1,0:T(8,128)(2,1)S(1)}, u32[]{:S(2)}, u32[]{:S(2)}) async-start(bf16[4,2,64,384]{3,2,1,0:T(8,128)(2,1)} %get-tuple-element.56), calls=%async_computation | async-start | bytes 786432 | tf_op jit(solution)/shard_map/all_to_all | solution.py:639
  115.5 14.1 %tile.3 = (f32[32,128]{1,0:T(8,128)S(1)}, bf16[4,2,64,384]{3,2,1,0:T(8,128)(2,1)}) custom-call(s32[1]{0:T(128)} %get-tuple-element.65.step_ref, bf16[2,4096,384]{2,1,0:T(8,128)(2,1)} %v_ref.3, bf16[3,2,4096,384]{3,2,1,0:T(8,128)(2,1)} %g_ref.3, f32[2,32,128]{2,1,0:T(8,128)S(1)} %bitcast.10, bf16[4,2,64,384]{3,2,1,0:T(8,128)(2,1)S(1)} %all_to_all.20.pieces_ref), custom_call_target="tpu_custom_call" | custom-call | tf_op jit(solution)/shard_map/tile/pallas_call | solution.py:541
  129.6 4.3 %all-to-all-start.3 = ((bf16[4,2,64,384]{3,2,1,0:T(8,128)(2,1)}), bf16[4,2,64,384]{3,2,1,0:T(8,128)(2,1)S(1)}, u32[]{:S(2)}, u32[]{:S(2)}) async-start(bf16[4,2,64,384]{3,2,1,0:T(8,128)(2,1)} %get-tuple-element.59), calls=%async_computation.3 | async-start | bytes 786432 | tf_op jit(solution)/shard_map/all_to_all | solution.py:644
  133.9 14.1 %tile.2 = (f32[32,128]{1,0:T(8,128)S(1)}, bf16[4,2,64,384]{3,2,1,0:T(8,128)(2,1)}) custom-call(s32[1]{0:T(128)} %get-tuple-element.66.step_ref, bf16[2,4096,384]{2,1,0:T(8,128)(2,1)} %v_ref.3, bf16[3,2,4096,384]{3,2,1,0:T(8,128)(2,1)} %g_ref.3, f32[2,32,128]{2,1,0:T(8,128)S(1)} %bitcast.11, bf16[4,2,64,384]{3,2,1,0:T(8,128)(2,1)S(1)} %all-to-all-done.pieces_ref), custom_call_target="tpu_custom_call" | custom-call | tf_op jit(solution)/shard_map/tile/pallas_call | solution.py:541
  148.0 4.5 %all-to-all-start.1 = ((bf16[4,2,64,384]{3,2,1,0:T(8,128)(2,1)}), bf16[4,2,64,384]{3,2,1,0:T(8,128)(2,1)S(1)}, u32[]{:S(2)}, u32[]{:S(2)}) async-start(bf16[4,2,64,384]{3,2,1,0:T(8,128)(2,1)} %get-tuple-element.57), calls=%async_computation.1 | async-start | bytes 786432 | tf_op jit(solution)/shard_map/all_to_all | solution.py:644
  152.5 11.7 %all-to-all-done.1.refs_0_ = bf16[4,2,64,384]{3,2,1,0:T(8,128)(2,1)S(1)} async-done(((bf16[4,2,64,384]{3,2,1,0:T(8,128)(2,1)}), bf16[4,2,64,384]{3,2,1,0:T(8,128)(2,1)S(1)}, u32[]{:S(2)}, u32[]{:S(2)}) %all-to-all-start.1) | async-done | bytes 393248 | tf_op jit(solution)/shard_map/all_to_all | solution.py:644
  164.2 1.0 add_terms.1
  165.2 1.9 %collective-permute-start.18 = (bf16[2,64,256]{2,1,0:T(8,128)(2,1)S(1)}, bf16[2,64,256]{2,1,0:T(8,128)(2,1)S(1)}, u32[]{:S(2)}, u32[]{:S(2)}) collective-permute-start(bf16[2,64,256]{2,1,0:T(8,128)(2,1)S(1)} %get-tuple-element.61), channel_id=1, source_target_pairs={{0,4},{4,8},{8,12},{12,16},{16,20},{20,24},{24,28},{1,5},{5,9},{9,... | collective-permute-start | bytes 196616 | tf_op jit(solution)/shard_map/ppermute | solution.py:36
  167.2 2.8 %collective-permute-start.19 = (bf16[2,64,256]{2,1,0:T(8,128)(2,1)S(1)}, bf16[2,64,256]{2,1,0:T(8,128)(2,1)S(1)}, u32[]{:S(2)}, u32[]{:S(2)}) collective-permute-start(bf16[2,64,256]{2,1,0:T(8,128)(2,1)S(1)} %get-tuple-element.62), channel_id=1, source_target_pairs={{4,0},{8,4},{12,8},{16,12},{20,16},{24,20},{28,24},{5,1},{9,5},{13... | collective-permute-start | bytes 196616 | tf_op jit(solution)/shard_map/ppermute | solution.py:36
  170.0 0.6 pad_maximum_fusion
  170.7 3.0 %collective-permute-done.19 = bf16[2,64,256]{2,1,0:T(8,128)(2,1)S(1)} collective-permute-done((bf16[2,64,256]{2,1,0:T(8,128)(2,1)S(1)}, bf16[2,64,256]{2,1,0:T(8,128)(2,1)S(1)}, u32[]{:S(2)}, u32[]{:S(2)}) %collective-permute-start.19) | collective-permute-done | bytes 65568 | tf_op jit(solution)/shard_map/ppermute | solution.py:36
  173.7 1.2 pad_select_fusion
  (37 shorter events, 3.4 us)
Async XLA Ops:
  1.3 1.1 copy-start
  2.4 0.7 copy-start.4
  3.7 7.7 %collective-permute-start = (bf16[208,256]{1,0:T(8,128)(2,1)S(1)}, bf16[208,256]{1,0:T(8,128)(2,1)S(1)}, u32[]{:S(2)}, u32[]{:S(2)}) collective-permute-start(bf16[208,256]{1,0:T(8,128)(2,1)S(1)} %get-tuple-element.34), channel_id=1, source_target_pairs={{0,0},{1,4},{2,1},{3,5},{4,2},{5,6},{6,3},{7,7},{8,11},{9,15},{10,... | collective-permute-start | bytes 319496 | tf_op jit(solution)/shard_map/ppermute | solution.py:619
  7.5 5.5 %collective-permute-start.1 = (bf16[208,256]{1,0:T(8,128)(2,1)S(1)}, bf16[208,256]{1,0:T(8,128)(2,1)S(1)}, u32[]{:S(2)}, u32[]{:S(2)}) collective-permute-start(bf16[208,256]{1,0:T(8,128)(2,1)S(1)} %get-tuple-element.35), channel_id=1, source_target_pairs={{0,4},{1,0},{2,5},{3,1},{4,6},{5,2},{6,7},{7,3},{8,15},{9,11},{10,... | collective-permute-start | bytes 319496 | tf_op jit(solution)/shard_map/ppermute | solution.py:619
  7.6 6.5 %collective-permute-start.2 = (bf16[208,256]{1,0:T(8,128)(2,1)S(1)}, bf16[208,256]{1,0:T(8,128)(2,1)S(1)}, u32[]{:S(2)}, u32[]{:S(2)}) collective-permute-start(bf16[208,256]{1,0:T(8,128)(2,1)S(1)} %get-tuple-element.36), channel_id=1, source_target_pairs={{0,1},{1,5},{2,0},{3,4},{4,3},{5,7},{6,2},{7,6},{8,10},{9,14},{10,... | collective-permute-start | bytes 319496 | tf_op jit(solution)/shard_map/ppermute | solution.py:619
  10.0 4.0 %collective-permute-start.3 = (bf16[208,256]{1,0:T(8,128)(2,1)S(1)}, bf16[208,256]{1,0:T(8,128)(2,1)S(1)}, u32[]{:S(2)}, u32[]{:S(2)}) collective-permute-start(bf16[208,256]{1,0:T(8,128)(2,1)S(1)} %get-tuple-element.37), channel_id=1, source_target_pairs={{0,5},{1,1},{2,4},{3,0},{4,7},{5,3},{6,6},{7,2},{8,14},{9,10},{10,... | collective-permute-start | bytes 319496 | tf_op jit(solution)/shard_map/ppermute | solution.py:619
  14.1 24.3 %collective-permute-start.6 = (bf16[3,256,256]{2,1,0:T(8,128)(2,1)S(1)}, bf16[3,256,256]{2,1,0:T(8,128)(2,1)S(1)}, u32[]{:S(2)}, u32[]{:S(2)}) collective-permute-start(bf16[3,256,256]{2,1,0:T(8,128)(2,1)S(1)} %get-tuple-element.39.own_ref), channel_id=1, source_target_pairs={{4,0},{1,4},{5,1},{2,5},{6,2},{3,6},{7,3},{11,7},{15,11},{10,15},{... | collective-permute-start | bytes 1179656 | tf_op jit(solution)/shard_map/ppermute | solution.py:285
  19.0 11.0 %collective-permute-start.4 = (bf16[2,256,256]{2,1,0:T(8,128)(2,1)S(1)}, bf16[2,256,256]{2,1,0:T(8,128)(2,1)S(1)}, u32[]{:S(2)}, u32[]{:S(2)}) collective-permute-start(bf16[2,256,256]{2,1,0:T(8,128)(2,1)S(1)} %get-tuple-element.40), channel_id=1, source_target_pairs={{0,4},{4,1},{1,5},{5,2},{2,6},{6,3},{3,7},{7,11},{11,15},{15,10},{... | collective-permute-start | bytes 786440 | tf_op jit(solution)/shard_map/ppermute | solution.py:285
  23.9 10.3 %collective-permute-start.5 = (bf16[2,256,256]{2,1,0:T(8,128)(2,1)S(1)}, bf16[2,256,256]{2,1,0:T(8,128)(2,1)S(1)}, u32[]{:S(2)}, u32[]{:S(2)}) collective-permute-start(bf16[2,256,256]{2,1,0:T(8,128)(2,1)S(1)} %get-tuple-element.40), channel_id=1, source_target_pairs={{0,1},{4,5},{1,2},{5,6},{2,3},{6,7},{3,11},{7,15},{11,10},{15,14},... | collective-permute-start | bytes 786440 | tf_op jit(solution)/shard_map/ppermute | solution.py:284
  28.1 10.3 %collective-permute-start.7 = (bf16[2,256,256]{2,1,0:T(8,128)(2,1)S(1)}, bf16[2,256,256]{2,1,0:T(8,128)(2,1)S(1)}, u32[]{:S(2)}, u32[]{:S(2)}) collective-permute-start(bf16[2,256,256]{2,1,0:T(8,128)(2,1)S(1)} %get-tuple-element.41), channel_id=1, source_target_pairs={{1,0},{5,4},{2,1},{6,5},{3,2},{7,6},{11,3},{15,7},{10,11},{14,15},... | collective-permute-start | bytes 786440 | tf_op jit(solution)/shard_map/ppermute | solution.py:284
  40.0 21.0 %collective-permute-start.10 = (bf16[4,256,256]{2,1,0:T(8,128)(2,1)S(1)}, bf16[4,256,256]{2,1,0:T(8,128)(2,1)S(1)}, u32[]{:S(2)}, u32[]{:S(2)}) collective-permute-start(bf16[4,256,256]{2,1,0:T(8,128)(2,1)S(1)} %get-tuple-element.45), channel_id=1, source_target_pairs={{4,0},{1,4},{5,1},{2,5},{6,2},{3,6},{7,3},{11,7},{15,11},{10,15},{... | collective-permute-start | bytes 1572872 | tf_op jit(solution)/shard_map/ppermute | solution.py:285
  42.1 18.9 %collective-permute-start.8 = (bf16[4,256,256]{2,1,0:T(8,128)(2,1)S(1)}, bf16[4,256,256]{2,1,0:T(8,128)(2,1)S(1)}, u32[]{:S(2)}, u32[]{:S(2)}) collective-permute-start(bf16[4,256,256]{2,1,0:T(8,128)(2,1)S(1)} %get-tuple-element.43), channel_id=1, source_target_pairs={{0,4},{4,1},{1,5},{5,2},{2,6},{6,3},{3,7},{7,11},{11,15},{15,10},{... | collective-permute-start | bytes 1572872 | tf_op jit(solution)/shard_map/ppermute | solution.py:285
  46.4 13.4 %collective-permute-start.11 = (bf16[3,256,256]{2,1,0:T(8,128)(2,1)S(1)}, bf16[3,256,256]{2,1,0:T(8,128)(2,1)S(1)}, u32[]{:S(2)}, u32[]{:S(2)}) collective-permute-start(bf16[3,256,256]{2,1,0:T(8,128)(2,1)S(1)} %get-tuple-element.46), channel_id=1, source_target_pairs={{1,0},{5,4},{2,1},{6,5},{3,2},{7,6},{11,3},{15,7},{10,11},{14,15},... | collective-permute-start | bytes 1179656 | tf_op jit(solution)/shard_map/ppermute | solution.py:284
  48.4 12.6 %collective-permute-start.9 = (bf16[3,256,256]{2,1,0:T(8,128)(2,1)S(1)}, bf16[3,256,256]{2,1,0:T(8,128)(2,1)S(1)}, u32[]{:S(2)}, u32[]{:S(2)}) collective-permute-start(bf16[3,256,256]{2,1,0:T(8,128)(2,1)S(1)} %get-tuple-element.44), channel_id=1, source_target_pairs={{0,1},{4,5},{1,2},{5,6},{2,3},{6,7},{3,11},{7,15},{11,10},{15,14},... | collective-permute-start | bytes 1179656 | tf_op jit(solution)/shard_map/ppermute | solution.py:284
  62.5 12.7 %collective-permute-start.12 = (bf16[336,256]{1,0:T(8,128)(2,1)S(1)}, bf16[336,256]{1,0:T(8,128)(2,1)S(1)}, u32[]{:S(2)}, u32[]{:S(2)}) collective-permute-start(bf16[336,256]{1,0:T(8,128)(2,1)S(1)} %get-tuple-element.48), channel_id=1, source_target_pairs={{0,0},{4,1},{1,2},{5,3},{2,4},{6,5},{3,6},{7,7},{11,8},{15,9},{10,... | collective-permute-start | bytes 516104 | tf_op jit(solution)/shard_map/ppermute | solution.py:630
  65.2 10.4 %collective-permute-start.13 = (bf16[336,256]{1,0:T(8,128)(2,1)S(1)}, bf16[336,256]{1,0:T(8,128)(2,1)S(1)}, u32[]{:S(2)}, u32[]{:S(2)}) collective-permute-start(bf16[336,256]{1,0:T(8,128)(2,1)S(1)} %get-tuple-element.49), channel_id=1, source_target_pairs={{4,0},{0,1},{5,2},{1,3},{6,4},{2,5},{7,6},{3,7},{15,8},{11,9},{14,... | collective-permute-start | bytes 516104 | tf_op jit(solution)/shard_map/ppermute | solution.py:630
  65.6 10.4 %collective-permute-start.14 = (bf16[336,256]{1,0:T(8,128)(2,1)S(1)}, bf16[336,256]{1,0:T(8,128)(2,1)S(1)}, u32[]{:S(2)}, u32[]{:S(2)}) collective-permute-start(bf16[336,256]{1,0:T(8,128)(2,1)S(1)} %get-tuple-element.50), channel_id=1, source_target_pairs={{1,0},{5,1},{0,2},{4,3},{3,4},{7,5},{2,6},{6,7},{10,8},{14,9},{11,... | collective-permute-start | bytes 516104 | tf_op jit(solution)/shard_map/ppermute | solution.py:630
  66.8 9.3 %collective-permute-start.15 = (bf16[336,256]{1,0:T(8,128)(2,1)S(1)}, bf16[336,256]{1,0:T(8,128)(2,1)S(1)}, u32[]{:S(2)}, u32[]{:S(2)}) collective-permute-start(bf16[336,256]{1,0:T(8,128)(2,1)S(1)} %get-tuple-element.51), channel_id=1, source_target_pairs={{5,0},{1,1},{4,2},{0,3},{7,4},{3,5},{6,6},{2,7},{14,8},{10,9},{15,... | collective-permute-start | bytes 516104 | tf_op jit(solution)/shard_map/ppermute | solution.py:630
  75.2 0.8 copy-start.6
  75.7 0.7 copy-start.7
  76.0 0.7 copy-start.8
  76.7 0.7 copy-start.9
  77.4 37.5 %copy-start.10 = (f32[2,4096]{1,0:T(2,128)S(1)}, f32[2,4096]{1,0:T(2,128)}, u32[]{:S(2)}) copy-start(f32[2,4096]{1,0:T(2,128)} %param.11) | copy-start | bytes 98308
  79.5 9.2 %collective-permute-start.16 = (bf16[2,64,256]{2,1,0:T(8,128)(2,1)}, bf16[2,64,256]{2,1,0:T(8,128)(2,1)S(1)}, u32[]{:S(2)}, u32[]{:S(2)}) collective-permute-start(bf16[2,64,256]{2,1,0:T(8,128)(2,1)} %get-tuple-element.54), channel_id=1, source_target_pairs={{0,4},{4,8},{8,12},{12,16},{16,20},{20,24},{24,28},{1,5},{5,9},{9,... | collective-permute-start | bytes 196616 | tf_op jit(solution)/shard_map/ppermute | solution.py:36
  84.0 8.1 %collective-permute-start.17 = (bf16[2,64,256]{2,1,0:T(8,128)(2,1)}, bf16[2,64,256]{2,1,0:T(8,128)(2,1)S(1)}, u32[]{:S(2)}, u32[]{:S(2)}) collective-permute-start(bf16[2,64,256]{2,1,0:T(8,128)(2,1)} %get-tuple-element.55), channel_id=1, source_target_pairs={{4,0},{8,4},{12,8},{16,12},{20,16},{24,20},{28,24},{5,1},{9,5},{13... | collective-permute-start | bytes 196616 | tf_op jit(solution)/shard_map/ppermute | solution.py:36
  92.1 1.1 copy-start.1
  93.2 0.7 copy-start.2
  111.2 18.3 %all-to-all-start = ((bf16[4,2,64,384]{3,2,1,0:T(8,128)(2,1)}), bf16[4,2,64,384]{3,2,1,0:T(8,128)(2,1)S(1)}, u32[]{:S(2)}, u32[]{:S(2)}) async-start(bf16[4,2,64,384]{3,2,1,0:T(8,128)(2,1)} %get-tuple-element.56), calls=%async_computation | async-start | bytes 786432 | tf_op jit(solution)/shard_map/all_to_all | solution.py:639
  129.6 18.4 %all-to-all-start.3 = ((bf16[4,2,64,384]{3,2,1,0:T(8,128)(2,1)}), bf16[4,2,64,384]{3,2,1,0:T(8,128)(2,1)S(1)}, u32[]{:S(2)}, u32[]{:S(2)}) async-start(bf16[4,2,64,384]{3,2,1,0:T(8,128)(2,1)} %get-tuple-element.59), calls=%async_computation.3 | async-start | bytes 786432 | tf_op jit(solution)/shard_map/all_to_all | solution.py:644
  133.9 18.6 %copy-start.5 = (s32[4,5]{1,0:T(4,128)S(1)}, s32[4,5]{1,0:T(4,128)}, u32[]{:S(2)}) copy-start(s32[4,5]{1,0:T(4,128)} %pattern_ref.1) | copy-start | bytes 244
  133.9 30.3 %copy-start.3 = (s32[4,2]{1,0:T(4,128)S(1)}, s32[4,2]{1,0:T(4,128)}, u32[]{:S(2)}) copy-start(s32[4,2]{1,0:T(4,128)} %get-tuple-element.53.steps_ref) | copy-start | bytes 100
  148.0 16.2 %all-to-all-start.1 = ((bf16[4,2,64,384]{3,2,1,0:T(8,128)(2,1)}), bf16[4,2,64,384]{3,2,1,0:T(8,128)(2,1)S(1)}, u32[]{:S(2)}, u32[]{:S(2)}) async-start(bf16[4,2,64,384]{3,2,1,0:T(8,128)(2,1)} %get-tuple-element.57), calls=%async_computation.1 | async-start | bytes 786432 | tf_op jit(solution)/shard_map/all_to_all | solution.py:644
  165.2 5.4 %collective-permute-start.18 = (bf16[2,64,256]{2,1,0:T(8,128)(2,1)S(1)}, bf16[2,64,256]{2,1,0:T(8,128)(2,1)S(1)}, u32[]{:S(2)}, u32[]{:S(2)}) collective-permute-start(bf16[2,64,256]{2,1,0:T(8,128)(2,1)S(1)} %get-tuple-element.61), channel_id=1, source_target_pairs={{0,4},{4,8},{8,12},{12,16},{16,20},{20,24},{24,28},{1,5},{5,9},{9,... | collective-permute-start | bytes 196616 | tf_op jit(solution)/shard_map/ppermute | solution.py:36
  167.2 6.5 %collective-permute-start.19 = (bf16[2,64,256]{2,1,0:T(8,128)(2,1)S(1)}, bf16[2,64,256]{2,1,0:T(8,128)(2,1)S(1)}, u32[]{:S(2)}, u32[]{:S(2)}) collective-permute-start(bf16[2,64,256]{2,1,0:T(8,128)(2,1)S(1)} %get-tuple-element.62), channel_id=1, source_target_pairs={{4,0},{8,4},{12,8},{16,12},{20,16},{24,20},{28,24},{5,1},{9,5},{13... | collective-permute-start | bytes 196616 | tf_op jit(solution)/shard_map/ppermute | solution.py:36

commit v5 on v4

--- a/solution.py
+++ b/solution.py
@@ -126,7 +126,7 @@
     step_size = functions // 3
     kept = (pattern > 0)[:, :, None, None]
     current = jnp.where(kept, density, jnp.zeros_like(density))
-    for iteration in range(ITERS):
+    for _ in range(ITERS):
         square = jnp.where(kept, times_current(current, current), 0.0).astype(jnp.bfloat16)
         cubic = times_current(square, current)
         current = jnp.where(kept, 3.0 * square.astype(jnp.float32) - 2.0 * cubic, 0.0).astype(
@@ -204,20 +204,20 @@
         return [(self.device(i), self.device(i + by)) for i in range(self.count) if 0 <= i + by < self.count]
 
 
+SMALL = 12 << 20
 BOTH = ("row", "col")
 VMEM_SPEC = pl.BlockSpec(memory_space=pltpu.VMEM)
 SMEM_SPEC = pl.BlockSpec(memory_space=pltpu.SMEM)
 
 
-def small_call(body, name, scalars, arrays, outs, scratch=()):
+def small_call(body, scalars, arrays, outs, scratch=()):
     return pl.pallas_call(
         body,
         in_specs=[SMEM_SPEC] * len(scalars) + [VMEM_SPEC] * len(arrays),
         out_specs=[VMEM_SPEC] * len(outs),
         out_shape=[jax.ShapeDtypeStruct(s, d) for s, d in outs],
         scratch_shapes=[pltpu.VMEM(s, d) for s, d in scratch],
-        compiler_params=pltpu.CompilerParams(vmem_limit_bytes=48 << 20),
-        name=name,
+        compiler_params=pltpu.CompilerParams(vmem_limit_bytes=SMALL),
     )(*scalars, *arrays)
 
 
@@ -249,7 +249,7 @@
             outs[turn][3 * high :] = note.astype(BF16)
 
     shapes = [((3 * high + NOTE, block), BF16)] * cols
-    return small_call(body, "prepare", [pattern, steps, slice_here], [density], shapes)
+    return small_call(body, [pattern, steps, slice_here], [density], shapes)
 
 
 def join_rows(pieces, place, block):
@@ -277,13 +277,14 @@
 
     two, three = ((2, block, block), BF16), ((3, block, block), BF16)
     shapes = [three, two, two, ((NOTE, block), F32), ((NOTE, block), BF16)]
-    return small_call(body, "join_rows", [place], pieces, shapes)
+    return small_call(body, [place], pieces, shapes)
 
 
 def exchange_rows(chain, sends):
-    far = [lax.ppermute(s, BOTH, chain.shift(by)) for s, by in zip(sends[1::2], (2, -2))]
-    near = [lax.ppermute(s, BOTH, chain.shift(by)) for s, by in zip(sends[0::2], (1, -1))]
-    return near[0], far[0], near[1], far[1]
+    got = {}
+    for by, send in zip((1, 2, -1, -2), sends):
+        got[by] = lax.ppermute(send, BOTH, chain.shift(by))
+    return got[1], got[2], got[-1], got[-2]
 
 
 def purify_math(kept_ref, left, right, square, store):
@@ -331,7 +332,7 @@
     whole = ((5, block, block), BF16)
     shapes = [whole] + [((top - low, block, block), BF16) for low, top in SENDS]
     scratch = [whole, ((len(flipped), block, block), BF16)]
-    return small_call(body, "purify_first", [], [kept, own] + list(near), shapes, scratch)
+    return small_call(body, [], [kept, own] + list(near), shapes, scratch)
 
 
 def purify_next(own, near, kept, block, place, steps, cols):
@@ -368,41 +369,46 @@
         shapes = [((5 * high + NOTE, block), BF16)] * cols
     else:
         shapes = [whole] + [((top - low, block, block), BF16) for low, top in SENDS]
-    return small_call(
-        body, "purify", [place] if last else [], [kept, own] + list(near) + [steps], shapes, [whole, whole]
-    )
-
-
-def join_slices(pieces, place, tiles, block):
+    return small_call(body, [place] if last else [], [kept, own] + list(near) + [steps], shapes, [whole, whole])
+
+
+def join_slices(pieces, place, block):
     cols = len(pieces)
     high = block // cols
 
     def body(place_ref, *refs):
-        ins, (out, down, up, steps) = refs[:cols], refs[cols:]
+        ins, (out, down, up) = refs[:cols], refs[cols:]
         for turn in range(cols):
             j = mixed(place_ref[0], turn, cols)
             for d in range(5):
                 out[j, d] = ins[turn][d * high : (d + 1) * high]
         down[...] = out[cols - 1, 2:4]
         up[...] = out[0, 1:3]
-        note = ins[0][5 * high :].astype(F32)
+
+    edge = ((2, high, block), BF16)
+    return small_call(body, [place], pieces, [((cols, 5, high, block), BF16), edge, edge])
+
+
+def read_steps(piece, cols, tiles):
+    rows, block = piece.shape
+
+    def body(piece_ref, steps):
+        note = piece_ref[...].astype(F32)
         row, lane = grid_of((NOTE, block), 0), grid_of((NOTE, block), 1)
         for source in range(cols):
             for tile in range(tiles):
                 here = jnp.where((row == source) & (lane == tile), note, 0.0)
                 steps[source, tile] = jnp.sum(here).astype(jnp.int32)
 
-    edge = jax.ShapeDtypeStruct((2, high, block), BF16)
     return pl.pallas_call(
         body,
-        in_specs=[SMEM_SPEC] + [VMEM_SPEC] * cols,
-        out_specs=[VMEM_SPEC] * 3 + [SMEM_SPEC],
-        out_shape=[
-            jax.ShapeDtypeStruct((cols, 5, high, block), BF16), edge, edge,
-            jax.ShapeDtypeStruct((cols, tiles), jnp.int32),
-        ],
-        name="join_slices",
-    )(place, *pieces)
+        grid=(1,),
+        in_specs=[pl.BlockSpec((NOTE, block), lambda i: (rows // NOTE - 1, 0))],
+        out_specs=SMEM_SPEC,
+        out_shape=jax.ShapeDtypeStruct((cols, tiles), jnp.int32),
+        compiler_params=pltpu.CompilerParams(vmem_limit_bytes=1 << 20),
+        name="read_steps",
+    )(piece)
 
 
 def slot_of(step, half):
@@ -438,7 +444,7 @@
                 outs[tile][to, 1] = near[1, step // 2 + 1, :, lanes]
 
     return small_call(
-        body, "pack_windows", [steps, place], [purified, above, below],
+        body, [steps, place], [purified, above, below],
         [((cols, 2, high, functions), BF16)] * tiles, [((2, cols + 2, high, 2 * block), BF16)],
     )
 
@@ -457,75 +463,79 @@
     return 0.5 * by_density * scaled, [2.0 * by_gradient * scaled * gk for gk in g]
 
 
-def tile_call(tile, basis_values, basis_grads, quadrature, pieces, step, rows=1024):
-    points, functions = basis_values.shape[1:]
+def tile_call(tile, basis_values, basis_grads, weights, pieces, step, rows=1024, parts=2):
+    tiles, points, functions = basis_values.shape
     cols, _, high, _ = pieces.shape
     part = functions // 3
     per_half = part // high
-    count, blocks = points // rows, rows // 128
-
-    def body(step_ref, v_ref, g_ref, w_ref, pieces_ref, dens_ref, term_ref, win_ref, vs_ref, z_ref, y_ref):
+    count, sub, lanes = points // rows, rows // parts, functions // 128
+
+    def body(step_ref, v_ref, g_ref, w_ref, pieces_ref, dens_ref, term_ref, win_ref, kept_ref, y_ref, *bufs):
         i = pl.program_id(0)
         offset = step_ref[0] % 2
+        x_refs, z_refs = bufs[:parts], bufs[parts:]
+        ones = jnp.ones((8, 128), BF16)
 
         @pl.when(i == 0)
         def _():
+            kept_ref[...] = jnp.zeros(kept_ref.shape, BF16)
+            z_refs[-1][...] = jnp.zeros(z_refs[-1].shape, BF16)
+            y_ref[...] = jnp.zeros(y_ref.shape, F32)
             for h in range(3):
-                for sub in range(per_half):
-                    source = per_half * ((offset + h) % 2) + sub
-                    win_ref[part * h + high * sub : part * h + high * (sub + 1)] = pieces_ref[source, h // 2]
-
-        def forward():
-            window = win_ref[...]
-            lane = lax.broadcasted_iota(jnp.int32, (128, 128), 1)
-            sums = jnp.zeros((128, 128), F32)
-            for b in range(blocks):
-                at = slice(128 * b, 128 * (b + 1))
-                v = v_ref[at]
-                x = jnp.dot(v, window, preferred_element_type=F32)
-                sums = jnp.where(lane == b, jnp.sum(x * v.astype(F32), axis=1, keepdims=True), sums)
-                for k in range(3):
-                    gk = g_ref[k, at].astype(F32)
-                    sums = jnp.where(lane == blocks * (k + 1) + b, jnp.sum(x * gk, axis=1, keepdims=True), sums)
-            sums = sums.T
-            n = sums[:blocks] * (1.0 / functions)
-            g = [sums[blocks * (k + 1) : blocks * (k + 2)] * (2.0 / functions) for k in range(3)]
-            dens_ref[...] = n
-            c0, ck = pointwise(n, g, w_ref[...], points)
-            c = jnp.concatenate([c0] + ck + [jnp.zeros((128 - 4 * blocks, 128), F32)], axis=0).T
-            for b in range(blocks):
-                at = slice(128 * b, 128 * (b + 1))
-                v = v_ref[at]
-                z = c[:, b : b + 1] * v.astype(F32)
-                for k in range(3):
-                    col = blocks * (k + 1) + b
-                    z = z + c[:, col : col + 1] * g_ref[k, at].astype(F32)
-                z_ref[i % 2, at] = z.astype(BF16)
-                vs_ref[i % 2, at] = v
-
-        def backward(first):
-            y = lax.dot_general(
-                vs_ref[(i + 1) % 2], z_ref[(i + 1) % 2], (((0,), (0,)), ((), ())), preferred_element_type=F32
+                for s in range(per_half):
+                    source = per_half * ((offset + h) % 2) + s
+                    win_ref[part * h + high * s : part * h + high * (s + 1)] = pieces_ref[source, h // 2]
+
+        def columns(x):
+            return [x[:, 128 * j : 128 * (j + 1)] for j in range(lanes)]
+
+        def project(k):
+            v = v_ref[sub * k : sub * (k + 1)]
+            x_refs[k][...] = jnp.dot(v, win_ref[...], preferred_element_type=F32).astype(BF16)
+
+        def row_sums(k):
+            at = slice(sub * k, sub * (k + 1))
+            x = columns(x_refs[k][...])
+
+            def total(a):
+                partial = sum(p * q for p, q in zip(x, columns(a)))
+                return lax.dot_general(ones, partial, (((1,), (1,)), ((), ())), preferred_element_type=F32)
+
+            return [total(v_ref[at])] + [total(g_ref[q, at]) for q in range(3)]
+
+        def back(k):
+            v = kept_ref[...] if k < 0 else v_ref[sub * k : sub * (k + 1)]
+            y_ref[...] += lax.dot_general(
+                v, z_refs[k][...], (((0,), (0,)), ((), ())), preferred_element_type=F32
             )
-            y_ref[...] = y if first else y_ref[...] + y
-
-        @pl.when(i == 0)
+
+        def weigh(k, sums):
+            at = slice(sub * k, sub * (k + 1))
+            n = sums[0] * (1.0 / functions)
+            g = [q * (2.0 / functions) for q in sums[1:]]
+            dens_ref[:, at] = n[0:1]
+            c0, ck = pointwise(n, g, jnp.broadcast_to(w_ref[tile : tile + 1, at], (8, sub)), points)
+            factors = [c.astype(BF16) for c in [c0] + ck]
+            for b in range(sub // 128):
+                r = slice(sub * k + 128 * b, sub * k + 128 * (b + 1))
+                f = [jnp.concatenate([c[:, 128 * b : 128 * (b + 1)]] * 16, axis=0).T for c in factors]
+                arrays = [v_ref[r]] + [g_ref[q, r] for q in range(3)]
+                for j in range(lanes):
+                    t = [u * a[:, 128 * j : 128 * (j + 1)] for u, a in zip(f, arrays)]
+                    z_refs[k][128 * b : 128 * (b + 1), 128 * j : 128 * (j + 1)] = (t[0] + t[1]) + (t[2] + t[3])
+
+        project(0)
+        for k in range(parts):
+            if k + 1 < parts:
+                project(k + 1)
+            sums = row_sums(k)
+            back(k - 1)
+            weigh(k, sums)
+        kept_ref[...] = v_ref[sub * (parts - 1) :]
+
+        @pl.when(i == count - 1)
         def _():
-            forward()
-
-        @pl.when(i == 1)
-        def _():
-            backward(True)
-            forward()
-
-        @pl.when((i > 1) & (i < count))
-        def _():
-            backward(False)
-            forward()
-
-        @pl.when(i == count)
-        def _():
-            backward(False)
+            back(-1)
             y = y_ref[...]
             y_ref[...] = y + y.T
             for to in range(cols):
@@ -535,36 +545,30 @@
                 start = 2 * part + high * (to % per_half)
                 term_ref[to, 1] = y_ref[start : start + high].astype(BF16)
 
-    def chunk(i):
-        return jnp.minimum(i, count - 1)
-
     return pl.pallas_call(
         body,
-        grid=(count + 1,),
+        grid=(count,),
         in_specs=[
             SMEM_SPEC,
-            pl.BlockSpec((None, rows, functions), lambda i: (tile, chunk(i), 0)),
-            pl.BlockSpec((3, None, rows, functions), lambda i: (0, tile, chunk(i), 0)),
-            pl.BlockSpec((None, blocks, 128), lambda i: (tile, chunk(i), 0)),
-            pl.BlockSpec(pieces.shape, lambda i: (0, 0, 0, 0)),
+            pl.BlockSpec((None, rows, functions), lambda i: (tile, i, 0)),
+            pl.BlockSpec((3, None, rows, functions), lambda i: (0, tile, i, 0)),
+            pl.BlockSpec((tiles, rows), lambda i: (0, i)),
+            VMEM_SPEC,
         ],
-        out_specs=[
-            pl.BlockSpec((blocks, 128), lambda i: (chunk(i), 0)),
-            pl.BlockSpec(pieces.shape, lambda i: (0, 0, 0, 0)),
-        ],
+        out_specs=[pl.BlockSpec((1, rows), lambda i: (0, i)), VMEM_SPEC],
         out_shape=[
-            jax.ShapeDtypeStruct((points // 128, 128), F32),
+            jax.ShapeDtypeStruct((1, points), F32),
             jax.ShapeDtypeStruct(pieces.shape, BF16),
         ],
         scratch_shapes=[
             pltpu.VMEM((functions, functions), BF16),
-            pltpu.VMEM((2, rows, functions), BF16),
-            pltpu.VMEM((2, rows, functions), BF16),
+            pltpu.VMEM((sub, functions), BF16),
             pltpu.VMEM((functions, functions), F32),
-        ],
+        ]
+        + [pltpu.VMEM((sub, functions), BF16)] * (2 * parts),
         compiler_params=pltpu.CompilerParams(vmem_limit_bytes=48 << 20),
         name="tile",
-    )(step, basis_values, basis_grads, quadrature, pieces)
+    )(step, basis_values, basis_grads, weights, pieces)
 
 
 def add_terms(terms, steps, place, block):
@@ -599,7 +603,7 @@
 
     edge = ((2, high, block), BF16)
     return small_call(
-        body, "add_terms", [steps, place], list(terms),
+        body, [steps, place], list(terms),
         [((cols, 3, high, block), F32), edge, edge], [((2, cols + 2, high, 2 * block), F32)],
     )
 
@@ -608,7 +612,7 @@
     rows, cols = lax.axis_size("row"), lax.axis_size("col")
     row_index, col_index = lax.axis_index("row"), lax.axis_index("col")
     block = density.shape[3]
-    tiles, points, functions = basis_values.shape
+    tiles, _, functions = basis_values.shape
     chain = Chain(rows, cols)
     step_here = chain.step(row_index, col_index)
     place = (step_here % cols).astype(jnp.int32).reshape(1)
@@ -628,19 +632,19 @@
             out = purify_next(own, near, kept_row, block, last, steps, cols)
         own, sends = out[0], out[1:]
     pieces = [lax.ppermute(p, BOTH, chain.to_slices(turn)) for turn, p in enumerate(out)]
-    purified, down, up, steps = join_slices(pieces, slice_here, tiles, block)
+    purified, down, up = join_slices(pieces, slice_here, block)
+    steps = read_steps(pieces[0], cols, tiles)
     above = shifted_2(down, "row", 1)
     below = shifted_2(up, "row", -1)
     sent = pack_windows(purified, above, below, steps, slice_here, tiles, functions)
 
-    quadrature = weights.reshape(tiles, points // 128, 128)
     densities, terms = [], []
     for tile in range(tiles):
         window = lax.all_to_all(sent[tile], "col", 0, 0, tiled=True)
         dens, term = tile_call(
-            tile, basis_values, basis_grads, quadrature, window, steps_here[tile : tile + 1]
+            tile, basis_values, basis_grads, weights, window, steps_here[tile : tile + 1]
         )
-        densities.append(dens.reshape(points))
+        densities.append(dens)
         terms.append(lax.all_to_all(term, "col", 0, 0, tiled=True))
     mine, to_above, to_below = add_terms(terms, steps, slice_here, block)
     from_below = shifted_2(to_above, "row", -1).astype(F32)
@@ -649,7 +653,7 @@
     last = jnp.pad(from_below[None], ((cols - 1, 0), (1, 0), (0, 0), (0, 0)))
     summed = mine + first + last
     xc_matrix = jnp.where(kept, jnp.pad(summed, ((0, 0), (1, 1), (0, 0), (0, 0))), 0.0)
-    return purified, xc_matrix, jnp.stack(densities)
+    return purified, xc_matrix, jnp.concatenate(densities)
 
 
 def on_device(density, pattern, windows, basis_values, basis_grads, weights):
@@ -661,6 +665,7 @@
         and 2 * functions == 3 * block
         and functions // 3 % density.shape[2] == 0
         and cols <= NOTE
+        and (5 * density.shape[2]) % NOTE == 0
         and 2 * cols + 2 <= 256
         and basis_values.shape[1] % 1024 == 0
     )

time: 178 us -> 168 us (0.944)
  Pallas kernels: 36.5 us -> 29.4 us
  local copies, waits for them, and re-layouts: 5.49 us -> 3.45 us
    pallas_call x3, Pallas kernels: 30.2 us -> 22.3 us  [the longest x2 21.5 us: tile_call(): pl.pallas_call(body, grid=(count,), in_specs=[SMEM_SPEC, pl.BlockSpec((No...]
    unnamed x23 -> x10, local copies, waits for them, and re-layouts: 4.89 us -> 2.86 us
    pallas_call x6 -> x7, Pallas kernels: 6.25 us -> 7.14 us  [small_call(): pl.pallas_call(body, in_specs=[SMEM_SPEC] * len(scalars) + [VMEM_SPEC] *...]
  transfers between devices with their start and end apart: 23 -> 23, of which waited for: 13 -> 14; matrix products, arithmetic and copies ran while one was open for 1% -> 1% of each run, Pallas kernels for 16% -> 13%
where the time goes in v5:
time: 168 us; the launch traced here: 166 us
  starting transfers between devices  66.8 us (40%)
  waiting for transfers between devices  46.7 us (28%)
  Pallas kernels  29.4 us (18%)
  blocking collectives  16 us (10%)
  local copies, waits for them, and re-layouts  3.45 us (2%)
  other arithmetic  2.57 us (2%)
    ppermute x8, starting transfers between devices, exchange_rows(): got[by] = lax.ppermute(send, BOTH, chain.shift(by))  28.5 us
    pallas_call x2, Pallas kernels, tile_call(): pl.pallas_call(body, grid=(count,), in_specs=[SMEM_SPEC, pl.BlockSpec((No...  21.5 us
    ppermute x8, waiting for transfers between devices, exchange_rows(): got[by] = lax.ppermute(send, BOTH, chain.shift(by))  16.7 us
    all_to_all x1, blocking collectives, by_block_rows(): window = lax.all_to_all(sent[tile], 'col', 0, 0, tiled=True)  16 us
    ppermute x4, starting transfers between devices, shifted_2(): return lax.ppermute(value, axis, pairs)  15.1 us
    all_to_all x2, waiting for transfers between devices, by_block_rows(): terms.append(lax.all_to_all(term, 'col', 0, 0, tiled=True))  12.7 us
    ppermute x4, waiting for transfers between devices, by_block_rows(): lax.ppermute(p, BOTH, chain.to_slices(turn))  8.59 us
    all_to_all x2, starting transfers between devices, by_block_rows(): terms.append(lax.all_to_all(term, 'col', 0, 0, tiled=True))  7.95 us
  transfers between devices with their start and end apart: 23, of which 14 were waited for; matrix products, arithmetic and copies ran while one was open for 1% of the time, Pallas kernels for 13%

profile of v5, /device:TPU:3, one launch (start us, length us, event | category | flops | bytes accessed | tf_op | source)
XLA Modules:
  0.0 165.9 jit_solution(2400038338872696765)
XLA Ops:
  0.6 0.7 broadcast_subtract_fusion.steps_ref
  1.3 1.1 copy-done
  2.4 0.7 copy-done.3
  3.1 0.6 shard_map.85
  3.7 3.8 %collective-permute-start = (bf16[208,256]{1,0:T(8,128)(2,1)S(1)}, bf16[208,256]{1,0:T(8,128)(2,1)S(1)}, u32[]{:S(2)}, u32[]{:S(2)}) collective-permute-start(bf16[208,256]{1,0:T(8,128)(2,1)S(1)} %get-tuple-element.33), channel_id=1, source_target_pairs={{0,0},{1,4},{2,1},{3,5},{4,2},{5,6},{6,3},{7,7},{8,11},{9,15},{10,... | collective-permute-start | bytes 319496 | tf_op jit(solution)/shard_map/ppermute | solution.py:623
  7.6 2.5 %collective-permute-start.2 = (bf16[208,256]{1,0:T(8,128)(2,1)S(1)}, bf16[208,256]{1,0:T(8,128)(2,1)S(1)}, u32[]{:S(2)}, u32[]{:S(2)}) collective-permute-start(bf16[208,256]{1,0:T(8,128)(2,1)S(1)} %get-tuple-element.35), channel_id=1, source_target_pairs={{0,1},{1,5},{2,0},{3,4},{4,3},{5,7},{6,2},{7,6},{8,10},{9,14},{10,... | collective-permute-start | bytes 319496 | tf_op jit(solution)/shard_map/ppermute | solution.py:623
  10.0 0.7 collective-permute-start.3
  11.4 1.6 collective-permute-done.1.refs_1_
  13.0 1.0 collective-permute-done.2.refs_2_
  14.1 4.9 %collective-permute-start.6 = (bf16[3,256,256]{2,1,0:T(8,128)(2,1)S(1)}, bf16[3,256,256]{2,1,0:T(8,128)(2,1)S(1)}, u32[]{:S(2)}, u32[]{:S(2)}) collective-permute-start(bf16[3,256,256]{2,1,0:T(8,128)(2,1)S(1)} %get-tuple-element.38.own_ref), channel_id=1, source_target_pairs={{4,0},{1,4},{5,1},{2,5},{6,2},{3,6},{7,3},{11,7},{15,11},{10,15},{... | collective-permute-start | bytes 1179656 | tf_op jit(solution)/shard_map/ppermute | solution.py:286
  19.0 4.8 %collective-permute-start.4 = (bf16[2,256,256]{2,1,0:T(8,128)(2,1)S(1)}, bf16[2,256,256]{2,1,0:T(8,128)(2,1)S(1)}, u32[]{:S(2)}, u32[]{:S(2)}) collective-permute-start(bf16[2,256,256]{2,1,0:T(8,128)(2,1)S(1)} %get-tuple-element.39), channel_id=1, source_target_pairs={{0,4},{4,1},{1,5},{5,2},{2,6},{6,3},{3,7},{7,11},{11,15},{15,10},{... | collective-permute-start | bytes 786440 | tf_op jit(solution)/shard_map/ppermute | solution.py:286
  23.9 4.2 %collective-permute-start.5 = (bf16[2,256,256]{2,1,0:T(8,128)(2,1)S(1)}, bf16[2,256,256]{2,1,0:T(8,128)(2,1)S(1)}, u32[]{:S(2)}, u32[]{:S(2)}) collective-permute-start(bf16[2,256,256]{2,1,0:T(8,128)(2,1)S(1)} %get-tuple-element.39), channel_id=1, source_target_pairs={{0,1},{4,5},{1,2},{5,6},{2,3},{6,7},{3,11},{7,15},{11,10},{15,14},... | collective-permute-start | bytes 786440 | tf_op jit(solution)/shard_map/ppermute | solution.py:286
  28.1 1.9 %collective-permute-start.7 = (bf16[2,256,256]{2,1,0:T(8,128)(2,1)S(1)}, bf16[2,256,256]{2,1,0:T(8,128)(2,1)S(1)}, u32[]{:S(2)}, u32[]{:S(2)}) collective-permute-start(bf16[2,256,256]{2,1,0:T(8,128)(2,1)S(1)} %get-tuple-element.40), channel_id=1, source_target_pairs={{1,0},{5,4},{2,1},{6,5},{3,2},{7,6},{11,3},{15,7},{10,11},{14,15},... | collective-permute-start | bytes 786440 | tf_op jit(solution)/shard_map/ppermute | solution.py:286
  30.0 4.2 %collective-permute-done.5.m2 = bf16[2,256,256]{2,1,0:T(8,128)(2,1)S(1)} collective-permute-done((bf16[2,256,256]{2,1,0:T(8,128)(2,1)S(1)}, bf16[2,256,256]{2,1,0:T(8,128)(2,1)S(1)}, u32[]{:S(2)}, u32[]{:S(2)}) %collective-permute-start.5) | collective-permute-done | bytes 262176 | tf_op jit(solution)/shard_map/ppermute | solution.py:286
  34.2 4.2 %collective-permute-done.7.p2 = bf16[2,256,256]{2,1,0:T(8,128)(2,1)S(1)} collective-permute-done((bf16[2,256,256]{2,1,0:T(8,128)(2,1)S(1)}, bf16[2,256,256]{2,1,0:T(8,128)(2,1)S(1)}, u32[]{:S(2)}, u32[]{:S(2)}) %collective-permute-start.7) | collective-permute-done | bytes 262176 | tf_op jit(solution)/shard_map/ppermute | solution.py:286
  38.4 1.5 shard_map.87
  40.0 2.1 %collective-permute-start.10 = (bf16[4,256,256]{2,1,0:T(8,128)(2,1)S(1)}, bf16[4,256,256]{2,1,0:T(8,128)(2,1)S(1)}, u32[]{:S(2)}, u32[]{:S(2)}) collective-permute-start(bf16[4,256,256]{2,1,0:T(8,128)(2,1)S(1)} %get-tuple-element.44), channel_id=1, source_target_pairs={{4,0},{1,4},{5,1},{2,5},{6,2},{3,6},{7,3},{11,7},{15,11},{10,15},{... | collective-permute-start | bytes 1572872 | tf_op jit(solution)/shard_map/ppermute | solution.py:286
  42.1 4.4 %collective-permute-start.8 = (bf16[4,256,256]{2,1,0:T(8,128)(2,1)S(1)}, bf16[4,256,256]{2,1,0:T(8,128)(2,1)S(1)}, u32[]{:S(2)}, u32[]{:S(2)}) collective-permute-start(bf16[4,256,256]{2,1,0:T(8,128)(2,1)S(1)} %get-tuple-element.42), channel_id=1, source_target_pairs={{0,4},{4,1},{1,5},{5,2},{2,6},{6,3},{3,7},{7,11},{11,15},{15,10},{... | collective-permute-start | bytes 1572872 | tf_op jit(solution)/shard_map/ppermute | solution.py:286
  46.4 1.9 %collective-permute-start.11 = (bf16[3,256,256]{2,1,0:T(8,128)(2,1)S(1)}, bf16[3,256,256]{2,1,0:T(8,128)(2,1)S(1)}, u32[]{:S(2)}, u32[]{:S(2)}) collective-permute-start(bf16[3,256,256]{2,1,0:T(8,128)(2,1)S(1)} %get-tuple-element.45), channel_id=1, source_target_pairs={{1,0},{5,4},{2,1},{6,5},{3,2},{7,6},{11,3},{15,7},{10,11},{14,15},... | collective-permute-start | bytes 1179656 | tf_op jit(solution)/shard_map/ppermute | solution.py:286
  48.4 4.3 %collective-permute-start.9 = (bf16[3,256,256]{2,1,0:T(8,128)(2,1)S(1)}, bf16[3,256,256]{2,1,0:T(8,128)(2,1)S(1)}, u32[]{:S(2)}, u32[]{:S(2)}) collective-permute-start(bf16[3,256,256]{2,1,0:T(8,128)(2,1)S(1)} %get-tuple-element.43), channel_id=1, source_target_pairs={{0,1},{4,5},{1,2},{5,6},{2,3},{6,7},{3,11},{7,15},{11,10},{15,14},... | collective-permute-start | bytes 1179656 | tf_op jit(solution)/shard_map/ppermute | solution.py:286
  52.6 7.2 %collective-permute-done.11.refs_6_ = bf16[3,256,256]{2,1,0:T(8,128)(2,1)S(1)} collective-permute-done((bf16[3,256,256]{2,1,0:T(8,128)(2,1)S(1)}, bf16[3,256,256]{2,1,0:T(8,128)(2,1)S(1)}, u32[]{:S(2)}, u32[]{:S(2)}) %collective-permute-start.11) | collective-permute-done | bytes 393248 | tf_op jit(solution)/shard_map/ppermute | solution.py:286
  59.8 1.2 collective-permute-done.9.refs_4_
  61.0 1.5 shard_map.88
  62.5 2.7 %collective-permute-start.12 = (bf16[336,256]{1,0:T(8,128)(2,1)S(1)}, bf16[336,256]{1,0:T(8,128)(2,1)S(1)}, u32[]{:S(2)}, u32[]{:S(2)}) collective-permute-start(bf16[336,256]{1,0:T(8,128)(2,1)S(1)} %get-tuple-element.47), channel_id=1, source_target_pairs={{0,0},{4,1},{1,2},{5,3},{2,4},{6,5},{3,6},{7,7},{11,8},{15,9},{10,... | collective-permute-start | bytes 516104 | tf_op jit(solution)/shard_map/ppermute | solution.py:634
  65.7 1.1 collective-permute-start.14
  66.8 0.7 collective-permute-start.15
  67.4 7.8 %collective-permute-done.12.refs_0_.piece_ref = bf16[336,256]{1,0:T(8,128)(2,1)S(1)} collective-permute-done((bf16[336,256]{1,0:T(8,128)(2,1)S(1)}, bf16[336,256]{1,0:T(8,128)(2,1)S(1)}, u32[]{:S(2)}, u32[]{:S(2)}) %collective-permute-start.12) | collective-permute-done | bytes 172064 | tf_op jit(solution)/shard_map/ppermute | solution.py:634
  76.0 0.9 shard_map.89
  76.9 5.3 %collective-permute-start.16 = (bf16[2,64,256]{2,1,0:T(8,128)(2,1)S(1)}, bf16[2,64,256]{2,1,0:T(8,128)(2,1)S(1)}, u32[]{:S(2)}, u32[]{:S(2)}) collective-permute-start(bf16[2,64,256]{2,1,0:T(8,128)(2,1)S(1)} %get-tuple-element.52), channel_id=1, source_target_pairs={{0,4},{4,8},{8,12},{12,16},{16,20},{20,24},{24,28},{1,5},{5,9},{9,... | collective-permute-start | bytes 196616 | tf_op jit(solution)/shard_map/ppermute | solution.py:36
  82.2 4.7 %collective-permute-start.17 = (bf16[2,64,256]{2,1,0:T(8,128)(2,1)S(1)}, bf16[2,64,256]{2,1,0:T(8,128)(2,1)S(1)}, u32[]{:S(2)}, u32[]{:S(2)}) collective-permute-start(bf16[2,64,256]{2,1,0:T(8,128)(2,1)S(1)} %get-tuple-element.53), channel_id=1, source_target_pairs={{4,0},{8,4},{12,8},{16,12},{20,16},{24,20},{28,24},{5,1},{9,5},{13... | collective-permute-start | bytes 196616 | tf_op jit(solution)/shard_map/ppermute | solution.py:36
  86.9 0.8 read_steps.1.steps_ref
  87.7 1.7 %collective-permute-done.17.below_ref = bf16[2,64,256]{2,1,0:T(8,128)(2,1)S(1)} collective-permute-done((bf16[2,64,256]{2,1,0:T(8,128)(2,1)S(1)}, bf16[2,64,256]{2,1,0:T(8,128)(2,1)S(1)}, u32[]{:S(2)}, u32[]{:S(2)}) %collective-permute-start.17) | collective-permute-done | bytes 65568 | tf_op jit(solution)/shard_map/ppermute | solution.py:36
  89.4 1.1 copy-done.1
  90.5 1.5 shard_map.90
  91.9 16.0 %all_to_all.20.pieces_ref = bf16[4,2,64,384]{3,2,1,0:T(8,128)(2,1)S(1)} all-to-all(bf16[4,2,64,384]{3,2,1,0:T(8,128)(2,1)S(1)} %get-tuple-element.56), channel_id=1, replica_groups=mesh['row'=8,'col'=4] {'col'}, dimensions={0} | all-to-all | bytes 786432 | tf_op jit(solution)/shard_map/all_to_all | solution.py:643
  107.9 3.5 %all-to-all-start = ((bf16[4,2,64,384]{3,2,1,0:T(8,128)(2,1)}), bf16[4,2,64,384]{3,2,1,0:T(8,128)(2,1)S(1)}, u32[]{:S(2)}, u32[]{:S(2)}) async-start(bf16[4,2,64,384]{3,2,1,0:T(8,128)(2,1)} %get-tuple-element.54), calls=%async_computation | async-start | bytes 786432 | tf_op jit(solution)/shard_map/all_to_all | solution.py:643
  112.0 10.7 %tile.3 = (f32[1,4096]{1,0:T(1,128)S(1)}, bf16[4,2,64,384]{3,2,1,0:T(8,128)(2,1)}) custom-call(s32[1]{0:T(128)} %get-tuple-element.63.step_ref, bf16[2,4096,384]{2,1,0:T(8,128)(2,1)} %v_ref.3, bf16[3,2,4096,384]{3,2,1,0:T(8,128)(2,1)} %g_ref.3, f32[2,4096]{1,0:T(2,128)S(1)} %copy-done.2, bf16[4,2,64,384]{3,2,1,0:T(8,128)(2,1)S(1)} %all_to_all.20.pieces_ref), custom_call_target="tpu_custom_call" | custom-call | tf_op jit(solution)/shard_map/tile/pallas_call | solution.py:548
  122.7 4.5 %all-to-all-start.3 = ((bf16[4,2,64,384]{3,2,1,0:T(8,128)(2,1)}), bf16[4,2,64,384]{3,2,1,0:T(8,128)(2,1)S(1)}, u32[]{:S(2)}, u32[]{:S(2)}) async-start(bf16[4,2,64,384]{3,2,1,0:T(8,128)(2,1)} %get-tuple-element.57), calls=%async_computation.3 | async-start | bytes 786432 | tf_op jit(solution)/shard_map/all_to_all | solution.py:648
  127.2 10.8 %tile.2 = (f32[1,4096]{1,0:T(1,128)S(1)}, bf16[4,2,64,384]{3,2,1,0:T(8,128)(2,1)}) custom-call(s32[1]{0:T(128)} %get-tuple-element.64.step_ref, bf16[2,4096,384]{2,1,0:T(8,128)(2,1)} %v_ref.3, bf16[3,2,4096,384]{3,2,1,0:T(8,128)(2,1)} %g_ref.3, f32[2,4096]{1,0:T(2,128)S(1)} %copy-done.2, bf16[4,2,64,384]{3,2,1,0:T(8,128)(2,1)S(1)} %all-to-all-done.pieces_ref), custom_call_target="tpu_custom_call" | custom-call | tf_op jit(solution)/shard_map/tile/pallas_call | solution.py:548
  138.0 1.4 all-to-all-done.3.refs_1_
  139.4 3.5 %all-to-all-start.1 = ((bf16[4,2,64,384]{3,2,1,0:T(8,128)(2,1)}), bf16[4,2,64,384]{3,2,1,0:T(8,128)(2,1)S(1)}, u32[]{:S(2)}, u32[]{:S(2)}) async-start(bf16[4,2,64,384]{3,2,1,0:T(8,128)(2,1)} %get-tuple-element.55), calls=%async_computation.1 | async-start | bytes 786432 | tf_op jit(solution)/shard_map/all_to_all | solution.py:648
  142.9 11.3 %all-to-all-done.1.refs_0_ = bf16[4,2,64,384]{3,2,1,0:T(8,128)(2,1)S(1)} async-done(((bf16[4,2,64,384]{3,2,1,0:T(8,128)(2,1)}), bf16[4,2,64,384]{3,2,1,0:T(8,128)(2,1)S(1)}, u32[]{:S(2)}, u32[]{:S(2)}) %all-to-all-start.1) | async-done | bytes 393248 | tf_op jit(solution)/shard_map/all_to_all | solution.py:648
  154.2 1.0 shard_map.91
  155.2 2.9 %collective-permute-start.18 = (bf16[2,64,256]{2,1,0:T(8,128)(2,1)S(1)}, bf16[2,64,256]{2,1,0:T(8,128)(2,1)S(1)}, u32[]{:S(2)}, u32[]{:S(2)}) collective-permute-start(bf16[2,64,256]{2,1,0:T(8,128)(2,1)S(1)} %get-tuple-element.59), channel_id=1, source_target_pairs={{0,4},{4,8},{8,12},{12,16},{16,20},{20,24},{24,28},{1,5},{5,9},{9,... | collective-permute-start | bytes 196616 | tf_op jit(solution)/shard_map/ppermute | solution.py:36
  158.1 2.1 %collective-permute-start.19 = (bf16[2,64,256]{2,1,0:T(8,128)(2,1)S(1)}, bf16[2,64,256]{2,1,0:T(8,128)(2,1)S(1)}, u32[]{:S(2)}, u32[]{:S(2)}) collective-permute-start(bf16[2,64,256]{2,1,0:T(8,128)(2,1)S(1)} %get-tuple-element.60), channel_id=1, source_target_pairs={{4,0},{8,4},{12,8},{16,12},{20,16},{24,20},{28,24},{5,1},{9,5},{13... | collective-permute-start | bytes 196616 | tf_op jit(solution)/shard_map/ppermute | solution.py:36
  160.3 0.6 pad_maximum_fusion
  160.9 3.7 %collective-permute-done.19 = bf16[2,64,256]{2,1,0:T(8,128)(2,1)S(1)} collective-permute-done((bf16[2,64,256]{2,1,0:T(8,128)(2,1)S(1)}, bf16[2,64,256]{2,1,0:T(8,128)(2,1)S(1)}, u32[]{:S(2)}, u32[]{:S(2)}) %collective-permute-start.19) | collective-permute-done | bytes 65568 | tf_op jit(solution)/shard_map/ppermute | solution.py:36
  164.7 1.2 pad_select_fusion
  (25 shorter events, 2.7 us)
Async XLA Ops:
  1.3 1.1 copy-start
  2.4 0.7 copy-start.3
  3.7 7.7 %collective-permute-start = (bf16[208,256]{1,0:T(8,128)(2,1)S(1)}, bf16[208,256]{1,0:T(8,128)(2,1)S(1)}, u32[]{:S(2)}, u32[]{:S(2)}) collective-permute-start(bf16[208,256]{1,0:T(8,128)(2,1)S(1)} %get-tuple-element.33), channel_id=1, source_target_pairs={{0,0},{1,4},{2,1},{3,5},{4,2},{5,6},{6,3},{7,7},{8,11},{9,15},{10,... | collective-permute-start | bytes 319496 | tf_op jit(solution)/shard_map/ppermute | solution.py:623
  7.5 5.5 %collective-permute-start.1 = (bf16[208,256]{1,0:T(8,128)(2,1)S(1)}, bf16[208,256]{1,0:T(8,128)(2,1)S(1)}, u32[]{:S(2)}, u32[]{:S(2)}) collective-permute-start(bf16[208,256]{1,0:T(8,128)(2,1)S(1)} %get-tuple-element.34), channel_id=1, source_target_pairs={{0,4},{1,0},{2,5},{3,1},{4,6},{5,2},{6,7},{7,3},{8,15},{9,11},{10,... | collective-permute-start | bytes 319496 | tf_op jit(solution)/shard_map/ppermute | solution.py:623
  7.6 6.5 %collective-permute-start.2 = (bf16[208,256]{1,0:T(8,128)(2,1)S(1)}, bf16[208,256]{1,0:T(8,128)(2,1)S(1)}, u32[]{:S(2)}, u32[]{:S(2)}) collective-permute-start(bf16[208,256]{1,0:T(8,128)(2,1)S(1)} %get-tuple-element.35), channel_id=1, source_target_pairs={{0,1},{1,5},{2,0},{3,4},{4,3},{5,7},{6,2},{7,6},{8,10},{9,14},{10,... | collective-permute-start | bytes 319496 | tf_op jit(solution)/shard_map/ppermute | solution.py:623
  10.0 4.0 %collective-permute-start.3 = (bf16[208,256]{1,0:T(8,128)(2,1)S(1)}, bf16[208,256]{1,0:T(8,128)(2,1)S(1)}, u32[]{:S(2)}, u32[]{:S(2)}) collective-permute-start(bf16[208,256]{1,0:T(8,128)(2,1)S(1)} %get-tuple-element.36), channel_id=1, source_target_pairs={{0,5},{1,1},{2,4},{3,0},{4,7},{5,3},{6,6},{7,2},{8,14},{9,10},{10,... | collective-permute-start | bytes 319496 | tf_op jit(solution)/shard_map/ppermute | solution.py:623
  14.1 24.3 %collective-permute-start.6 = (bf16[3,256,256]{2,1,0:T(8,128)(2,1)S(1)}, bf16[3,256,256]{2,1,0:T(8,128)(2,1)S(1)}, u32[]{:S(2)}, u32[]{:S(2)}) collective-permute-start(bf16[3,256,256]{2,1,0:T(8,128)(2,1)S(1)} %get-tuple-element.38.own_ref), channel_id=1, source_target_pairs={{4,0},{1,4},{5,1},{2,5},{6,2},{3,6},{7,3},{11,7},{15,11},{10,15},{... | collective-permute-start | bytes 1179656 | tf_op jit(solution)/shard_map/ppermute | solution.py:286
  19.0 11.0 %collective-permute-start.4 = (bf16[2,256,256]{2,1,0:T(8,128)(2,1)S(1)}, bf16[2,256,256]{2,1,0:T(8,128)(2,1)S(1)}, u32[]{:S(2)}, u32[]{:S(2)}) collective-permute-start(bf16[2,256,256]{2,1,0:T(8,128)(2,1)S(1)} %get-tuple-element.39), channel_id=1, source_target_pairs={{0,4},{4,1},{1,5},{5,2},{2,6},{6,3},{3,7},{7,11},{11,15},{15,10},{... | collective-permute-start | bytes 786440 | tf_op jit(solution)/shard_map/ppermute | solution.py:286
  23.9 10.3 %collective-permute-start.5 = (bf16[2,256,256]{2,1,0:T(8,128)(2,1)S(1)}, bf16[2,256,256]{2,1,0:T(8,128)(2,1)S(1)}, u32[]{:S(2)}, u32[]{:S(2)}) collective-permute-start(bf16[2,256,256]{2,1,0:T(8,128)(2,1)S(1)} %get-tuple-element.39), channel_id=1, source_target_pairs={{0,1},{4,5},{1,2},{5,6},{2,3},{6,7},{3,11},{7,15},{11,10},{15,14},... | collective-permute-start | bytes 786440 | tf_op jit(solution)/shard_map/ppermute | solution.py:286
  28.1 10.3 %collective-permute-start.7 = (bf16[2,256,256]{2,1,0:T(8,128)(2,1)S(1)}, bf16[2,256,256]{2,1,0:T(8,128)(2,1)S(1)}, u32[]{:S(2)}, u32[]{:S(2)}) collective-permute-start(bf16[2,256,256]{2,1,0:T(8,128)(2,1)S(1)} %get-tuple-element.40), channel_id=1, source_target_pairs={{1,0},{5,4},{2,1},{6,5},{3,2},{7,6},{11,3},{15,7},{10,11},{14,15},... | collective-permute-start | bytes 786440 | tf_op jit(solution)/shard_map/ppermute | solution.py:286
  40.0 21.0 %collective-permute-start.10 = (bf16[4,256,256]{2,1,0:T(8,128)(2,1)S(1)}, bf16[4,256,256]{2,1,0:T(8,128)(2,1)S(1)}, u32[]{:S(2)}, u32[]{:S(2)}) collective-permute-start(bf16[4,256,256]{2,1,0:T(8,128)(2,1)S(1)} %get-tuple-element.44), channel_id=1, source_target_pairs={{4,0},{1,4},{5,1},{2,5},{6,2},{3,6},{7,3},{11,7},{15,11},{10,15},{... | collective-permute-start | bytes 1572872 | tf_op jit(solution)/shard_map/ppermute | solution.py:286
  42.1 18.9 %collective-permute-start.8 = (bf16[4,256,256]{2,1,0:T(8,128)(2,1)S(1)}, bf16[4,256,256]{2,1,0:T(8,128)(2,1)S(1)}, u32[]{:S(2)}, u32[]{:S(2)}) collective-permute-start(bf16[4,256,256]{2,1,0:T(8,128)(2,1)S(1)} %get-tuple-element.42), channel_id=1, source_target_pairs={{0,4},{4,1},{1,5},{5,2},{2,6},{6,3},{3,7},{7,11},{11,15},{15,10},{... | collective-permute-start | bytes 1572872 | tf_op jit(solution)/shard_map/ppermute | solution.py:286
  46.4 13.4 %collective-permute-start.11 = (bf16[3,256,256]{2,1,0:T(8,128)(2,1)S(1)}, bf16[3,256,256]{2,1,0:T(8,128)(2,1)S(1)}, u32[]{:S(2)}, u32[]{:S(2)}) collective-permute-start(bf16[3,256,256]{2,1,0:T(8,128)(2,1)S(1)} %get-tuple-element.45), channel_id=1, source_target_pairs={{1,0},{5,4},{2,1},{6,5},{3,2},{7,6},{11,3},{15,7},{10,11},{14,15},... | collective-permute-start | bytes 1179656 | tf_op jit(solution)/shard_map/ppermute | solution.py:286
  48.4 12.6 %collective-permute-start.9 = (bf16[3,256,256]{2,1,0:T(8,128)(2,1)S(1)}, bf16[3,256,256]{2,1,0:T(8,128)(2,1)S(1)}, u32[]{:S(2)}, u32[]{:S(2)}) collective-permute-start(bf16[3,256,256]{2,1,0:T(8,128)(2,1)S(1)} %get-tuple-element.43), channel_id=1, source_target_pairs={{0,1},{4,5},{1,2},{5,6},{2,3},{6,7},{3,11},{7,15},{11,10},{15,14},... | collective-permute-start | bytes 1179656 | tf_op jit(solution)/shard_map/ppermute | solution.py:286
  62.5 12.7 %collective-permute-start.12 = (bf16[336,256]{1,0:T(8,128)(2,1)S(1)}, bf16[336,256]{1,0:T(8,128)(2,1)S(1)}, u32[]{:S(2)}, u32[]{:S(2)}) collective-permute-start(bf16[336,256]{1,0:T(8,128)(2,1)S(1)} %get-tuple-element.47), channel_id=1, source_target_pairs={{0,0},{4,1},{1,2},{5,3},{2,4},{6,5},{3,6},{7,7},{11,8},{15,9},{10,... | collective-permute-start | bytes 516104 | tf_op jit(solution)/shard_map/ppermute | solution.py:634
  65.2 10.4 %collective-permute-start.13 = (bf16[336,256]{1,0:T(8,128)(2,1)S(1)}, bf16[336,256]{1,0:T(8,128)(2,1)S(1)}, u32[]{:S(2)}, u32[]{:S(2)}) collective-permute-start(bf16[336,256]{1,0:T(8,128)(2,1)S(1)} %get-tuple-element.48), channel_id=1, source_target_pairs={{4,0},{0,1},{5,2},{1,3},{6,4},{2,5},{7,6},{3,7},{15,8},{11,9},{14,... | collective-permute-start | bytes 516104 | tf_op jit(solution)/shard_map/ppermute | solution.py:634
  65.7 10.4 %collective-permute-start.14 = (bf16[336,256]{1,0:T(8,128)(2,1)S(1)}, bf16[336,256]{1,0:T(8,128)(2,1)S(1)}, u32[]{:S(2)}, u32[]{:S(2)}) collective-permute-start(bf16[336,256]{1,0:T(8,128)(2,1)S(1)} %get-tuple-element.49), channel_id=1, source_target_pairs={{1,0},{5,1},{0,2},{4,3},{3,4},{7,5},{2,6},{6,7},{10,8},{14,9},{11,... | collective-permute-start | bytes 516104 | tf_op jit(solution)/shard_map/ppermute | solution.py:634
  66.8 9.3 %collective-permute-start.15 = (bf16[336,256]{1,0:T(8,128)(2,1)S(1)}, bf16[336,256]{1,0:T(8,128)(2,1)S(1)}, u32[]{:S(2)}, u32[]{:S(2)}) collective-permute-start(bf16[336,256]{1,0:T(8,128)(2,1)S(1)} %get-tuple-element.50), channel_id=1, source_target_pairs={{5,0},{1,1},{4,2},{0,3},{7,4},{3,5},{6,6},{2,7},{14,8},{10,9},{15,... | collective-permute-start | bytes 516104 | tf_op jit(solution)/shard_map/ppermute | solution.py:634
  76.9 35.0 %copy-start.2 = (f32[2,4096]{1,0:T(2,128)S(1)}, f32[2,4096]{1,0:T(2,128)}, u32[]{:S(2)}) copy-start(f32[2,4096]{1,0:T(2,128)} %w_ref.3) | copy-start | bytes 98308
  76.9 10.8 %collective-permute-start.16 = (bf16[2,64,256]{2,1,0:T(8,128)(2,1)S(1)}, bf16[2,64,256]{2,1,0:T(8,128)(2,1)S(1)}, u32[]{:S(2)}, u32[]{:S(2)}) collective-permute-start(bf16[2,64,256]{2,1,0:T(8,128)(2,1)S(1)} %get-tuple-element.52), channel_id=1, source_target_pairs={{0,4},{4,8},{8,12},{12,16},{16,20},{20,24},{24,28},{1,5},{5,9},{9,... | collective-permute-start | bytes 196616 | tf_op jit(solution)/shard_map/ppermute | solution.py:36
  82.2 7.2 %collective-permute-start.17 = (bf16[2,64,256]{2,1,0:T(8,128)(2,1)S(1)}, bf16[2,64,256]{2,1,0:T(8,128)(2,1)S(1)}, u32[]{:S(2)}, u32[]{:S(2)}) collective-permute-start(bf16[2,64,256]{2,1,0:T(8,128)(2,1)S(1)} %get-tuple-element.53), channel_id=1, source_target_pairs={{4,0},{8,4},{12,8},{16,12},{20,16},{24,20},{28,24},{5,1},{9,5},{13... | collective-permute-start | bytes 196616 | tf_op jit(solution)/shard_map/ppermute | solution.py:36
  89.4 1.1 copy-start.1
  107.9 14.8 %all-to-all-start = ((bf16[4,2,64,384]{3,2,1,0:T(8,128)(2,1)}), bf16[4,2,64,384]{3,2,1,0:T(8,128)(2,1)S(1)}, u32[]{:S(2)}, u32[]{:S(2)}) async-start(bf16[4,2,64,384]{3,2,1,0:T(8,128)(2,1)} %get-tuple-element.54), calls=%async_computation | async-start | bytes 786432 | tf_op jit(solution)/shard_map/all_to_all | solution.py:643
  122.7 16.7 %all-to-all-start.3 = ((bf16[4,2,64,384]{3,2,1,0:T(8,128)(2,1)}), bf16[4,2,64,384]{3,2,1,0:T(8,128)(2,1)S(1)}, u32[]{:S(2)}, u32[]{:S(2)}) async-start(bf16[4,2,64,384]{3,2,1,0:T(8,128)(2,1)} %get-tuple-element.57), calls=%async_computation.3 | async-start | bytes 786432 | tf_op jit(solution)/shard_map/all_to_all | solution.py:648
  127.2 15.7 %copy-start.4 = (s32[4,5]{1,0:T(4,128)S(1)}, s32[4,5]{1,0:T(4,128)}, u32[]{:S(2)}) copy-start(s32[4,5]{1,0:T(4,128)} %pattern_ref.1) | copy-start | bytes 244
  139.4 14.8 %all-to-all-start.1 = ((bf16[4,2,64,384]{3,2,1,0:T(8,128)(2,1)}), bf16[4,2,64,384]{3,2,1,0:T(8,128)(2,1)S(1)}, u32[]{:S(2)}, u32[]{:S(2)}) async-start(bf16[4,2,64,384]{3,2,1,0:T(8,128)(2,1)} %get-tuple-element.55), calls=%async_computation.1 | async-start | bytes 786432 | tf_op jit(solution)/shard_map/all_to_all | solution.py:648
  155.2 5.7 %collective-permute-start.18 = (bf16[2,64,256]{2,1,0:T(8,128)(2,1)S(1)}, bf16[2,64,256]{2,1,0:T(8,128)(2,1)S(1)}, u32[]{:S(2)}, u32[]{:S(2)}) collective-permute-start(bf16[2,64,256]{2,1,0:T(8,128)(2,1)S(1)} %get-tuple-element.59), channel_id=1, source_target_pairs={{0,4},{4,8},{8,12},{12,16},{16,20},{20,24},{24,28},{1,5},{5,9},{9,... | collective-permute-start | bytes 196616 | tf_op jit(solution)/shard_map/ppermute | solution.py:36
  158.1 6.5 %collective-permute-start.19 = (bf16[2,64,256]{2,1,0:T(8,128)(2,1)S(1)}, bf16[2,64,256]{2,1,0:T(8,128)(2,1)S(1)}, u32[]{:S(2)}, u32[]{:S(2)}) collective-permute-start(bf16[2,64,256]{2,1,0:T(8,128)(2,1)S(1)} %get-tuple-element.60), channel_id=1, source_target_pairs={{4,0},{8,4},{12,8},{16,12},{20,16},{24,20},{28,24},{5,1},{9,5},{13... | collective-permute-start | bytes 196616 | tf_op jit(solution)/shard_map/ppermute | solution.py:36

commit v6 on v5

--- a/solution.py
+++ b/solution.py
@@ -200,44 +200,63 @@
     def to_slices(self, turn):
         return [(b, a) for a, b in self.to_rows(turn)]
 
+    def edges(self, turn):
+        pairs, other = [], (turn + self.cols // 2) % self.cols
+        for row in range(self.rows):
+            if row + 1 < self.rows:
+                pairs.append((self.device((row + 1) * self.cols - 1), (row + 1) * self.cols + turn))
+            if row > 0:
+                pairs.append((self.device(row * self.cols), (row - 1) * self.cols + other))
+        return pairs
+
     def shift(self, by):
         return [(self.device(i), self.device(i + by)) for i in range(self.count) if 0 <= i + by < self.count]
 
 
 SMALL = 12 << 20
+LARGE = 60 << 20
 BOTH = ("row", "col")
 VMEM_SPEC = pl.BlockSpec(memory_space=pltpu.VMEM)
 SMEM_SPEC = pl.BlockSpec(memory_space=pltpu.SMEM)
 
 
-def small_call(body, scalars, arrays, outs, scratch=()):
+def with_ids(body, before):
+    def wrapped(*refs):
+        ids = [ref[0] for ref in refs[before : before + 3]]
+        return body(*refs[:before], ids, *refs[before + 3 :])
+
+    return wrapped
+
+
+def small_call(body, scalars, arrays, outs, scratch=(), limit=SMALL):
     return pl.pallas_call(
-        body,
+        with_ids(body, len(scalars) - 3) if len(scalars) >= 3 else body,
         in_specs=[SMEM_SPEC] * len(scalars) + [VMEM_SPEC] * len(arrays),
         out_specs=[VMEM_SPEC] * len(outs),
         out_shape=[jax.ShapeDtypeStruct(s, d) for s, d in outs],
         scratch_shapes=[pltpu.VMEM(s, d) for s, d in scratch],
-        compiler_params=pltpu.CompilerParams(vmem_limit_bytes=SMALL),
+        compiler_params=pltpu.CompilerParams(vmem_limit_bytes=limit),
     )(*scalars, *arrays)
 
 
 HELD = (0, 2, 3)
 SENDS = ((1, 5), (2, 5), (0, 4), (0, 3))
 NOTE = 16
+PLACE, SLICE, BASE = range(3)
 
 
 def grid_of(shape, axis):
     return lax.broadcasted_iota(jnp.int32, shape, axis)
 
 
-def prepare(density, pattern, steps, slice_here):
+def prepare(density, pattern, windows, ids):
     cols, _, high, block = density.shape
-    tiles = steps.shape[0]
-
-    def body(pattern_ref, steps_ref, slice_ref, density_ref, *outs):
+    tiles = windows.shape[0]
+
+    def body(pattern_ref, windows_ref, ids, density_ref, *outs):
         row, lane = grid_of((NOTE, block), 0), grid_of((NOTE, block), 1)
         for turn in range(cols):
-            j = mixed(slice_ref[0], turn, cols)
+            j = mixed(ids[SLICE], turn, cols)
             for k, d in enumerate(HELD):
                 value = density_ref[j, d]
                 outs[turn][k * high : (k + 1) * high] = jnp.where(pattern_ref[j, d] > 0, value, jnp.zeros_like(value))
@@ -245,23 +264,23 @@
             for d in range(5):
                 note = jnp.where((row == 0) & (lane == d), (pattern_ref[j, d] > 0).astype(F32), note)
             for tile in range(tiles):
-                note = jnp.where((row == 1) & (lane == tile), steps_ref[tile].astype(F32), note)
+                note = jnp.where((row == 1) & (lane == tile), (windows_ref[tile] - ids[BASE]).astype(F32), note)
             outs[turn][3 * high :] = note.astype(BF16)
 
     shapes = [((3 * high + NOTE, block), BF16)] * cols
-    return small_call(body, [pattern, steps, slice_here], [density], shapes)
+    return small_call(body, [pattern, windows, *ids], [density], shapes, limit=LARGE)
 
 
 def join_rows(pieces, place, block):
     cols = len(pieces)
     high = block // cols
 
-    def body(place_ref, *refs):
+    def body(ids, *refs):
         ins, (own, up, down, kept, steps) = refs[:cols], refs[cols:]
         row = grid_of((NOTE, block), 0)
         total = jnp.zeros((NOTE, block), F32)
         for turn in range(cols):
-            source = mixed(place_ref[0], turn, cols)
+            source = mixed(ids[PLACE], turn, cols)
             at = pl.ds(pl.multiple_of(source * high, high), high)
             for k in range(3):
                 value = ins[turn][k * high : (k + 1) * high]
@@ -277,7 +296,7 @@
 
     two, three = ((2, block, block), BF16), ((3, block, block), BF16)
     shapes = [three, two, two, ((NOTE, block), F32), ((NOTE, block), BF16)]
-    return small_call(body, [place], pieces, shapes)
+    return small_call(body, place, pieces, shapes)
 
 
 def exchange_rows(chain, sends):
@@ -340,7 +359,7 @@
     last = place is not None
 
     def body(*refs):
-        place_ref, refs = (refs[0], refs[1:]) if last else (None, refs)
+        ids, refs = (refs[0], refs[1:]) if last else (None, refs)
         kept_ref, own_ref, m1, m2, p1, p2, steps_ref = refs[:7]
         outs, (square, whole_ref) = refs[7:-2], refs[-2:]
 
@@ -359,34 +378,47 @@
         purify_math(kept_ref, lambda o: own_ref[o + 2], right, square, store)
         if last:
             for turn in range(cols):
-                at = pl.ds(pl.multiple_of(mixed(place_ref[0], turn, cols) * high, high), high)
+                at = pl.ds(pl.multiple_of(mixed(ids[PLACE], turn, cols) * high, high), high)
                 for d in range(5):
                     outs[turn][d * high : (d + 1) * high] = whole_ref[d, at]
                 outs[turn][5 * high :] = steps_ref[...]
 
+                @pl.when(ids[PLACE] == cols - 1)
+                def _():
+                    outs[cols + turn][...] = whole_ref[2:4, high * turn : high * (turn + 1)]
+
+                @pl.when(ids[PLACE] == 0)
+                def _():
+                    other = (turn + cols // 2) % cols
+                    outs[cols + turn][...] = whole_ref[1:3, high * other : high * (other + 1)]
+
     whole = ((5, block, block), BF16)
     if last:
-        shapes = [((5 * high + NOTE, block), BF16)] * cols
+        shapes = [((5 * high + NOTE, block), BF16)] * cols + [((2, high, block), BF16)] * cols
     else:
         shapes = [whole] + [((top - low, block, block), BF16) for low, top in SENDS]
-    return small_call(body, [place] if last else [], [kept, own] + list(near) + [steps], shapes, [whole, whole])
-
-
-def join_slices(pieces, place, block):
+    return small_call(body, place if last else [], [kept, own] + list(near) + [steps], shapes, [whole, whole])
+
+
+def join_slices(pieces, ids, block, after):
     cols = len(pieces)
     high = block // cols
 
-    def body(place_ref, *refs):
-        ins, (out, down, up) = refs[:cols], refs[cols:]
+    def body(ids, *refs):
+        ins, out = refs[:cols], refs[-1]
         for turn in range(cols):
-            j = mixed(place_ref[0], turn, cols)
+            j = mixed(ids[SLICE], turn, cols)
             for d in range(5):
                 out[j, d] = ins[turn][d * high : (d + 1) * high]
-        down[...] = out[cols - 1, 2:4]
-        up[...] = out[0, 1:3]
-
-    edge = ((2, high, block), BF16)
-    return small_call(body, [place], pieces, [((cols, 5, high, block), BF16), edge, edge])
+
+    return pl.pallas_call(
+        with_ids(body, 0),
+        in_specs=[SMEM_SPEC] * 3 + [VMEM_SPEC] * cols + [pl.BlockSpec(memory_space=pl.ANY)],
+        out_specs=VMEM_SPEC,
+        out_shape=jax.ShapeDtypeStruct((cols, 5, high, block), BF16),
+        compiler_params=pltpu.CompilerParams(vmem_limit_bytes=SMALL),
+        name="join_slices",
+    )(*ids, *pieces, after)
 
 
 def read_steps(piece, cols, tiles):
@@ -417,24 +449,33 @@
     return offset, first, (offset + first) // 2
 
 
-def pack_windows(purified, above, below, steps, place, tiles, functions):
-    cols, _, high, block = purified.shape
+def pack_windows(pieces, edges, steps, ids, block, tiles, functions):
+    cols = len(pieces)
+    high = block // cols
     part = functions // 3
     per_half = part // high
 
-    def body(steps_ref, place_ref, pur, above_ref, below_ref, *refs):
-        outs, near = refs[:-1], refs[-1]
-        for low in range(2):
-            for b in range(2):
-                at = slice(b * block, (b + 1) * block)
-                for row in range(cols + 2):
-                    if low == 0 and row == 0:
-                        near[low, row, :, at] = above_ref[b]
-                    elif low == 1 and row == cols + 1:
-                        near[low, row, :, at] = below_ref[b]
-                    elif 0 < row < cols + 1:
-                        near[low, row, :, at] = pur[row - 1, 2 - low + b]
-        half = place_ref[0] // per_half
+    def body(steps_ref, ids, *refs):
+        ins, edge_ins, outs, near = refs[:cols], refs[cols : 2 * cols], refs[2 * cols : -1], refs[-1]
+        here = ids[SLICE]
+        for turn in range(cols):
+            row = mixed(here, turn, cols) + 1
+            for low in range(2):
+                for b in range(2):
+                    d = 2 - low + b
+                    near[low, row, :, b * block : (b + 1) * block] = ins[turn][d * high : (d + 1) * high]
+
+            @pl.when(here == turn)
+            def _():
+                for b in range(2):
+                    near[0, 0, :, b * block : (b + 1) * block] = edge_ins[turn][b]
+
+            @pl.when(here == (turn + cols // 2) % cols)
+            def _():
+                for b in range(2):
+                    near[1, cols + 1, :, b * block : (b + 1) * block] = edge_ins[turn][b]
+
+        half = here // per_half
         for to in range(cols):
             for tile in range(tiles):
                 step = steps_ref[to, tile]
@@ -444,7 +485,7 @@
                 outs[tile][to, 1] = near[1, step // 2 + 1, :, lanes]
 
     return small_call(
-        body, [steps, place], [purified, above, below],
+        body, [steps, *ids], list(pieces) + list(edges),
         [((cols, 2, high, functions), BF16)] * tiles, [((2, cols + 2, high, 2 * block), BF16)],
     )
 
@@ -463,16 +504,17 @@
     return 0.5 * by_density * scaled, [2.0 * by_gradient * scaled * gk for gk in g]
 
 
-def tile_call(tile, basis_values, basis_grads, weights, pieces, step, rows=1024, parts=2):
+def tile_call(tile, basis_values, basis_grads, weights, pieces, windows, ids, rows=1024, parts=2):
     tiles, points, functions = basis_values.shape
     cols, _, high, _ = pieces.shape
     part = functions // 3
     per_half = part // high
     count, sub, lanes = points // rows, rows // parts, functions // 128
 
-    def body(step_ref, v_ref, g_ref, w_ref, pieces_ref, dens_ref, term_ref, win_ref, kept_ref, y_ref, *bufs):
+    def body(windows_ref, ids, v_ref, g_ref, w_ref, pieces_ref, dens_ref, term_ref, win_ref, kept_ref, y_ref, *bufs):
         i = pl.program_id(0)
-        offset = step_ref[0] % 2
+        step = windows_ref[tile] - ids[BASE]
+        offset = step % 2
         x_refs, z_refs = bufs[:parts], bufs[parts:]
         ones = jnp.ones((8, 128), BF16)
 
@@ -539,16 +581,19 @@
             y = y_ref[...]
             y_ref[...] = y + y.T
             for to in range(cols):
-                _, first, _ = slot_of(step_ref[0], to // per_half)
+                _, first, _ = slot_of(step, to // per_half)
                 start = pl.multiple_of(part * first + high * (to % per_half), high)
                 term_ref[to, 0] = y_ref[pl.ds(start, high)].astype(BF16)
                 start = 2 * part + high * (to % per_half)
                 term_ref[to, 1] = y_ref[start : start + high].astype(BF16)
 
     return pl.pallas_call(
-        body,
+        with_ids(body, 1),
         grid=(count,),
         in_specs=[
+            SMEM_SPEC,
+            SMEM_SPEC,
+            SMEM_SPEC,
             SMEM_SPEC,
             pl.BlockSpec((None, rows, functions), lambda i: (tile, i, 0)),
             pl.BlockSpec((3, None, rows, functions), lambda i: (0, tile, i, 0)),
@@ -568,7 +613,7 @@
         + [pltpu.VMEM((sub, functions), BF16)] * (2 * parts),
         compiler_params=pltpu.CompilerParams(vmem_limit_bytes=48 << 20),
         name="tile",
-    )(step, basis_values, basis_grads, weights, pieces)
+    )(windows, *ids, basis_values, basis_grads, weights, pieces)
 
 
 def add_terms(terms, steps, place, block):
@@ -577,10 +622,10 @@
     part = functions // 3
     per_half = part // high
 
-    def body(steps_ref, place_ref, *refs):
+    def body(steps_ref, ids, *refs):
         ins, (own, to_above, to_below, total) = refs[:tiles], refs[tiles:]
         total[...] = jnp.zeros(total.shape, F32)
-        half = place_ref[0] // per_half
+        half = ids[SLICE] // per_half
         for source in range(cols):
             for tile in range(tiles):
                 step = steps_ref[source, tile]
@@ -603,7 +648,7 @@
 
     edge = ((2, high, block), BF16)
     return small_call(
-        body, [steps, place], list(terms),
+        body, [steps, *place], list(terms),
         [((cols, 3, high, block), F32), edge, edge], [((2, cols + 2, high, 2 * block), F32)],
     )
 
@@ -614,45 +659,41 @@
     block = density.shape[3]
     tiles, _, functions = basis_values.shape
     chain = Chain(rows, cols)
-    step_here = chain.step(row_index, col_index)
-    place = (step_here % cols).astype(jnp.int32).reshape(1)
-    slice_here = col_index.astype(jnp.int32).reshape(1)
-    kept = (pattern > 0)[:, :, None, None]
-    steps_here = (windows - (2 * cols * row_index - 2)).astype(jnp.int32)
-    pieces = prepare(density, pattern, steps_here, slice_here)
+    place = chain.step(row_index, col_index) % cols
+    ids = [x.astype(jnp.int32).reshape(1) for x in (place, col_index, 2 * cols * row_index - 2)]
+    pieces = prepare(density, pattern, windows, ids)
     pieces = [lax.ppermute(p, BOTH, chain.to_rows(turn)) for turn, p in enumerate(pieces)]
-    own, up, down, kept_row, steps = join_rows(pieces, place, block)
+    own, up, down, kept_row, steps = join_rows(pieces, ids, block)
     sends = (up, up, own, down)
     for iteration in range(ITERS):
         near = exchange_rows(chain, sends)
-        last = place if iteration == ITERS - 1 else None
         if iteration == 0:
             out = purify_first(own, near, kept_row, block)
         else:
-            out = purify_next(own, near, kept_row, block, last, steps, cols)
+            out = purify_next(own, near, kept_row, block, ids if iteration == ITERS - 1 else None, steps, cols)
         own, sends = out[0], out[1:]
-    pieces = [lax.ppermute(p, BOTH, chain.to_slices(turn)) for turn, p in enumerate(out)]
-    purified, down, up = join_slices(pieces, slice_here, block)
+    pieces, edges = [], []
+    for turn in range(cols):
+        pieces.append(lax.ppermute(out[turn], BOTH, chain.to_slices(turn)))
+    for turn in range(cols):
+        edges.append(lax.ppermute(out[cols + turn], BOTH, chain.edges(turn)))
     steps = read_steps(pieces[0], cols, tiles)
-    above = shifted_2(down, "row", 1)
-    below = shifted_2(up, "row", -1)
-    sent = pack_windows(purified, above, below, steps, slice_here, tiles, functions)
+    sent = pack_windows(pieces, edges, steps, ids, block, tiles, functions)
+    purified = join_slices(pieces, ids, block, sent[0])
 
     densities, terms = [], []
     for tile in range(tiles):
         window = lax.all_to_all(sent[tile], "col", 0, 0, tiled=True)
-        dens, term = tile_call(
-            tile, basis_values, basis_grads, weights, window, steps_here[tile : tile + 1]
-        )
+        dens, term = tile_call(tile, basis_values, basis_grads, weights, window, windows, ids)
         densities.append(dens)
         terms.append(lax.all_to_all(term, "col", 0, 0, tiled=True))
-    mine, to_above, to_below = add_terms(terms, steps, slice_here, block)
+    mine, to_above, to_below = add_terms(terms, steps, ids, block)
     from_below = shifted_2(to_above, "row", -1).astype(F32)
     from_above = shifted_2(to_below, "row", 1).astype(F32)
     first = jnp.pad(from_above[None], ((0, cols - 1), (0, 1), (0, 0), (0, 0)))
     last = jnp.pad(from_below[None], ((cols - 1, 0), (1, 0), (0, 0), (0, 0)))
-    summed = mine + first + last
-    xc_matrix = jnp.where(kept, jnp.pad(summed, ((0, 0), (1, 1), (0, 0), (0, 0))), 0.0)
+    summed = jnp.pad(mine + first + last, ((0, 0), (1, 1), (0, 0), (0, 0)))
+    xc_matrix = jnp.where((pattern > 0)[:, :, None, None], summed, 0.0)
     return purified, xc_matrix, jnp.concatenate(densities)
 
 
@@ -662,6 +703,7 @@
     fits = (
         band_rows == cols
         and rows % 2 == 0
+        and cols > 1
         and 2 * functions == 3 * block
         and functions // 3 % density.shape[2] == 0
         and cols <= NOTE

time: 168 us -> 163 us (0.970)
  waiting for transfers between devices: 46.7 us -> 37 us
  starting transfers between devices: 66.8 us -> 74.6 us
  local copies, waits for them, and re-layouts: 3.45 us -> 0.02 us
  blocking collectives: 16 us -> 18 us
    ppermute x4 -> x8, starting transfers between devices: 4.91 us -> 15.2 us  [the longest x4 10.1 us: by_block_rows(): edges.append(lax.ppermute(out[cols + turn], BOTH, chain.edges(turn)))]
    all_to_all x2, waiting for transfers between devices: 12.7 us -> 6.85 us  [by_block_rows(): terms.append(lax.all_to_all(term, 'col', 0, 0, tiled=True))]
    ppermute x4 -> x2, starting transfers between devices: 15.1 us -> 10.7 us  [shifted_2(): return lax.ppermute(value, axis, pairs)]
    unnamed x10 -> x6, local copies, waits for them, and re-layouts: 2.86 us -> 0.02 us
    all_to_all x1, blocking collectives: 16 us -> 18 us  [by_block_rows(): window = lax.all_to_all(sent[tile], 'col', 0, 0, tiled=True)]
    ppermute x4 -> x8, waiting for transfers between devices: 8.59 us -> 6.86 us  [the longest x4 6.85 us: by_block_rows(): edges.append(lax.ppermute(out[cols + turn], BOTH, chain.edges(turn)))]
    ppermute x4 -> x2, waiting for transfers between devices: 5.35 us -> 3.91 us  [shifted_2(): return lax.ppermute(value, axis, pairs)]
  transfers between devices with their start and end apart: 23 -> 25, of which waited for: 14 -> 11; matrix products, arithmetic and copies ran while one was open for 1% -> 0% of each run, Pallas kernels for 13% -> 14%
where the time goes in v6:
time: 163 us; the launch traced here: 162 us
  starting transfers between devices  74.6 us (46%)
  waiting for transfers between devices  37 us (23%)
  Pallas kernels  29.7 us (18%)
  blocking collectives  18 us (11%)
  other arithmetic  1.9 us (1%)
    ppermute x8, starting transfers between devices, exchange_rows(): got[by] = lax.ppermute(send, BOTH, chain.shift(by))  28.5 us
    pallas_call x2, Pallas kernels, tile_call(): pl.pallas_call(with_ids(body, 1), grid=(count,), in_specs=[SMEM_SPEC, SME...  20.4 us
    all_to_all x1, blocking collectives, by_block_rows(): window = lax.all_to_all(sent[tile], 'col', 0, 0, tiled=True)  18 us
    ppermute x8, waiting for transfers between devices, exchange_rows(): got[by] = lax.ppermute(send, BOTH, chain.shift(by))  16.7 us
    ppermute x2, starting transfers between devices, shifted_2(): return lax.ppermute(value, axis, pairs)  10.7 us
    ppermute x4, starting transfers between devices, by_block_rows(): edges.append(lax.ppermute(out[cols + turn], BOTH, chain.edges(turn)))  10.1 us
    all_to_all x2, starting transfers between devices, by_block_rows(): terms.append(lax.all_to_all(term, 'col', 0, 0, tiled=True))  9 us
    ppermute x4, starting transfers between devices, by_block_rows(): lax.ppermute(p, BOTH, chain.to_rows(turn))  7.84 us
  transfers between devices with their start and end apart: 25, of which 11 were waited for; matrix products, arithmetic and copies ran while one was open for 0% of the time, Pallas kernels for 14%

profile of v6, /device:TPU:3, one launch (start us, length us, event | category | flops | bytes accessed | tf_op | source)
XLA Modules:
  0.0 162.2 jit_solution(9635425148261350555)
XLA Ops:
  0.7 1.9 %shard_map.85 = (bf16[208,256]{1,0:T(8,128)(2,1)}, bf16[208,256]{1,0:T(8,128)(2,1)}, bf16[208,256]{1,0:T(8,128)(2,1)}, bf16[208,256]{1,0:T(8,128)(2,1)}) custom-call(s32[4,5]{1,0:T(4,128)} %refs_0_.3, s32[2]{0:T(128)} %refs_0_.5, s32[1]{0:T(128)} %bitcast.refs_2_.refs_0_.refs_1_, s32[1]{0:T(128)} %bitcast.1.refs_3_.refs_1_.refs_2_, ...), custom_call_target="tpu_custom_call" | custom-call | tf_op jit(solution)/shard_map/pallas_call | solution.py:232
  2.6 3.8 %collective-permute-start = (bf16[208,256]{1,0:T(8,128)(2,1)}, bf16[208,256]{1,0:T(8,128)(2,1)S(1)}, u32[]{:S(2)}, u32[]{:S(2)}) collective-permute-start(bf16[208,256]{1,0:T(8,128)(2,1)} %get-tuple-element.34), channel_id=1, source_target_pairs={{0,0},{1,4},{2,1},{3,5},{4,2},{5,6},{6,3},{7,7},{8,11},{9,15},{10,... | collective-permute-start | bytes 319496 | tf_op jit(solution)/shard_map/ppermute | solution.py:665
  6.3 0.1 collective-permute-start.1
  6.4 2.5 %collective-permute-start.2 = (bf16[208,256]{1,0:T(8,128)(2,1)}, bf16[208,256]{1,0:T(8,128)(2,1)S(1)}, u32[]{:S(2)}, u32[]{:S(2)}) collective-permute-start(bf16[208,256]{1,0:T(8,128)(2,1)} %get-tuple-element.36), channel_id=1, source_target_pairs={{0,1},{1,5},{2,0},{3,4},{4,3},{5,7},{6,2},{7,6},{8,10},{9,14},{10,... | collective-permute-start | bytes 319496 | tf_op jit(solution)/shard_map/ppermute | solution.py:665
  8.9 1.5 collective-permute-start.3
  10.5 1.6 collective-permute-done.1.refs_4_
  12.1 1.0 collective-permute-done.2.refs_5_
  13.2 4.9 %collective-permute-start.6 = (bf16[3,256,256]{2,1,0:T(8,128)(2,1)S(1)}, bf16[3,256,256]{2,1,0:T(8,128)(2,1)S(1)}, u32[]{:S(2)}, u32[]{:S(2)}) collective-permute-start(bf16[3,256,256]{2,1,0:T(8,128)(2,1)S(1)} %get-tuple-element.39.own_ref), channel_id=1, source_target_pairs={{4,0},{1,4},{5,1},{2,5},{6,2},{3,6},{7,3},{11,7},{15,11},{10,15},{... | collective-permute-start | bytes 1179656 | tf_op jit(solution)/shard_map/ppermute | solution.py:305
  18.1 4.8 %collective-permute-start.4 = (bf16[2,256,256]{2,1,0:T(8,128)(2,1)S(1)}, bf16[2,256,256]{2,1,0:T(8,128)(2,1)S(1)}, u32[]{:S(2)}, u32[]{:S(2)}) collective-permute-start(bf16[2,256,256]{2,1,0:T(8,128)(2,1)S(1)} %get-tuple-element.40), channel_id=1, source_target_pairs={{0,4},{4,1},{1,5},{5,2},{2,6},{6,3},{3,7},{7,11},{11,15},{15,10},{... | collective-permute-start | bytes 786440 | tf_op jit(solution)/shard_map/ppermute | solution.py:305
  23.0 4.2 %collective-permute-start.5 = (bf16[2,256,256]{2,1,0:T(8,128)(2,1)S(1)}, bf16[2,256,256]{2,1,0:T(8,128)(2,1)S(1)}, u32[]{:S(2)}, u32[]{:S(2)}) collective-permute-start(bf16[2,256,256]{2,1,0:T(8,128)(2,1)S(1)} %get-tuple-element.40), channel_id=1, source_target_pairs={{0,1},{4,5},{1,2},{5,6},{2,3},{6,7},{3,11},{7,15},{11,10},{15,14},... | collective-permute-start | bytes 786440 | tf_op jit(solution)/shard_map/ppermute | solution.py:305
  27.1 1.9 %collective-permute-start.7 = (bf16[2,256,256]{2,1,0:T(8,128)(2,1)S(1)}, bf16[2,256,256]{2,1,0:T(8,128)(2,1)S(1)}, u32[]{:S(2)}, u32[]{:S(2)}) collective-permute-start(bf16[2,256,256]{2,1,0:T(8,128)(2,1)S(1)} %get-tuple-element.41), channel_id=1, source_target_pairs={{1,0},{5,4},{2,1},{6,5},{3,2},{7,6},{11,3},{15,7},{10,11},{14,15},... | collective-permute-start | bytes 786440 | tf_op jit(solution)/shard_map/ppermute | solution.py:305
  29.1 4.2 %collective-permute-done.5.m2 = bf16[2,256,256]{2,1,0:T(8,128)(2,1)S(1)} collective-permute-done((bf16[2,256,256]{2,1,0:T(8,128)(2,1)S(1)}, bf16[2,256,256]{2,1,0:T(8,128)(2,1)S(1)}, u32[]{:S(2)}, u32[]{:S(2)}) %collective-permute-start.5) | collective-permute-done | bytes 262176 | tf_op jit(solution)/shard_map/ppermute | solution.py:305
  33.3 4.2 %collective-permute-done.7.p2 = bf16[2,256,256]{2,1,0:T(8,128)(2,1)S(1)} collective-permute-done((bf16[2,256,256]{2,1,0:T(8,128)(2,1)S(1)}, bf16[2,256,256]{2,1,0:T(8,128)(2,1)S(1)}, u32[]{:S(2)}, u32[]{:S(2)}) %collective-permute-start.7) | collective-permute-done | bytes 262176 | tf_op jit(solution)/shard_map/ppermute | solution.py:305
  37.5 1.5 shard_map.87
  39.0 2.1 %collective-permute-start.10 = (bf16[4,256,256]{2,1,0:T(8,128)(2,1)S(1)}, bf16[4,256,256]{2,1,0:T(8,128)(2,1)S(1)}, u32[]{:S(2)}, u32[]{:S(2)}) collective-permute-start(bf16[4,256,256]{2,1,0:T(8,128)(2,1)S(1)} %get-tuple-element.45), channel_id=1, source_target_pairs={{4,0},{1,4},{5,1},{2,5},{6,2},{3,6},{7,3},{11,7},{15,11},{10,15},{... | collective-permute-start | bytes 1572872 | tf_op jit(solution)/shard_map/ppermute | solution.py:305
  41.1 4.4 %collective-permute-start.8 = (bf16[4,256,256]{2,1,0:T(8,128)(2,1)S(1)}, bf16[4,256,256]{2,1,0:T(8,128)(2,1)S(1)}, u32[]{:S(2)}, u32[]{:S(2)}) collective-permute-start(bf16[4,256,256]{2,1,0:T(8,128)(2,1)S(1)} %get-tuple-element.43), channel_id=1, source_target_pairs={{0,4},{4,1},{1,5},{5,2},{2,6},{6,3},{3,7},{7,11},{11,15},{15,10},{... | collective-permute-start | bytes 1572872 | tf_op jit(solution)/shard_map/ppermute | solution.py:305
  45.5 1.9 %collective-permute-start.11 = (bf16[3,256,256]{2,1,0:T(8,128)(2,1)S(1)}, bf16[3,256,256]{2,1,0:T(8,128)(2,1)S(1)}, u32[]{:S(2)}, u32[]{:S(2)}) collective-permute-start(bf16[3,256,256]{2,1,0:T(8,128)(2,1)S(1)} %get-tuple-element.46), channel_id=1, source_target_pairs={{1,0},{5,4},{2,1},{6,5},{3,2},{7,6},{11,3},{15,7},{10,11},{14,15},... | collective-permute-start | bytes 1179656 | tf_op jit(solution)/shard_map/ppermute | solution.py:305
  47.4 4.3 %collective-permute-start.9 = (bf16[3,256,256]{2,1,0:T(8,128)(2,1)S(1)}, bf16[3,256,256]{2,1,0:T(8,128)(2,1)S(1)}, u32[]{:S(2)}, u32[]{:S(2)}) collective-permute-start(bf16[3,256,256]{2,1,0:T(8,128)(2,1)S(1)} %get-tuple-element.44), channel_id=1, source_target_pairs={{0,1},{4,5},{1,2},{5,6},{2,3},{6,7},{3,11},{7,15},{11,10},{15,14},... | collective-permute-start | bytes 1179656 | tf_op jit(solution)/shard_map/ppermute | solution.py:305
  51.7 7.2 %collective-permute-done.11.refs_8_ = bf16[3,256,256]{2,1,0:T(8,128)(2,1)S(1)} collective-permute-done((bf16[3,256,256]{2,1,0:T(8,128)(2,1)S(1)}, bf16[3,256,256]{2,1,0:T(8,128)(2,1)S(1)}, u32[]{:S(2)}, u32[]{:S(2)}) %collective-permute-start.11) | collective-permute-done | bytes 393248 | tf_op jit(solution)/shard_map/ppermute | solution.py:305
  58.9 1.2 collective-permute-done.9.refs_6_
  60.0 1.6 shard_map.88
  61.6 2.7 %collective-permute-start.12 = (bf16[336,256]{1,0:T(8,128)(2,1)S(1)}, bf16[336,256]{1,0:T(8,128)(2,1)S(1)}, u32[]{:S(2)}, u32[]{:S(2)}) collective-permute-start(bf16[336,256]{1,0:T(8,128)(2,1)S(1)} %get-tuple-element.48), channel_id=1, source_target_pairs={{0,0},{4,1},{1,2},{5,3},{2,4},{6,5},{3,6},{7,7},{11,8},{15,9},{10,... | collective-permute-start | bytes 516104 | tf_op jit(solution)/shard_map/ppermute | solution.py:677
  64.3 2.6 %collective-permute-start.16 = (bf16[2,64,256]{2,1,0:T(8,128)(2,1)S(1)}, bf16[2,64,256]{2,1,0:T(8,128)(2,1)S(1)}, u32[]{:S(2)}, u32[]{:S(2)}) collective-permute-start(bf16[2,64,256]{2,1,0:T(8,128)(2,1)S(1)} %get-tuple-element.52), channel_id=1, source_target_pairs={{5,4},{7,8},{2,2},{14,12},{11,6},{12,16},{9,10},{21,20},{16,14},{2... | collective-permute-start | bytes 196616 | tf_op jit(solution)/shard_map/ppermute | solution.py:679
  67.0 1.7 %collective-permute-start.13 = (bf16[336,256]{1,0:T(8,128)(2,1)S(1)}, bf16[336,256]{1,0:T(8,128)(2,1)S(1)}, u32[]{:S(2)}, u32[]{:S(2)}) collective-permute-start(bf16[336,256]{1,0:T(8,128)(2,1)S(1)} %get-tuple-element.49), channel_id=1, source_target_pairs={{4,0},{0,1},{5,2},{1,3},{6,4},{2,5},{7,6},{3,7},{15,8},{11,9},{14,... | collective-permute-start | bytes 516104 | tf_op jit(solution)/shard_map/ppermute | solution.py:677
  68.7 0.7 collective-permute-start.15
  69.3 5.0 %collective-permute-done.16.refs_8_ = bf16[2,64,256]{2,1,0:T(8,128)(2,1)S(1)} collective-permute-done((bf16[2,64,256]{2,1,0:T(8,128)(2,1)S(1)}, bf16[2,64,256]{2,1,0:T(8,128)(2,1)S(1)}, u32[]{:S(2)}, u32[]{:S(2)}) %collective-permute-start.16) | collective-permute-done | bytes 65568 | tf_op jit(solution)/shard_map/ppermute | solution.py:679
  74.3 1.3 collective-permute-start.17
  75.6 1.3 collective-permute-done.17.refs_9_
  76.9 3.6 %collective-permute-start.18 = (bf16[2,64,256]{2,1,0:T(8,128)(2,1)S(1)}, bf16[2,64,256]{2,1,0:T(8,128)(2,1)S(1)}, u32[]{:S(2)}, u32[]{:S(2)}) collective-permute-start(bf16[2,64,256]{2,1,0:T(8,128)(2,1)S(1)} %get-tuple-element.54), channel_id=1, source_target_pairs={{5,6},{7,10},{2,0},{14,14},{11,4},{12,18},{9,8},{21,22},{16,12},{2... | collective-permute-start | bytes 196616 | tf_op jit(solution)/shard_map/ppermute | solution.py:679
  80.6 2.5 %collective-permute-start.19 = (bf16[2,64,256]{2,1,0:T(8,128)(2,1)S(1)}, bf16[2,64,256]{2,1,0:T(8,128)(2,1)S(1)}, u32[]{:S(2)}, u32[]{:S(2)}) collective-permute-start(bf16[2,64,256]{2,1,0:T(8,128)(2,1)S(1)} %get-tuple-element.55), channel_id=1, source_target_pairs={{5,7},{7,11},{2,1},{14,15},{11,5},{12,19},{9,9},{21,23},{16,13},{2... | collective-permute-start | bytes 196616 | tf_op jit(solution)/shard_map/ppermute | solution.py:679
  83.2 0.8 read_steps.1.refs_0_
  83.9 0.6 collective-permute-done.18.refs_10_
  84.5 1.5 shard_map.89
  86.0 18.0 %all_to_all.20.refs_7_ = bf16[4,2,64,384]{3,2,1,0:T(8,128)(2,1)S(1)} all-to-all(bf16[4,2,64,384]{3,2,1,0:T(8,128)(2,1)S(1)} %get-tuple-element.56.refs_7_), channel_id=1, replica_groups=mesh['row'=8,'col'=4] {'col'}, dimensions={0} | all-to-all | bytes 786432 | tf_op jit(solution)/shard_map/all_to_all | solution.py:686
  104.0 3.5 %all-to-all-start.2 = ((bf16[4,2,64,384]{3,2,1,0:T(8,128)(2,1)}), bf16[4,2,64,384]{3,2,1,0:T(8,128)(2,1)S(1)}, u32[]{:S(2)}, u32[]{:S(2)}) async-start(bf16[4,2,64,384]{3,2,1,0:T(8,128)(2,1)} %get-tuple-element.58), calls=%async_computation.2 | async-start | bytes 786432 | tf_op jit(solution)/shard_map/all_to_all | solution.py:686
  107.5 10.2 %tile.2 = (f32[1,4096]{1,0:T(1,128)S(1)}, bf16[4,2,64,384]{3,2,1,0:T(8,128)(2,1)}) custom-call(s32[2]{0:T(128)S(1)} %copy-done.1, s32[1]{0:T(128)} %bitcast.refs_2_.refs_0_.refs_1_, s32[1]{0:T(128)} %bitcast.1.refs_3_.refs_1_.refs_2_, s32[1]{0:T(128)} %bitcast.2.refs_4_.refs_2_.refs_3_, bf16[2,4096,384]{2,1,0:T(8,128)(2,1)} %refs_4_.3, ...), custom_call_target="tpu_custom_call" | custom-call | tf_op jit(solution)/shard_map/tile/pallas_call | solution.py:590
  117.7 4.5 %all-to-all-start.1 = ((bf16[4,2,64,384]{3,2,1,0:T(8,128)(2,1)}), bf16[4,2,64,384]{3,2,1,0:T(8,128)(2,1)S(1)}, u32[]{:S(2)}, u32[]{:S(2)}) async-start(bf16[4,2,64,384]{3,2,1,0:T(8,128)(2,1)} %get-tuple-element.57), calls=%async_computation.1 | async-start | bytes 786432 | tf_op jit(solution)/shard_map/all_to_all | solution.py:689
  122.2 10.2 %tile.3 = (f32[1,4096]{1,0:T(1,128)S(1)}, bf16[4,2,64,384]{3,2,1,0:T(8,128)(2,1)}) custom-call(s32[2]{0:T(128)S(1)} %copy-done.1, s32[1]{0:T(128)} %bitcast.refs_2_.refs_0_.refs_1_, s32[1]{0:T(128)} %bitcast.1.refs_3_.refs_1_.refs_2_, s32[1]{0:T(128)} %bitcast.2.refs_4_.refs_2_.refs_3_, bf16[2,4096,384]{2,1,0:T(8,128)(2,1)} %refs_4_.3, ...), custom_call_target="tpu_custom_call" | custom-call | tf_op jit(solution)/shard_map/tile/pallas_call | solution.py:590
  132.4 4.5 %all-to-all-start.3 = ((bf16[4,2,64,384]{3,2,1,0:T(8,128)(2,1)}), bf16[4,2,64,384]{3,2,1,0:T(8,128)(2,1)S(1)}, u32[]{:S(2)}, u32[]{:S(2)}) async-start(bf16[4,2,64,384]{3,2,1,0:T(8,128)(2,1)} %get-tuple-element.59), calls=%async_computation.3 | async-start | bytes 786432 | tf_op jit(solution)/shard_map/all_to_all | solution.py:689
  136.9 0.9 join_slices.1
  137.8 6.8 %all-to-all-done.3.refs_5_ = bf16[4,2,64,384]{3,2,1,0:T(8,128)(2,1)S(1)} async-done(((bf16[4,2,64,384]{3,2,1,0:T(8,128)(2,1)}), bf16[4,2,64,384]{3,2,1,0:T(8,128)(2,1)S(1)}, u32[]{:S(2)}, u32[]{:S(2)}) %all-to-all-start.3) | async-done | bytes 393248 | tf_op jit(solution)/shard_map/all_to_all | solution.py:689
  144.7 1.0 shard_map.90
  145.7 8.7 %collective-permute-start.20 = (bf16[2,64,256]{2,1,0:T(8,128)(2,1)S(1)}, bf16[2,64,256]{2,1,0:T(8,128)(2,1)S(1)}, u32[]{:S(2)}, u32[]{:S(2)}) collective-permute-start(bf16[2,64,256]{2,1,0:T(8,128)(2,1)S(1)} %get-tuple-element.61), channel_id=1, source_target_pairs={{0,4},{4,8},{8,12},{12,16},{16,20},{20,24},{24,28},{1,5},{5,9},{9,... | collective-permute-start | bytes 196616 | tf_op jit(solution)/shard_map/ppermute | solution.py:36
  154.4 1.9 %collective-permute-start.21 = (bf16[2,64,256]{2,1,0:T(8,128)(2,1)S(1)}, bf16[2,64,256]{2,1,0:T(8,128)(2,1)S(1)}, u32[]{:S(2)}, u32[]{:S(2)}) collective-permute-start(bf16[2,64,256]{2,1,0:T(8,128)(2,1)S(1)} %get-tuple-element.62), channel_id=1, source_target_pairs={{4,0},{8,4},{12,8},{16,12},{20,16},{24,20},{28,24},{5,1},{9,5},{13... | collective-permute-start | bytes 196616 | tf_op jit(solution)/shard_map/ppermute | solution.py:36
  156.4 0.6 pad_maximum_fusion
  157.0 3.9 %collective-permute-done.21 = bf16[2,64,256]{2,1,0:T(8,128)(2,1)S(1)} collective-permute-done((bf16[2,64,256]{2,1,0:T(8,128)(2,1)S(1)}, bf16[2,64,256]{2,1,0:T(8,128)(2,1)S(1)}, u32[]{:S(2)}, u32[]{:S(2)}) %collective-permute-start.21) | collective-permute-done | bytes 65568 | tf_op jit(solution)/shard_map/ppermute | solution.py:36
  160.9 0.1 convert_add_fusion
  161.0 1.2 pad_select_fusion
  (23 shorter events, 0.1 us)
Async XLA Ops:
  2.6 7.9 %collective-permute-start = (bf16[208,256]{1,0:T(8,128)(2,1)}, bf16[208,256]{1,0:T(8,128)(2,1)S(1)}, u32[]{:S(2)}, u32[]{:S(2)}) collective-permute-start(bf16[208,256]{1,0:T(8,128)(2,1)} %get-tuple-element.34), channel_id=1, source_target_pairs={{0,0},{1,4},{2,1},{3,5},{4,2},{5,6},{6,3},{7,7},{8,11},{9,15},{10,... | collective-permute-start | bytes 319496 | tf_op jit(solution)/shard_map/ppermute | solution.py:665
  6.3 5.7 %collective-permute-start.1 = (bf16[208,256]{1,0:T(8,128)(2,1)}, bf16[208,256]{1,0:T(8,128)(2,1)S(1)}, u32[]{:S(2)}, u32[]{:S(2)}) collective-permute-start(bf16[208,256]{1,0:T(8,128)(2,1)} %get-tuple-element.35), channel_id=1, source_target_pairs={{0,4},{1,0},{2,5},{3,1},{4,6},{5,2},{6,7},{7,3},{8,15},{9,11},{10,... | collective-permute-start | bytes 319496 | tf_op jit(solution)/shard_map/ppermute | solution.py:665
  6.4 6.7 %collective-permute-start.2 = (bf16[208,256]{1,0:T(8,128)(2,1)}, bf16[208,256]{1,0:T(8,128)(2,1)S(1)}, u32[]{:S(2)}, u32[]{:S(2)}) collective-permute-start(bf16[208,256]{1,0:T(8,128)(2,1)} %get-tuple-element.36), channel_id=1, source_target_pairs={{0,1},{1,5},{2,0},{3,4},{4,3},{5,7},{6,2},{7,6},{8,10},{9,14},{10,... | collective-permute-start | bytes 319496 | tf_op jit(solution)/shard_map/ppermute | solution.py:665
  8.9 4.2 %collective-permute-start.3 = (bf16[208,256]{1,0:T(8,128)(2,1)}, bf16[208,256]{1,0:T(8,128)(2,1)S(1)}, u32[]{:S(2)}, u32[]{:S(2)}) collective-permute-start(bf16[208,256]{1,0:T(8,128)(2,1)} %get-tuple-element.37), channel_id=1, source_target_pairs={{0,5},{1,1},{2,4},{3,0},{4,7},{5,3},{6,6},{7,2},{8,14},{9,10},{10,... | collective-permute-start | bytes 319496 | tf_op jit(solution)/shard_map/ppermute | solution.py:665
  13.2 24.3 %collective-permute-start.6 = (bf16[3,256,256]{2,1,0:T(8,128)(2,1)S(1)}, bf16[3,256,256]{2,1,0:T(8,128)(2,1)S(1)}, u32[]{:S(2)}, u32[]{:S(2)}) collective-permute-start(bf16[3,256,256]{2,1,0:T(8,128)(2,1)S(1)} %get-tuple-element.39.own_ref), channel_id=1, source_target_pairs={{4,0},{1,4},{5,1},{2,5},{6,2},{3,6},{7,3},{11,7},{15,11},{10,15},{... | collective-permute-start | bytes 1179656 | tf_op jit(solution)/shard_map/ppermute | solution.py:305
  18.1 11.0 %collective-permute-start.4 = (bf16[2,256,256]{2,1,0:T(8,128)(2,1)S(1)}, bf16[2,256,256]{2,1,0:T(8,128)(2,1)S(1)}, u32[]{:S(2)}, u32[]{:S(2)}) collective-permute-start(bf16[2,256,256]{2,1,0:T(8,128)(2,1)S(1)} %get-tuple-element.40), channel_id=1, source_target_pairs={{0,4},{4,1},{1,5},{5,2},{2,6},{6,3},{3,7},{7,11},{11,15},{15,10},{... | collective-permute-start | bytes 786440 | tf_op jit(solution)/shard_map/ppermute | solution.py:305
  23.0 10.3 %collective-permute-start.5 = (bf16[2,256,256]{2,1,0:T(8,128)(2,1)S(1)}, bf16[2,256,256]{2,1,0:T(8,128)(2,1)S(1)}, u32[]{:S(2)}, u32[]{:S(2)}) collective-permute-start(bf16[2,256,256]{2,1,0:T(8,128)(2,1)S(1)} %get-tuple-element.40), channel_id=1, source_target_pairs={{0,1},{4,5},{1,2},{5,6},{2,3},{6,7},{3,11},{7,15},{11,10},{15,14},... | collective-permute-start | bytes 786440 | tf_op jit(solution)/shard_map/ppermute | solution.py:305
  27.1 10.3 %collective-permute-start.7 = (bf16[2,256,256]{2,1,0:T(8,128)(2,1)S(1)}, bf16[2,256,256]{2,1,0:T(8,128)(2,1)S(1)}, u32[]{:S(2)}, u32[]{:S(2)}) collective-permute-start(bf16[2,256,256]{2,1,0:T(8,128)(2,1)S(1)} %get-tuple-element.41), channel_id=1, source_target_pairs={{1,0},{5,4},{2,1},{6,5},{3,2},{7,6},{11,3},{15,7},{10,11},{14,15},... | collective-permute-start | bytes 786440 | tf_op jit(solution)/shard_map/ppermute | solution.py:305
  39.0 21.0 %collective-permute-start.10 = (bf16[4,256,256]{2,1,0:T(8,128)(2,1)S(1)}, bf16[4,256,256]{2,1,0:T(8,128)(2,1)S(1)}, u32[]{:S(2)}, u32[]{:S(2)}) collective-permute-start(bf16[4,256,256]{2,1,0:T(8,128)(2,1)S(1)} %get-tuple-element.45), channel_id=1, source_target_pairs={{4,0},{1,4},{5,1},{2,5},{6,2},{3,6},{7,3},{11,7},{15,11},{10,15},{... | collective-permute-start | bytes 1572872 | tf_op jit(solution)/shard_map/ppermute | solution.py:305
  41.1 18.9 %collective-permute-start.8 = (bf16[4,256,256]{2,1,0:T(8,128)(2,1)S(1)}, bf16[4,256,256]{2,1,0:T(8,128)(2,1)S(1)}, u32[]{:S(2)}, u32[]{:S(2)}) collective-permute-start(bf16[4,256,256]{2,1,0:T(8,128)(2,1)S(1)} %get-tuple-element.43), channel_id=1, source_target_pairs={{0,4},{4,1},{1,5},{5,2},{2,6},{6,3},{3,7},{7,11},{11,15},{15,10},{... | collective-permute-start | bytes 1572872 | tf_op jit(solution)/shard_map/ppermute | solution.py:305
  45.5 13.4 %collective-permute-start.11 = (bf16[3,256,256]{2,1,0:T(8,128)(2,1)S(1)}, bf16[3,256,256]{2,1,0:T(8,128)(2,1)S(1)}, u32[]{:S(2)}, u32[]{:S(2)}) collective-permute-start(bf16[3,256,256]{2,1,0:T(8,128)(2,1)S(1)} %get-tuple-element.46), channel_id=1, source_target_pairs={{1,0},{5,4},{2,1},{6,5},{3,2},{7,6},{11,3},{15,7},{10,11},{14,15},... | collective-permute-start | bytes 1179656 | tf_op jit(solution)/shard_map/ppermute | solution.py:305
  47.4 12.6 %collective-permute-start.9 = (bf16[3,256,256]{2,1,0:T(8,128)(2,1)S(1)}, bf16[3,256,256]{2,1,0:T(8,128)(2,1)S(1)}, u32[]{:S(2)}, u32[]{:S(2)}) collective-permute-start(bf16[3,256,256]{2,1,0:T(8,128)(2,1)S(1)} %get-tuple-element.44), channel_id=1, source_target_pairs={{0,1},{4,5},{1,2},{5,6},{2,3},{6,7},{3,11},{7,15},{11,10},{15,14},... | collective-permute-start | bytes 1179656 | tf_op jit(solution)/shard_map/ppermute | solution.py:305
  61.6 19.0 %collective-permute-start.12 = (bf16[336,256]{1,0:T(8,128)(2,1)S(1)}, bf16[336,256]{1,0:T(8,128)(2,1)S(1)}, u32[]{:S(2)}, u32[]{:S(2)}) collective-permute-start(bf16[336,256]{1,0:T(8,128)(2,1)S(1)} %get-tuple-element.48), channel_id=1, source_target_pairs={{0,0},{4,1},{1,2},{5,3},{2,4},{6,5},{3,6},{7,7},{11,8},{15,9},{10,... | collective-permute-start | bytes 516104 | tf_op jit(solution)/shard_map/ppermute | solution.py:677
  64.3 10.0 %collective-permute-start.16 = (bf16[2,64,256]{2,1,0:T(8,128)(2,1)S(1)}, bf16[2,64,256]{2,1,0:T(8,128)(2,1)S(1)}, u32[]{:S(2)}, u32[]{:S(2)}) collective-permute-start(bf16[2,64,256]{2,1,0:T(8,128)(2,1)S(1)} %get-tuple-element.52), channel_id=1, source_target_pairs={{5,4},{7,8},{2,2},{14,12},{11,6},{12,16},{9,10},{21,20},{16,14},{2... | collective-permute-start | bytes 196616 | tf_op jit(solution)/shard_map/ppermute | solution.py:679
  67.0 17.5 %collective-permute-start.13 = (bf16[336,256]{1,0:T(8,128)(2,1)S(1)}, bf16[336,256]{1,0:T(8,128)(2,1)S(1)}, u32[]{:S(2)}, u32[]{:S(2)}) collective-permute-start(bf16[336,256]{1,0:T(8,128)(2,1)S(1)} %get-tuple-element.49), channel_id=1, source_target_pairs={{4,0},{0,1},{5,2},{1,3},{6,4},{2,5},{7,6},{3,7},{15,8},{11,9},{14,... | collective-permute-start | bytes 516104 | tf_op jit(solution)/shard_map/ppermute | solution.py:677
  68.7 15.8 %collective-permute-start.14 = (bf16[336,256]{1,0:T(8,128)(2,1)S(1)}, bf16[336,256]{1,0:T(8,128)(2,1)S(1)}, u32[]{:S(2)}, u32[]{:S(2)}) collective-permute-start(bf16[336,256]{1,0:T(8,128)(2,1)S(1)} %get-tuple-element.50), channel_id=1, source_target_pairs={{1,0},{5,1},{0,2},{4,3},{3,4},{7,5},{2,6},{6,7},{10,8},{14,9},{11,... | collective-permute-start | bytes 516104 | tf_op jit(solution)/shard_map/ppermute | solution.py:677
  68.7 15.8 %collective-permute-start.15 = (bf16[336,256]{1,0:T(8,128)(2,1)S(1)}, bf16[336,256]{1,0:T(8,128)(2,1)S(1)}, u32[]{:S(2)}, u32[]{:S(2)}) collective-permute-start(bf16[336,256]{1,0:T(8,128)(2,1)S(1)} %get-tuple-element.51), channel_id=1, source_target_pairs={{5,0},{1,1},{4,2},{0,3},{7,4},{3,5},{6,6},{2,7},{14,8},{10,9},{15,... | collective-permute-start | bytes 516104 | tf_op jit(solution)/shard_map/ppermute | solution.py:677
  74.3 2.6 %collective-permute-start.17 = (bf16[2,64,256]{2,1,0:T(8,128)(2,1)S(1)}, bf16[2,64,256]{2,1,0:T(8,128)(2,1)S(1)}, u32[]{:S(2)}, u32[]{:S(2)}) collective-permute-start(bf16[2,64,256]{2,1,0:T(8,128)(2,1)S(1)} %get-tuple-element.53), channel_id=1, source_target_pairs={{5,5},{7,9},{2,3},{14,13},{11,7},{12,17},{9,11},{21,21},{16,15},{2... | collective-permute-start | bytes 196616 | tf_op jit(solution)/shard_map/ppermute | solution.py:679
  76.9 7.5 %collective-permute-start.18 = (bf16[2,64,256]{2,1,0:T(8,128)(2,1)S(1)}, bf16[2,64,256]{2,1,0:T(8,128)(2,1)S(1)}, u32[]{:S(2)}, u32[]{:S(2)}) collective-permute-start(bf16[2,64,256]{2,1,0:T(8,128)(2,1)S(1)} %get-tuple-element.54), channel_id=1, source_target_pairs={{5,6},{7,10},{2,0},{14,14},{11,4},{12,18},{9,8},{21,22},{16,12},{2... | collective-permute-start | bytes 196616 | tf_op jit(solution)/shard_map/ppermute | solution.py:679
  80.6 26.9 %copy-start = (f32[2,4096]{1,0:T(2,128)S(1)}, f32[2,4096]{1,0:T(2,128)}, u32[]{:S(2)}) copy-start(f32[2,4096]{1,0:T(2,128)} %refs_6_.3) | copy-start | bytes 98308
  80.6 26.9 %copy-start.1 = (s32[2]{0:T(128)S(1)}, s32[2]{0:T(128)}, u32[]{:S(2)}) copy-start(s32[2]{0:T(128)} %refs_0_.5) | copy-start | bytes 28
  80.6 3.9 %collective-permute-start.19 = (bf16[2,64,256]{2,1,0:T(8,128)(2,1)S(1)}, bf16[2,64,256]{2,1,0:T(8,128)(2,1)S(1)}, u32[]{:S(2)}, u32[]{:S(2)}) collective-permute-start(bf16[2,64,256]{2,1,0:T(8,128)(2,1)S(1)} %get-tuple-element.55), channel_id=1, source_target_pairs={{5,7},{7,11},{2,1},{14,15},{11,5},{12,19},{9,9},{21,23},{16,13},{2... | collective-permute-start | bytes 196616 | tf_op jit(solution)/shard_map/ppermute | solution.py:679
  104.0 13.7 %all-to-all-start.2 = ((bf16[4,2,64,384]{3,2,1,0:T(8,128)(2,1)}), bf16[4,2,64,384]{3,2,1,0:T(8,128)(2,1)S(1)}, u32[]{:S(2)}, u32[]{:S(2)}) async-start(bf16[4,2,64,384]{3,2,1,0:T(8,128)(2,1)} %get-tuple-element.58), calls=%async_computation.2 | async-start | bytes 786432 | tf_op jit(solution)/shard_map/all_to_all | solution.py:686
  117.7 14.7 %all-to-all-start.1 = ((bf16[4,2,64,384]{3,2,1,0:T(8,128)(2,1)}), bf16[4,2,64,384]{3,2,1,0:T(8,128)(2,1)S(1)}, u32[]{:S(2)}, u32[]{:S(2)}) async-start(bf16[4,2,64,384]{3,2,1,0:T(8,128)(2,1)} %get-tuple-element.57), calls=%async_computation.1 | async-start | bytes 786432 | tf_op jit(solution)/shard_map/all_to_all | solution.py:689
  122.2 14.8 %copy-start.2 = (s32[4,5]{1,0:T(4,128)S(1)}, s32[4,5]{1,0:T(4,128)}, u32[]{:S(2)}) copy-start(s32[4,5]{1,0:T(4,128)} %refs_0_.3) | copy-start | bytes 244
  132.4 12.3 %all-to-all-start.3 = ((bf16[4,2,64,384]{3,2,1,0:T(8,128)(2,1)}), bf16[4,2,64,384]{3,2,1,0:T(8,128)(2,1)S(1)}, u32[]{:S(2)}, u32[]{:S(2)}) async-start(bf16[4,2,64,384]{3,2,1,0:T(8,128)(2,1)} %get-tuple-element.59), calls=%async_computation.3 | async-start | bytes 786432 | tf_op jit(solution)/shard_map/all_to_all | solution.py:689
  145.7 11.3 %collective-permute-start.20 = (bf16[2,64,256]{2,1,0:T(8,128)(2,1)S(1)}, bf16[2,64,256]{2,1,0:T(8,128)(2,1)S(1)}, u32[]{:S(2)}, u32[]{:S(2)}) collective-permute-start(bf16[2,64,256]{2,1,0:T(8,128)(2,1)S(1)} %get-tuple-element.61), channel_id=1, source_target_pairs={{0,4},{4,8},{8,12},{12,16},{16,20},{20,24},{24,28},{1,5},{5,9},{9,... | collective-permute-start | bytes 196616 | tf_op jit(solution)/shard_map/ppermute | solution.py:36
  154.4 6.5 %collective-permute-start.21 = (bf16[2,64,256]{2,1,0:T(8,128)(2,1)S(1)}, bf16[2,64,256]{2,1,0:T(8,128)(2,1)S(1)}, u32[]{:S(2)}, u32[]{:S(2)}) collective-permute-start(bf16[2,64,256]{2,1,0:T(8,128)(2,1)S(1)} %get-tuple-element.62), channel_id=1, source_target_pairs={{4,0},{8,4},{12,8},{16,12},{20,16},{24,20},{28,24},{5,1},{9,5},{13... | collective-permute-start | bytes 196616 | tf_op jit(solution)/shard_map/ppermute | solution.py:36

commit v7 on v6

--- a/solution.py
+++ b/solution.py
@@ -379,9 +379,11 @@
         if last:
             for turn in range(cols):
                 at = pl.ds(pl.multiple_of(mixed(ids[PLACE], turn, cols) * high, high), high)
-                for d in range(5):
-                    outs[turn][d * high : (d + 1) * high] = whole_ref[d, at]
-                outs[turn][5 * high :] = steps_ref[...]
+                for k in range(3):
+                    outs[turn][k * high : (k + 1) * high] = whole_ref[k + 1, at]
+                outs[turn][3 * high :] = steps_ref[...]
+                for k in range(2):
+                    outs[2 * cols + turn][k * high : (k + 1) * high] = whole_ref[4 * k, at]
 
                 @pl.when(ids[PLACE] == cols - 1)
                 def _():
@@ -394,31 +396,48 @@
 
     whole = ((5, block, block), BF16)
     if last:
-        shapes = [((5 * high + NOTE, block), BF16)] * cols + [((2, high, block), BF16)] * cols
+        shapes = [((3 * high + NOTE, block), BF16)] * cols + [((2, high, block), BF16)] * cols
+        shapes += [((2 * high, block), BF16)] * cols
     else:
         shapes = [whole] + [((top - low, block, block), BF16) for low, top in SENDS]
     return small_call(body, place if last else [], [kept, own] + list(near) + [steps], shapes, [whole, whole])
 
 
-def join_slices(pieces, ids, block, after):
+def join_slices(pieces, far_pieces, ids, block, after):
     cols = len(pieces)
     high = block // cols
 
     def body(ids, *refs):
-        ins, out = refs[:cols], refs[-1]
+        near, far, out = refs[:cols], refs[cols : 2 * cols], refs[-1]
         for turn in range(cols):
             j = mixed(ids[SLICE], turn, cols)
-            for d in range(5):
-                out[j, d] = ins[turn][d * high : (d + 1) * high]
+            for k in range(3):
+                out[j, k + 1] = near[turn][k * high : (k + 1) * high]
+            for k in range(2):
+                out[j, 4 * k] = far[turn][k * high : (k + 1) * high]
 
     return pl.pallas_call(
         with_ids(body, 0),
-        in_specs=[SMEM_SPEC] * 3 + [VMEM_SPEC] * cols + [pl.BlockSpec(memory_space=pl.ANY)],
+        in_specs=[SMEM_SPEC] * 3 + [VMEM_SPEC] * (2 * cols) + [pl.BlockSpec(memory_space=pl.ANY)],
         out_specs=VMEM_SPEC,
         out_shape=jax.ShapeDtypeStruct((cols, 5, high, block), BF16),
         compiler_params=pltpu.CompilerParams(vmem_limit_bytes=SMALL),
         name="join_slices",
-    )(*ids, *pieces, after)
+    )(*ids, *pieces, *far_pieces, after)
+
+
+def own_copy(windows):
+    def body(windows_ref, out):
+        for tile in range(windows.shape[0]):
+            out[tile] = windows_ref[tile]
+
+    return pl.pallas_call(
+        body,
+        in_specs=[SMEM_SPEC],
+        out_specs=SMEM_SPEC,
+        out_shape=jax.ShapeDtypeStruct(windows.shape, windows.dtype),
+        compiler_params=pltpu.CompilerParams(vmem_limit_bytes=1 << 20),
+    )(windows)
 
 
 def read_steps(piece, cols, tiles):
@@ -462,8 +481,8 @@
             row = mixed(here, turn, cols) + 1
             for low in range(2):
                 for b in range(2):
-                    d = 2 - low + b
-                    near[low, row, :, b * block : (b + 1) * block] = ins[turn][d * high : (d + 1) * high]
+                    k = 1 - low + b
+                    near[low, row, :, b * block : (b + 1) * block] = ins[turn][k * high : (k + 1) * high]
 
             @pl.when(here == turn)
             def _():
@@ -679,14 +698,18 @@
         edges.append(lax.ppermute(out[cols + turn], BOTH, chain.edges(turn)))
     steps = read_steps(pieces[0], cols, tiles)
     sent = pack_windows(pieces, edges, steps, ids, block, tiles, functions)
-    purified = join_slices(pieces, ids, block, sent[0])
-
+    far_pieces = []
+    for turn in range(cols):
+        far_pieces.append(lax.ppermute(out[2 * cols + turn], BOTH, chain.to_slices(turn)))
+
+    windows = own_copy(windows)
     densities, terms = [], []
     for tile in range(tiles):
         window = lax.all_to_all(sent[tile], "col", 0, 0, tiled=True)
         dens, term = tile_call(tile, basis_values, basis_grads, weights, window, windows, ids)
         densities.append(dens)
         terms.append(lax.all_to_all(term, "col", 0, 0, tiled=True))
+    purified = join_slices(pieces, far_pieces, ids, block, term)
     mine, to_above, to_below = add_terms(terms, steps, ids, block)
     from_below = shifted_2(to_above, "row", -1).astype(F32)
     from_above = shifted_2(to_below, "row", 1).astype(F32)
@@ -707,7 +730,7 @@
         and 2 * functions == 3 * block
         and functions // 3 % density.shape[2] == 0
         and cols <= NOTE
-        and (5 * density.shape[2]) % NOTE == 0
+        and density.shape[2] % NOTE == 0
         and 2 * cols + 2 <= 256
         and basis_values.shape[1] % 1024 == 0
     )

time: 163 us -> 163 us (level)
  starting transfers between devices: 74.6 us -> 90.8 us
  waiting for transfers between devices: 37 us -> 24.1 us
  blocking collectives: 18 us -> 13.7 us
    ppermute x0 -> x4, starting transfers between devices: none -> 9.67 us  [by_block_rows(): lax.ppermute(out[2 * cols + turn], BOTH, chain.to_slices(turn))]
    all_to_all x2, waiting for transfers between devices: 6.85 us -> 0.01 us  [by_block_rows(): terms.append(lax.all_to_all(term, 'col', 0, 0, tiled=True))]
    ppermute x4, waiting for transfers between devices: 6.85 us -> 1.59 us  [by_block_rows(): edges.append(lax.ppermute(out[cols + turn], BOTH, chain.edges(turn)))]
    ppermute x2, starting transfers between devices: 10.7 us -> 15.4 us  [shifted_2(): return lax.ppermute(value, axis, pairs)]
    all_to_all x1, blocking collectives: 18 us -> 13.7 us  [by_block_rows(): window = lax.all_to_all(sent[tile], 'col', 0, 0, tiled=True)]
    ppermute x4, starting transfers between devices: 10.1 us -> 12 us  [by_block_rows(): edges.append(lax.ppermute(out[cols + turn], BOTH, chain.edges(turn)))]
  transfers between devices with their start and end apart: 25 -> 29, of which waited for: 11 -> 9; matrix products, arithmetic and copies ran while one was open for 0% -> 0% of each run, Pallas kernels for 14% -> 15%
where the time goes in v7:
time: 163 us; the launch traced here: 162 us
  starting transfers between devices  90.8 us (56%)
  Pallas kernels  30.8 us (19%)
  waiting for transfers between devices  24.1 us (15%)
  blocking collectives  13.7 us (8%)
  other arithmetic  1.9 us (1%)
    ppermute x8, starting transfers between devices, exchange_rows(): got[by] = lax.ppermute(send, BOTH, chain.shift(by))  28.5 us
    pallas_call x2, Pallas kernels, tile_call(): pl.pallas_call(with_ids(body, 1), grid=(count,), in_specs=[SMEM_SPEC, SME...  20.4 us
    ppermute x8, waiting for transfers between devices, exchange_rows(): got[by] = lax.ppermute(send, BOTH, chain.shift(by))  16.7 us
    ppermute x2, starting transfers between devices, shifted_2(): return lax.ppermute(value, axis, pairs)  15.4 us
    all_to_all x1, blocking collectives, by_block_rows(): window = lax.all_to_all(sent[tile], 'col', 0, 0, tiled=True)  13.7 us
    ppermute x4, starting transfers between devices, by_block_rows(): edges.append(lax.ppermute(out[cols + turn], BOTH, chain.edges(turn)))  12 us
    ppermute x4, starting transfers between devices, by_block_rows(): lax.ppermute(out[2 * cols + turn], BOTH, chain.to_slices(turn))  9.67 us
    all_to_all x2, starting transfers between devices, by_block_rows(): terms.append(lax.all_to_all(term, 'col', 0, 0, tiled=True))  9.01 us
  transfers between devices with their start and end apart: 29, of which 9 were waited for; matrix products, arithmetic and copies ran while one was open for 0% of the time, Pallas kernels for 15%

profile of v7, /device:TPU:3, one launch (start us, length us, event | category | flops | bytes accessed | tf_op | source)
XLA Modules:
  0.0 162.4 jit_solution(12496763596066531834)
XLA Ops:
  0.7 1.9 %shard_map.85 = (bf16[208,256]{1,0:T(8,128)(2,1)}, bf16[208,256]{1,0:T(8,128)(2,1)}, bf16[208,256]{1,0:T(8,128)(2,1)}, bf16[208,256]{1,0:T(8,128)(2,1)}) custom-call(s32[4,5]{1,0:T(4,128)} %refs_0_.1, s32[2]{0:T(128)} %windows_ref.1, s32[1]{0:T(128)} %bitcast.refs_2_.refs_0_.refs_1_, s32[1]{0:T(128)} %bitcast.1.refs_3_.refs_1_.refs_2_, ...), custom_call_target="tpu_custom_call" | custom-call | tf_op jit(solution)/shard_map/pallas_call | solution.py:232
  2.6 3.8 %collective-permute-start = (bf16[208,256]{1,0:T(8,128)(2,1)}, bf16[208,256]{1,0:T(8,128)(2,1)S(1)}, u32[]{:S(2)}, u32[]{:S(2)}) collective-permute-start(bf16[208,256]{1,0:T(8,128)(2,1)} %get-tuple-element.38), channel_id=1, source_target_pairs={{0,0},{1,4},{2,1},{3,5},{4,2},{5,6},{6,3},{7,7},{8,11},{9,15},{10,... | collective-permute-start | bytes 319496 | tf_op jit(solution)/shard_map/ppermute | solution.py:684
  6.4 2.5 %collective-permute-start.2 = (bf16[208,256]{1,0:T(8,128)(2,1)}, bf16[208,256]{1,0:T(8,128)(2,1)S(1)}, u32[]{:S(2)}, u32[]{:S(2)}) collective-permute-start(bf16[208,256]{1,0:T(8,128)(2,1)} %get-tuple-element.40), channel_id=1, source_target_pairs={{0,1},{1,5},{2,0},{3,4},{4,3},{5,7},{6,2},{7,6},{8,10},{9,14},{10,... | collective-permute-start | bytes 319496 | tf_op jit(solution)/shard_map/ppermute | solution.py:684
  8.9 1.5 collective-permute-start.3
  10.5 1.6 collective-permute-done.1.refs_4_
  12.1 1.0 collective-permute-done.2.refs_5_
  13.2 4.9 %collective-permute-start.6 = (bf16[3,256,256]{2,1,0:T(8,128)(2,1)S(1)}, bf16[3,256,256]{2,1,0:T(8,128)(2,1)S(1)}, u32[]{:S(2)}, u32[]{:S(2)}) collective-permute-start(bf16[3,256,256]{2,1,0:T(8,128)(2,1)S(1)} %get-tuple-element.43.own_ref), channel_id=1, source_target_pairs={{4,0},{1,4},{5,1},{2,5},{6,2},{3,6},{7,3},{11,7},{15,11},{10,15},{... | collective-permute-start | bytes 1179656 | tf_op jit(solution)/shard_map/ppermute | solution.py:305
  18.1 4.8 %collective-permute-start.4 = (bf16[2,256,256]{2,1,0:T(8,128)(2,1)S(1)}, bf16[2,256,256]{2,1,0:T(8,128)(2,1)S(1)}, u32[]{:S(2)}, u32[]{:S(2)}) collective-permute-start(bf16[2,256,256]{2,1,0:T(8,128)(2,1)S(1)} %get-tuple-element.44), channel_id=1, source_target_pairs={{0,4},{4,1},{1,5},{5,2},{2,6},{6,3},{3,7},{7,11},{11,15},{15,10},{... | collective-permute-start | bytes 786440 | tf_op jit(solution)/shard_map/ppermute | solution.py:305
  23.0 4.2 %collective-permute-start.5 = (bf16[2,256,256]{2,1,0:T(8,128)(2,1)S(1)}, bf16[2,256,256]{2,1,0:T(8,128)(2,1)S(1)}, u32[]{:S(2)}, u32[]{:S(2)}) collective-permute-start(bf16[2,256,256]{2,1,0:T(8,128)(2,1)S(1)} %get-tuple-element.44), channel_id=1, source_target_pairs={{0,1},{4,5},{1,2},{5,6},{2,3},{6,7},{3,11},{7,15},{11,10},{15,14},... | collective-permute-start | bytes 786440 | tf_op jit(solution)/shard_map/ppermute | solution.py:305
  27.1 1.9 %collective-permute-start.7 = (bf16[2,256,256]{2,1,0:T(8,128)(2,1)S(1)}, bf16[2,256,256]{2,1,0:T(8,128)(2,1)S(1)}, u32[]{:S(2)}, u32[]{:S(2)}) collective-permute-start(bf16[2,256,256]{2,1,0:T(8,128)(2,1)S(1)} %get-tuple-element.45), channel_id=1, source_target_pairs={{1,0},{5,4},{2,1},{6,5},{3,2},{7,6},{11,3},{15,7},{10,11},{14,15},... | collective-permute-start | bytes 786440 | tf_op jit(solution)/shard_map/ppermute | solution.py:305
  29.1 4.2 %collective-permute-done.5.m2 = bf16[2,256,256]{2,1,0:T(8,128)(2,1)S(1)} collective-permute-done((bf16[2,256,256]{2,1,0:T(8,128)(2,1)S(1)}, bf16[2,256,256]{2,1,0:T(8,128)(2,1)S(1)}, u32[]{:S(2)}, u32[]{:S(2)}) %collective-permute-start.5) | collective-permute-done | bytes 262176 | tf_op jit(solution)/shard_map/ppermute | solution.py:305
  33.3 4.2 %collective-permute-done.7.p2 = bf16[2,256,256]{2,1,0:T(8,128)(2,1)S(1)} collective-permute-done((bf16[2,256,256]{2,1,0:T(8,128)(2,1)S(1)}, bf16[2,256,256]{2,1,0:T(8,128)(2,1)S(1)}, u32[]{:S(2)}, u32[]{:S(2)}) %collective-permute-start.7) | collective-permute-done | bytes 262176 | tf_op jit(solution)/shard_map/ppermute | solution.py:305
  37.5 1.5 shard_map.87
  39.0 2.1 %collective-permute-start.10 = (bf16[4,256,256]{2,1,0:T(8,128)(2,1)S(1)}, bf16[4,256,256]{2,1,0:T(8,128)(2,1)S(1)}, u32[]{:S(2)}, u32[]{:S(2)}) collective-permute-start(bf16[4,256,256]{2,1,0:T(8,128)(2,1)S(1)} %get-tuple-element.49), channel_id=1, source_target_pairs={{4,0},{1,4},{5,1},{2,5},{6,2},{3,6},{7,3},{11,7},{15,11},{10,15},{... | collective-permute-start | bytes 1572872 | tf_op jit(solution)/shard_map/ppermute | solution.py:305
  41.1 4.4 %collective-permute-start.8 = (bf16[4,256,256]{2,1,0:T(8,128)(2,1)S(1)}, bf16[4,256,256]{2,1,0:T(8,128)(2,1)S(1)}, u32[]{:S(2)}, u32[]{:S(2)}) collective-permute-start(bf16[4,256,256]{2,1,0:T(8,128)(2,1)S(1)} %get-tuple-element.47), channel_id=1, source_target_pairs={{0,4},{4,1},{1,5},{5,2},{2,6},{6,3},{3,7},{7,11},{11,15},{15,10},{... | collective-permute-start | bytes 1572872 | tf_op jit(solution)/shard_map/ppermute | solution.py:305
  45.5 1.9 %collective-permute-start.11 = (bf16[3,256,256]{2,1,0:T(8,128)(2,1)S(1)}, bf16[3,256,256]{2,1,0:T(8,128)(2,1)S(1)}, u32[]{:S(2)}, u32[]{:S(2)}) collective-permute-start(bf16[3,256,256]{2,1,0:T(8,128)(2,1)S(1)} %get-tuple-element.50), channel_id=1, source_target_pairs={{1,0},{5,4},{2,1},{6,5},{3,2},{7,6},{11,3},{15,7},{10,11},{14,15},... | collective-permute-start | bytes 1179656 | tf_op jit(solution)/shard_map/ppermute | solution.py:305
  47.4 4.3 %collective-permute-start.9 = (bf16[3,256,256]{2,1,0:T(8,128)(2,1)S(1)}, bf16[3,256,256]{2,1,0:T(8,128)(2,1)S(1)}, u32[]{:S(2)}, u32[]{:S(2)}) collective-permute-start(bf16[3,256,256]{2,1,0:T(8,128)(2,1)S(1)} %get-tuple-element.48), channel_id=1, source_target_pairs={{0,1},{4,5},{1,2},{5,6},{2,3},{6,7},{3,11},{7,15},{11,10},{15,14},... | collective-permute-start | bytes 1179656 | tf_op jit(solution)/shard_map/ppermute | solution.py:305
  51.7 7.2 %collective-permute-done.11.refs_8_ = bf16[3,256,256]{2,1,0:T(8,128)(2,1)S(1)} collective-permute-done((bf16[3,256,256]{2,1,0:T(8,128)(2,1)S(1)}, bf16[3,256,256]{2,1,0:T(8,128)(2,1)S(1)}, u32[]{:S(2)}, u32[]{:S(2)}) %collective-permute-start.11) | collective-permute-done | bytes 393248 | tf_op jit(solution)/shard_map/ppermute | solution.py:305
  58.9 1.2 collective-permute-done.9.refs_6_
  60.0 1.6 shard_map.88
  61.6 2.7 %collective-permute-start.12 = (bf16[208,256]{1,0:T(8,128)(2,1)S(1)}, bf16[208,256]{1,0:T(8,128)(2,1)S(1)}, u32[]{:S(2)}, u32[]{:S(2)}) collective-permute-start(bf16[208,256]{1,0:T(8,128)(2,1)S(1)} %get-tuple-element.52), channel_id=1, source_target_pairs={{0,0},{4,1},{1,2},{5,3},{2,4},{6,5},{3,6},{7,7},{11,8},{15,9},{10,... | collective-permute-start | bytes 319496 | tf_op jit(solution)/shard_map/ppermute | solution.py:696
  64.4 2.6 %collective-permute-start.20 = (bf16[2,64,256]{2,1,0:T(8,128)(2,1)S(1)}, bf16[2,64,256]{2,1,0:T(8,128)(2,1)S(1)}, u32[]{:S(2)}, u32[]{:S(2)}) collective-permute-start(bf16[2,64,256]{2,1,0:T(8,128)(2,1)S(1)} %get-tuple-element.60), channel_id=1, source_target_pairs={{5,4},{7,8},{2,2},{14,12},{11,6},{12,16},{9,10},{21,20},{16,14},{2... | collective-permute-start | bytes 196616 | tf_op jit(solution)/shard_map/ppermute | solution.py:698
  67.0 1.8 %collective-permute-start.21 = (bf16[2,64,256]{2,1,0:T(8,128)(2,1)S(1)}, bf16[2,64,256]{2,1,0:T(8,128)(2,1)S(1)}, u32[]{:S(2)}, u32[]{:S(2)}) collective-permute-start(bf16[2,64,256]{2,1,0:T(8,128)(2,1)S(1)} %get-tuple-element.61), channel_id=1, source_target_pairs={{5,5},{7,9},{2,3},{14,13},{11,7},{12,17},{9,11},{21,21},{16,15},{2... | collective-permute-start | bytes 196616 | tf_op jit(solution)/shard_map/ppermute | solution.py:698
  68.8 1.2 collective-permute-start.13
  70.4 1.0 collective-permute-done.20.refs_8_
  71.4 0.7 collective-permute-start.15
  72.1 5.4 %collective-permute-start.22 = (bf16[2,64,256]{2,1,0:T(8,128)(2,1)S(1)}, bf16[2,64,256]{2,1,0:T(8,128)(2,1)S(1)}, u32[]{:S(2)}, u32[]{:S(2)}) collective-permute-start(bf16[2,64,256]{2,1,0:T(8,128)(2,1)S(1)} %get-tuple-element.62), channel_id=1, source_target_pairs={{5,6},{7,10},{2,0},{14,14},{11,4},{12,18},{9,8},{21,22},{16,12},{2... | collective-permute-start | bytes 196616 | tf_op jit(solution)/shard_map/ppermute | solution.py:698
  77.5 2.2 %collective-permute-start.23 = (bf16[2,64,256]{2,1,0:T(8,128)(2,1)S(1)}, bf16[2,64,256]{2,1,0:T(8,128)(2,1)S(1)}, u32[]{:S(2)}, u32[]{:S(2)}) collective-permute-start(bf16[2,64,256]{2,1,0:T(8,128)(2,1)S(1)} %get-tuple-element.63), channel_id=1, source_target_pairs={{5,7},{7,11},{2,1},{14,15},{11,5},{12,19},{9,9},{21,23},{16,13},{2... | collective-permute-start | bytes 196616 | tf_op jit(solution)/shard_map/ppermute | solution.py:698
  79.7 0.8 read_steps.1.refs_0_
  80.5 0.5 collective-permute-done.23.refs_11_
  81.0 1.5 shard_map.90
  82.6 13.7 %all_to_all.20.refs_7_ = bf16[4,2,64,384]{3,2,1,0:T(8,128)(2,1)S(1)} all-to-all(bf16[4,2,64,384]{3,2,1,0:T(8,128)(2,1)S(1)} %get-tuple-element.66), channel_id=1, replica_groups=mesh['row'=8,'col'=4] {'col'}, dimensions={0} | all-to-all | bytes 786432 | tf_op jit(solution)/shard_map/all_to_all | solution.py:708
  96.3 3.5 %all-to-all-start = ((bf16[4,2,64,384]{3,2,1,0:T(8,128)(2,1)}), bf16[4,2,64,384]{3,2,1,0:T(8,128)(2,1)S(1)}, u32[]{:S(2)}, u32[]{:S(2)}) async-start(bf16[4,2,64,384]{3,2,1,0:T(8,128)(2,1)} %get-tuple-element.64), calls=%async_computation | async-start | bytes 786432 | tf_op jit(solution)/shard_map/all_to_all | solution.py:708
  99.8 1.1 shard_map.89.refs_0_
  100.9 10.2 %tile.3 = (f32[1,4096]{1,0:T(1,128)S(1)}, bf16[4,2,64,384]{3,2,1,0:T(8,128)(2,1)}) custom-call(s32[2]{0:T(128)S(1)} %shard_map.89.refs_0_, s32[1]{0:T(128)} %bitcast.refs_2_.refs_0_.refs_1_, s32[1]{0:T(128)} %bitcast.1.refs_3_.refs_1_.refs_2_, s32[1]{0:T(128)} %bitcast.2.refs_4_.refs_2_.refs_3_, bf16[2,4096,384]{2,1,0:T(8,128)(2,1)} %refs_4_.3, ...), custom_call_target="tpu_custom_call" | custom-call | tf_op jit(solution)/shard_map/tile/pallas_call | solution.py:609
  111.1 4.5 %all-to-all-start.2 = ((bf16[4,2,64,384]{3,2,1,0:T(8,128)(2,1)}), bf16[4,2,64,384]{3,2,1,0:T(8,128)(2,1)S(1)}, u32[]{:S(2)}, u32[]{:S(2)}) async-start(bf16[4,2,64,384]{3,2,1,0:T(8,128)(2,1)} %get-tuple-element.67), calls=%async_computation.2 | async-start | bytes 786432 | tf_op jit(solution)/shard_map/all_to_all | solution.py:711
  115.6 10.2 %tile.2 = (f32[1,4096]{1,0:T(1,128)S(1)}, bf16[4,2,64,384]{3,2,1,0:T(8,128)(2,1)}) custom-call(s32[2]{0:T(128)S(1)} %shard_map.89.refs_0_, s32[1]{0:T(128)} %bitcast.refs_2_.refs_0_.refs_1_, s32[1]{0:T(128)} %bitcast.1.refs_3_.refs_1_.refs_2_, s32[1]{0:T(128)} %bitcast.2.refs_4_.refs_2_.refs_3_, bf16[2,4096,384]{2,1,0:T(8,128)(2,1)} %refs_4_.3, ...), custom_call_target="tpu_custom_call" | custom-call | tf_op jit(solution)/shard_map/tile/pallas_call | solution.py:609
  125.8 4.5 %all-to-all-start.3 = ((bf16[4,2,64,384]{3,2,1,0:T(8,128)(2,1)}), bf16[4,2,64,384]{3,2,1,0:T(8,128)(2,1)S(1)}, u32[]{:S(2)}, u32[]{:S(2)}) async-start(bf16[4,2,64,384]{3,2,1,0:T(8,128)(2,1)} %get-tuple-element.65.refs_11_), calls=%async_computation.3 | async-start | bytes 786432 | tf_op jit(solution)/shard_map/all_to_all | solution.py:711
  130.4 5.2 %collective-permute-start.16 = (bf16[128,256]{1,0:T(8,128)(2,1)S(1)}, bf16[128,256]{1,0:T(8,128)(2,1)S(1)}, u32[]{:S(2)}, u32[]{:S(2)}) collective-permute-start(bf16[128,256]{1,0:T(8,128)(2,1)S(1)} %get-tuple-element.56), channel_id=1, source_target_pairs={{0,0},{4,1},{1,2},{5,3},{2,4},{6,5},{3,6},{7,7},{11,8},{15,9},{10,... | collective-permute-start | bytes 196616 | tf_op jit(solution)/shard_map/ppermute | solution.py:703
  135.6 3.9 %collective-permute-start.17 = (bf16[128,256]{1,0:T(8,128)(2,1)S(1)}, bf16[128,256]{1,0:T(8,128)(2,1)S(1)}, u32[]{:S(2)}, u32[]{:S(2)}) collective-permute-start(bf16[128,256]{1,0:T(8,128)(2,1)S(1)} %get-tuple-element.57), channel_id=1, source_target_pairs={{4,0},{0,1},{5,2},{1,3},{6,4},{2,5},{7,6},{3,7},{15,8},{11,9},{14,... | collective-permute-start | bytes 196616 | tf_op jit(solution)/shard_map/ppermute | solution.py:703
  139.4 0.7 collective-permute-start.19
  140.1 1.0 shard_map.91
  141.1 13.5 %collective-permute-start.24 = (bf16[2,64,256]{2,1,0:T(8,128)(2,1)S(1)}, bf16[2,64,256]{2,1,0:T(8,128)(2,1)S(1)}, u32[]{:S(2)}, u32[]{:S(2)}) collective-permute-start(bf16[2,64,256]{2,1,0:T(8,128)(2,1)S(1)} %get-tuple-element.69), channel_id=1, source_target_pairs={{0,4},{4,8},{8,12},{12,16},{16,20},{20,24},{24,28},{1,5},{5,9},{9,... | collective-permute-start | bytes 196616 | tf_op jit(solution)/shard_map/ppermute | solution.py:36
  154.6 1.9 %collective-permute-start.25 = (bf16[2,64,256]{2,1,0:T(8,128)(2,1)S(1)}, bf16[2,64,256]{2,1,0:T(8,128)(2,1)S(1)}, u32[]{:S(2)}, u32[]{:S(2)}) collective-permute-start(bf16[2,64,256]{2,1,0:T(8,128)(2,1)S(1)} %get-tuple-element.70), channel_id=1, source_target_pairs={{4,0},{8,4},{12,8},{16,12},{20,16},{24,20},{28,24},{5,1},{9,5},{13... | collective-permute-start | bytes 196616 | tf_op jit(solution)/shard_map/ppermute | solution.py:36
  156.5 0.6 pad_maximum_fusion
  157.2 0.9 join_slices.1
  158.1 3.0 %collective-permute-done.25 = bf16[2,64,256]{2,1,0:T(8,128)(2,1)S(1)} collective-permute-done((bf16[2,64,256]{2,1,0:T(8,128)(2,1)S(1)}, bf16[2,64,256]{2,1,0:T(8,128)(2,1)S(1)}, u32[]{:S(2)}, u32[]{:S(2)}) %collective-permute-start.25) | collective-permute-done | bytes 65568 | tf_op jit(solution)/shard_map/ppermute | solution.py:36
  161.2 1.2 pad_select_fusion
  (32 shorter events, 0.7 us)
Async XLA Ops:
  2.6 7.9 %collective-permute-start = (bf16[208,256]{1,0:T(8,128)(2,1)}, bf16[208,256]{1,0:T(8,128)(2,1)S(1)}, u32[]{:S(2)}, u32[]{:S(2)}) collective-permute-start(bf16[208,256]{1,0:T(8,128)(2,1)} %get-tuple-element.38), channel_id=1, source_target_pairs={{0,0},{1,4},{2,1},{3,5},{4,2},{5,6},{6,3},{7,7},{8,11},{9,15},{10,... | collective-permute-start | bytes 319496 | tf_op jit(solution)/shard_map/ppermute | solution.py:684
  6.4 5.7 %collective-permute-start.1 = (bf16[208,256]{1,0:T(8,128)(2,1)}, bf16[208,256]{1,0:T(8,128)(2,1)S(1)}, u32[]{:S(2)}, u32[]{:S(2)}) collective-permute-start(bf16[208,256]{1,0:T(8,128)(2,1)} %get-tuple-element.39), channel_id=1, source_target_pairs={{0,4},{1,0},{2,5},{3,1},{4,6},{5,2},{6,7},{7,3},{8,15},{9,11},{10,... | collective-permute-start | bytes 319496 | tf_op jit(solution)/shard_map/ppermute | solution.py:684
  6.4 6.7 %collective-permute-start.2 = (bf16[208,256]{1,0:T(8,128)(2,1)}, bf16[208,256]{1,0:T(8,128)(2,1)S(1)}, u32[]{:S(2)}, u32[]{:S(2)}) collective-permute-start(bf16[208,256]{1,0:T(8,128)(2,1)} %get-tuple-element.40), channel_id=1, source_target_pairs={{0,1},{1,5},{2,0},{3,4},{4,3},{5,7},{6,2},{7,6},{8,10},{9,14},{10,... | collective-permute-start | bytes 319496 | tf_op jit(solution)/shard_map/ppermute | solution.py:684
  8.9 4.2 %collective-permute-start.3 = (bf16[208,256]{1,0:T(8,128)(2,1)}, bf16[208,256]{1,0:T(8,128)(2,1)S(1)}, u32[]{:S(2)}, u32[]{:S(2)}) collective-permute-start(bf16[208,256]{1,0:T(8,128)(2,1)} %get-tuple-element.41), channel_id=1, source_target_pairs={{0,5},{1,1},{2,4},{3,0},{4,7},{5,3},{6,6},{7,2},{8,14},{9,10},{10,... | collective-permute-start | bytes 319496 | tf_op jit(solution)/shard_map/ppermute | solution.py:684
  13.2 24.3 %collective-permute-start.6 = (bf16[3,256,256]{2,1,0:T(8,128)(2,1)S(1)}, bf16[3,256,256]{2,1,0:T(8,128)(2,1)S(1)}, u32[]{:S(2)}, u32[]{:S(2)}) collective-permute-start(bf16[3,256,256]{2,1,0:T(8,128)(2,1)S(1)} %get-tuple-element.43.own_ref), channel_id=1, source_target_pairs={{4,0},{1,4},{5,1},{2,5},{6,2},{3,6},{7,3},{11,7},{15,11},{10,15},{... | collective-permute-start | bytes 1179656 | tf_op jit(solution)/shard_map/ppermute | solution.py:305
  18.1 11.0 %collective-permute-start.4 = (bf16[2,256,256]{2,1,0:T(8,128)(2,1)S(1)}, bf16[2,256,256]{2,1,0:T(8,128)(2,1)S(1)}, u32[]{:S(2)}, u32[]{:S(2)}) collective-permute-start(bf16[2,256,256]{2,1,0:T(8,128)(2,1)S(1)} %get-tuple-element.44), channel_id=1, source_target_pairs={{0,4},{4,1},{1,5},{5,2},{2,6},{6,3},{3,7},{7,11},{11,15},{15,10},{... | collective-permute-start | bytes 786440 | tf_op jit(solution)/shard_map/ppermute | solution.py:305
  23.0 10.3 %collective-permute-start.5 = (bf16[2,256,256]{2,1,0:T(8,128)(2,1)S(1)}, bf16[2,256,256]{2,1,0:T(8,128)(2,1)S(1)}, u32[]{:S(2)}, u32[]{:S(2)}) collective-permute-start(bf16[2,256,256]{2,1,0:T(8,128)(2,1)S(1)} %get-tuple-element.44), channel_id=1, source_target_pairs={{0,1},{4,5},{1,2},{5,6},{2,3},{6,7},{3,11},{7,15},{11,10},{15,14},... | collective-permute-start | bytes 786440 | tf_op jit(solution)/shard_map/ppermute | solution.py:305
  27.1 10.3 %collective-permute-start.7 = (bf16[2,256,256]{2,1,0:T(8,128)(2,1)S(1)}, bf16[2,256,256]{2,1,0:T(8,128)(2,1)S(1)}, u32[]{:S(2)}, u32[]{:S(2)}) collective-permute-start(bf16[2,256,256]{2,1,0:T(8,128)(2,1)S(1)} %get-tuple-element.45), channel_id=1, source_target_pairs={{1,0},{5,4},{2,1},{6,5},{3,2},{7,6},{11,3},{15,7},{10,11},{14,15},... | collective-permute-start | bytes 786440 | tf_op jit(solution)/shard_map/ppermute | solution.py:305
  39.0 21.0 %collective-permute-start.10 = (bf16[4,256,256]{2,1,0:T(8,128)(2,1)S(1)}, bf16[4,256,256]{2,1,0:T(8,128)(2,1)S(1)}, u32[]{:S(2)}, u32[]{:S(2)}) collective-permute-start(bf16[4,256,256]{2,1,0:T(8,128)(2,1)S(1)} %get-tuple-element.49), channel_id=1, source_target_pairs={{4,0},{1,4},{5,1},{2,5},{6,2},{3,6},{7,3},{11,7},{15,11},{10,15},{... | collective-permute-start | bytes 1572872 | tf_op jit(solution)/shard_map/ppermute | solution.py:305
  41.1 18.9 %collective-permute-start.8 = (bf16[4,256,256]{2,1,0:T(8,128)(2,1)S(1)}, bf16[4,256,256]{2,1,0:T(8,128)(2,1)S(1)}, u32[]{:S(2)}, u32[]{:S(2)}) collective-permute-start(bf16[4,256,256]{2,1,0:T(8,128)(2,1)S(1)} %get-tuple-element.47), channel_id=1, source_target_pairs={{0,4},{4,1},{1,5},{5,2},{2,6},{6,3},{3,7},{7,11},{11,15},{15,10},{... | collective-permute-start | bytes 1572872 | tf_op jit(solution)/shard_map/ppermute | solution.py:305
  45.5 13.4 %collective-permute-start.11 = (bf16[3,256,256]{2,1,0:T(8,128)(2,1)S(1)}, bf16[3,256,256]{2,1,0:T(8,128)(2,1)S(1)}, u32[]{:S(2)}, u32[]{:S(2)}) collective-permute-start(bf16[3,256,256]{2,1,0:T(8,128)(2,1)S(1)} %get-tuple-element.50), channel_id=1, source_target_pairs={{1,0},{5,4},{2,1},{6,5},{3,2},{7,6},{11,3},{15,7},{10,11},{14,15},... | collective-permute-start | bytes 1179656 | tf_op jit(solution)/shard_map/ppermute | solution.py:305
  47.4 12.6 %collective-permute-start.9 = (bf16[3,256,256]{2,1,0:T(8,128)(2,1)S(1)}, bf16[3,256,256]{2,1,0:T(8,128)(2,1)S(1)}, u32[]{:S(2)}, u32[]{:S(2)}) collective-permute-start(bf16[3,256,256]{2,1,0:T(8,128)(2,1)S(1)} %get-tuple-element.48), channel_id=1, source_target_pairs={{0,1},{4,5},{1,2},{5,6},{2,3},{6,7},{3,11},{7,15},{11,10},{15,14},... | collective-permute-start | bytes 1179656 | tf_op jit(solution)/shard_map/ppermute | solution.py:305
  61.6 38.2 %copy-start.1 = (s32[2]{0:T(128)S(1)}, s32[2]{0:T(128)}, u32[]{:S(2)}) copy-start(s32[2]{0:T(128)} %windows_ref.1) | copy-start | bytes 28
  61.6 39.3 %copy-start = (f32[2,4096]{1,0:T(2,128)S(1)}, f32[2,4096]{1,0:T(2,128)}, u32[]{:S(2)}) copy-start(f32[2,4096]{1,0:T(2,128)} %refs_6_.3) | copy-start | bytes 98308
  61.6 15.9 %collective-permute-start.12 = (bf16[208,256]{1,0:T(8,128)(2,1)S(1)}, bf16[208,256]{1,0:T(8,128)(2,1)S(1)}, u32[]{:S(2)}, u32[]{:S(2)}) collective-permute-start(bf16[208,256]{1,0:T(8,128)(2,1)S(1)} %get-tuple-element.52), channel_id=1, source_target_pairs={{0,0},{4,1},{1,2},{5,3},{2,4},{6,5},{3,6},{7,7},{11,8},{15,9},{10,... | collective-permute-start | bytes 319496 | tf_op jit(solution)/shard_map/ppermute | solution.py:696
  64.4 7.0 %collective-permute-start.20 = (bf16[2,64,256]{2,1,0:T(8,128)(2,1)S(1)}, bf16[2,64,256]{2,1,0:T(8,128)(2,1)S(1)}, u32[]{:S(2)}, u32[]{:S(2)}) collective-permute-start(bf16[2,64,256]{2,1,0:T(8,128)(2,1)S(1)} %get-tuple-element.60), channel_id=1, source_target_pairs={{5,4},{7,8},{2,2},{14,12},{11,6},{12,16},{9,10},{21,20},{16,14},{2... | collective-permute-start | bytes 196616 | tf_op jit(solution)/shard_map/ppermute | solution.py:698
  67.0 5.1 %collective-permute-start.21 = (bf16[2,64,256]{2,1,0:T(8,128)(2,1)S(1)}, bf16[2,64,256]{2,1,0:T(8,128)(2,1)S(1)}, u32[]{:S(2)}, u32[]{:S(2)}) collective-permute-start(bf16[2,64,256]{2,1,0:T(8,128)(2,1)S(1)} %get-tuple-element.61), channel_id=1, source_target_pairs={{5,5},{7,9},{2,3},{14,13},{11,7},{12,17},{9,11},{21,21},{16,15},{2... | collective-permute-start | bytes 196616 | tf_op jit(solution)/shard_map/ppermute | solution.py:698
  68.8 12.2 %collective-permute-start.13 = (bf16[208,256]{1,0:T(8,128)(2,1)S(1)}, bf16[208,256]{1,0:T(8,128)(2,1)S(1)}, u32[]{:S(2)}, u32[]{:S(2)}) collective-permute-start(bf16[208,256]{1,0:T(8,128)(2,1)S(1)} %get-tuple-element.53), channel_id=1, source_target_pairs={{4,0},{0,1},{5,2},{1,3},{6,4},{2,5},{7,6},{3,7},{15,8},{11,9},{14,... | collective-permute-start | bytes 319496 | tf_op jit(solution)/shard_map/ppermute | solution.py:696
  70.0 11.0 %collective-permute-start.14 = (bf16[208,256]{1,0:T(8,128)(2,1)S(1)}, bf16[208,256]{1,0:T(8,128)(2,1)S(1)}, u32[]{:S(2)}, u32[]{:S(2)}) collective-permute-start(bf16[208,256]{1,0:T(8,128)(2,1)S(1)} %get-tuple-element.54), channel_id=1, source_target_pairs={{1,0},{5,1},{0,2},{4,3},{3,4},{7,5},{2,6},{6,7},{10,8},{14,9},{11,... | collective-permute-start | bytes 319496 | tf_op jit(solution)/shard_map/ppermute | solution.py:696
  71.4 9.6 %collective-permute-start.15 = (bf16[208,256]{1,0:T(8,128)(2,1)S(1)}, bf16[208,256]{1,0:T(8,128)(2,1)S(1)}, u32[]{:S(2)}, u32[]{:S(2)}) collective-permute-start(bf16[208,256]{1,0:T(8,128)(2,1)S(1)} %get-tuple-element.55), channel_id=1, source_target_pairs={{5,0},{1,1},{4,2},{0,3},{7,4},{3,5},{6,6},{2,7},{14,8},{10,9},{15,... | collective-permute-start | bytes 319496 | tf_op jit(solution)/shard_map/ppermute | solution.py:696
  72.1 8.4 %collective-permute-start.22 = (bf16[2,64,256]{2,1,0:T(8,128)(2,1)S(1)}, bf16[2,64,256]{2,1,0:T(8,128)(2,1)S(1)}, u32[]{:S(2)}, u32[]{:S(2)}) collective-permute-start(bf16[2,64,256]{2,1,0:T(8,128)(2,1)S(1)} %get-tuple-element.62), channel_id=1, source_target_pairs={{5,6},{7,10},{2,0},{14,14},{11,4},{12,18},{9,8},{21,22},{16,12},{2... | collective-permute-start | bytes 196616 | tf_op jit(solution)/shard_map/ppermute | solution.py:698
  77.5 3.5 %collective-permute-start.23 = (bf16[2,64,256]{2,1,0:T(8,128)(2,1)S(1)}, bf16[2,64,256]{2,1,0:T(8,128)(2,1)S(1)}, u32[]{:S(2)}, u32[]{:S(2)}) collective-permute-start(bf16[2,64,256]{2,1,0:T(8,128)(2,1)S(1)} %get-tuple-element.63), channel_id=1, source_target_pairs={{5,7},{7,11},{2,1},{14,15},{11,5},{12,19},{9,9},{21,23},{16,13},{2... | collective-permute-start | bytes 196616 | tf_op jit(solution)/shard_map/ppermute | solution.py:698
  96.3 14.8 %all-to-all-start = ((bf16[4,2,64,384]{3,2,1,0:T(8,128)(2,1)}), bf16[4,2,64,384]{3,2,1,0:T(8,128)(2,1)S(1)}, u32[]{:S(2)}, u32[]{:S(2)}) async-start(bf16[4,2,64,384]{3,2,1,0:T(8,128)(2,1)} %get-tuple-element.64), calls=%async_computation | async-start | bytes 786432 | tf_op jit(solution)/shard_map/all_to_all | solution.py:708
  111.1 14.7 %all-to-all-start.2 = ((bf16[4,2,64,384]{3,2,1,0:T(8,128)(2,1)}), bf16[4,2,64,384]{3,2,1,0:T(8,128)(2,1)S(1)}, u32[]{:S(2)}, u32[]{:S(2)}) async-start(bf16[4,2,64,384]{3,2,1,0:T(8,128)(2,1)} %get-tuple-element.67), calls=%async_computation.2 | async-start | bytes 786432 | tf_op jit(solution)/shard_map/all_to_all | solution.py:711
  115.6 19.9 %copy-start.2 = (s32[4,5]{1,0:T(4,128)S(1)}, s32[4,5]{1,0:T(4,128)}, u32[]{:S(2)}) copy-start(s32[4,5]{1,0:T(4,128)} %refs_0_.1) | copy-start | bytes 244
  125.8 14.2 %all-to-all-start.3 = ((bf16[4,2,64,384]{3,2,1,0:T(8,128)(2,1)}), bf16[4,2,64,384]{3,2,1,0:T(8,128)(2,1)S(1)}, u32[]{:S(2)}, u32[]{:S(2)}) async-start(bf16[4,2,64,384]{3,2,1,0:T(8,128)(2,1)} %get-tuple-element.65.refs_11_), calls=%async_computation.3 | async-start | bytes 786432 | tf_op jit(solution)/shard_map/all_to_all | solution.py:711
  130.4 24.2 %collective-permute-start.16 = (bf16[128,256]{1,0:T(8,128)(2,1)S(1)}, bf16[128,256]{1,0:T(8,128)(2,1)S(1)}, u32[]{:S(2)}, u32[]{:S(2)}) collective-permute-start(bf16[128,256]{1,0:T(8,128)(2,1)S(1)} %get-tuple-element.56), channel_id=1, source_target_pairs={{0,0},{4,1},{1,2},{5,3},{2,4},{6,5},{3,6},{7,7},{11,8},{15,9},{10,... | collective-permute-start | bytes 196616 | tf_op jit(solution)/shard_map/ppermute | solution.py:703
  135.6 21.6 %collective-permute-start.17 = (bf16[128,256]{1,0:T(8,128)(2,1)S(1)}, bf16[128,256]{1,0:T(8,128)(2,1)S(1)}, u32[]{:S(2)}, u32[]{:S(2)}) collective-permute-start(bf16[128,256]{1,0:T(8,128)(2,1)S(1)} %get-tuple-element.57), channel_id=1, source_target_pairs={{4,0},{0,1},{5,2},{1,3},{6,4},{2,5},{7,6},{3,7},{15,8},{11,9},{14,... | collective-permute-start | bytes 196616 | tf_op jit(solution)/shard_map/ppermute | solution.py:703
  139.4 17.8 %collective-permute-start.18 = (bf16[128,256]{1,0:T(8,128)(2,1)S(1)}, bf16[128,256]{1,0:T(8,128)(2,1)S(1)}, u32[]{:S(2)}, u32[]{:S(2)}) collective-permute-start(bf16[128,256]{1,0:T(8,128)(2,1)S(1)} %get-tuple-element.58), channel_id=1, source_target_pairs={{1,0},{5,1},{0,2},{4,3},{3,4},{7,5},{2,6},{6,7},{10,8},{14,9},{11,... | collective-permute-start | bytes 196616 | tf_op jit(solution)/shard_map/ppermute | solution.py:703
  139.4 17.8 %collective-permute-start.19 = (bf16[128,256]{1,0:T(8,128)(2,1)S(1)}, bf16[128,256]{1,0:T(8,128)(2,1)S(1)}, u32[]{:S(2)}, u32[]{:S(2)}) collective-permute-start(bf16[128,256]{1,0:T(8,128)(2,1)S(1)} %get-tuple-element.59), channel_id=1, source_target_pairs={{5,0},{1,1},{4,2},{0,3},{7,4},{3,5},{6,6},{2,7},{14,8},{10,9},{15,... | collective-permute-start | bytes 196616 | tf_op jit(solution)/shard_map/ppermute | solution.py:703
  141.1 17.0 %collective-permute-start.24 = (bf16[2,64,256]{2,1,0:T(8,128)(2,1)S(1)}, bf16[2,64,256]{2,1,0:T(8,128)(2,1)S(1)}, u32[]{:S(2)}, u32[]{:S(2)}) collective-permute-start(bf16[2,64,256]{2,1,0:T(8,128)(2,1)S(1)} %get-tuple-element.69), channel_id=1, source_target_pairs={{0,4},{4,8},{8,12},{12,16},{16,20},{20,24},{24,28},{1,5},{5,9},{9,... | collective-permute-start | bytes 196616 | tf_op jit(solution)/shard_map/ppermute | solution.py:36
  154.6 6.5 %collective-permute-start.25 = (bf16[2,64,256]{2,1,0:T(8,128)(2,1)S(1)}, bf16[2,64,256]{2,1,0:T(8,128)(2,1)S(1)}, u32[]{:S(2)}, u32[]{:S(2)}) collective-permute-start(bf16[2,64,256]{2,1,0:T(8,128)(2,1)S(1)} %get-tuple-element.70), channel_id=1, source_target_pairs={{4,0},{8,4},{12,8},{16,12},{20,16},{24,20},{28,24},{5,1},{9,5},{13... | collective-permute-start | bytes 196616 | tf_op jit(solution)/shard_map/ppermute | solution.py:36
